TPU v7x, 256 devices: a whole 4x4x8 slice. The times are simulated.
256 devices in a mesh: region: 16 (over y, x), band: 16 (over z, core).
Axes of the slice: x: 4, y: 4, z: 8, core: 2. Of those that a mesh axis runs over, the one named last changes fastest.
Arguments:
- adjoint_in: float32 [128, 256, 2048], P(None, 'band', 'region'), may hold values from -6 to 6
- courant_y: float32 [128, 256, 2048], P(None, 'band', 'region'), may hold values from -0.45 to 0.45
- courant_x: float32 [128, 256, 2048], P('band', None, 'region'), may hold values from -0.45 to 0.45
- diffusion_inverse: float32 [256, 128, 128], P('band')
- conv_weight: float32 [256, 2048], P('band', 'region'), may hold values from 0.05 to 0.9
- cloud_base: int32 [256, 2048], P('band', 'region'), may hold values from 0 to 63
- cloud_top: int32 [256, 2048], P('band', 'region'), may hold values from 1 to 126, as said below
- sound_count: int32 [16, 256], P('region', 'band'), may hold values from 0 to 64, as said below
- xco2_adjoint: float32 [16, 256, 64], P('region', 'band'), may hold values from -6 to 6
- kernel: float32 [16, 256, 64, 128], P('region', 'band'), may hold values from 0.25 to 4
- sound_cols: int32 [16, 256, 64], P('region', 'band'), may hold values from 0 to 2047
Outputs:
- adjoint_out: float32 [128, 256, 2048], P('band', None, 'region')
Inputs may be any that keep to these rules, and one draw needn't show every extreme that they name: `sound_count`: in every region one destination band receives 64 live slots from every source band. `sound_cols`: several slots may name the same column; the column is the latitude row within the band times 128 plus the longitude within the region. cloud_top > cloud_base in every column.
All inputs are finite; a program needn't handle non-finite values.
Results may differ from a plain program's by a relative error of at most 0.00014.
Values sent between devices are 32-bit elements; how exact they have to be, the bound alone decides.
No kernel may reach another device: no remote copies, remote signals or barrier semaphores. Data moves between devices by JAX's collectives and lax.ppermute only.
A program may use at most 64 MiB of HBM per device.

v0:
```python
import jax
import jax.numpy as jnp
from jax import lax
from jax.sharding import PartitionSpec as P

YSTEPS = 2
XSTEPS = 4


def with_halo(cells, sides, width):
    for axis, dim in sides:
        count = lax.axis_size(axis)
        head = lax.slice_in_dim(cells, 0, width, axis=dim)
        tail = lax.slice_in_dim(cells, cells.shape[dim] - width, cells.shape[dim], axis=dim)
        cells = jnp.concatenate(
            [
                lax.ppermute(tail, axis, [(i, (i + 1) % count) for i in range(count)]),
                cells,
                lax.ppermute(head, axis, [((i + 1) % count, i) for i in range(count)]),
            ],
            axis=dim,
        )
    return cells


def take_next(field, dim):
    kept_part = lax.slice_in_dim(field, 1, field.shape[dim], axis=dim)
    zero_edge = jnp.zeros_like(lax.slice_in_dim(field, 0, 1, axis=dim))
    return jnp.concatenate([kept_part, zero_edge], axis=dim)


def take_prev(field, dim):
    kept_part = lax.slice_in_dim(field, 0, field.shape[dim] - 1, axis=dim)
    zero_edge = jnp.zeros_like(lax.slice_in_dim(field, 0, 1, axis=dim))
    return jnp.concatenate([zero_edge, kept_part], axis=dim)


def advect_sweep(tracer, courant, dim):
    outflow_up = jnp.maximum(courant, 0.0)
    lower_prev = take_prev(jnp.minimum(courant, 0.0), dim)
    return (
        (1.0 - outflow_up + lower_prev) * tracer
        + outflow_up * take_next(tracer, dim)
        - lower_prev * take_prev(tracer, dim)
    )


def vertical_mix(field, diffusion_inverse, conv_weight, cloud_base, cloud_top):
    levels = jnp.arange(field.shape[0], dtype=jnp.int32)[:, None, None]
    inside = ((levels >= cloud_base[None]) & (levels <= cloud_top[None])).astype(jnp.float32)
    cloud_depth = (cloud_top - cloud_base + 1).astype(jnp.float32)
    column_mean = jnp.sum(inside * field, axis=0) / cloud_depth
    convected = field + conv_weight[None] * inside * (column_mean[None] - field)
    return jnp.einsum("jlk,lji->kji", diffusion_inverse, convected, precision=lax.Precision.HIGHEST)


def lat_sweeps(pair_in):
    tracer, courant = pair_in
    row_count = tracer.shape[1]
    global_row = jnp.arange(row_count, dtype=jnp.int32)[None, :, None]
    courant_eff = jnp.where(global_row < row_count - 1, courant, 0.0)
    for substep in range(YSTEPS):
        tracer = advect_sweep(tracer, courant_eff, 1)
    return tracer


def per_device(
    adjoint_in,
    courant_y,
    courant_x,
    diffusion_inverse,
    conv_weight,
    cloud_base,
    cloud_top,
    sound_count,
    xco2_adjoint,
    kernel,
    sound_cols,
):
    levels, lat_rows, lon_cells = adjoint_in.shape
    slot_count = kernel.shape[2]
    slot_index = jnp.arange(slot_count, dtype=jnp.int32)
    live_slot = slot_index[None, None, :] < sound_count[:, :, None]
    partial_value = jnp.where(live_slot, xco2_adjoint, 0.0)[..., None] * kernel
    arrived = lax.all_to_all(partial_value, "band", split_axis=1, concat_axis=1, tiled=True)
    flat_cols = sound_cols.reshape(-1)
    update = arrived.reshape(-1, levels).T
    column = adjoint_in.reshape(levels, lat_rows * lon_cells)
    forced = column.at[:, flat_cols].add(update).reshape(adjoint_in.shape)
    mixed = vertical_mix(forced, diffusion_inverse, conv_weight, cloud_base, cloud_top)
    level_slab = lat_sweeps(
        (
            lax.all_to_all(mixed, "band", split_axis=0, concat_axis=1, tiled=True),
            lax.all_to_all(courant_y, "band", split_axis=0, concat_axis=1, tiled=True),
        )
    )
    result = level_slab
    for substep in range(XSTEPS):
        extended = with_halo(jnp.stack([result, courant_x]), (("region", 3),), 1)
        result = advect_sweep(extended[0], extended[1], 2)[:, :, 1:-1]
    return result


def solution(mesh):
    in_specs = (
        P(None, "band", "region"),
        P(None, "band", "region"),
        P("band", None, "region"),
        P("band", None, None),
        P("band", "region"),
        P("band", "region"),
        P("band", "region"),
        P("region", "band"),
        P("region", "band", None),
        P("region", "band", None, None),
        P("region", "band", None),
    )
    out_specs = P("band", None, "region")
    return jax.shard_map(
        per_device, mesh=mesh, in_specs=in_specs, out_specs=out_specs, check_vma=False
    )
```

profile of v0, /device:TPU:1, one launch (start us, length us, event | category | flops | bytes accessed | tf_op | source)
XLA Modules:
  0.0 184.3 jit_solution(8449328299236931976)
XLA Ops:
  0.0 0.9 select_bitcast_fusion
  0.9 1.3 bitcast_multiply_fusion
  2.1 27.0 %all_to_all.41 = f32[1,16,64,128]{3,2,0,1:T(8,128)S(1)} all-to-all(f32[1,16,64,128]{3,2,0,1:T(8,128)S(1)} %bitcast_multiply_fusion), channel_id=1, replica_groups=mesh['region'=16,'band'=16] {'band'}, dimensions={1} | all-to-all | bytes 1048576 | tf_op jit(solution)/shard_map/all_to_all | solution.py:85
  29.1 4.2 %all-to-all-start = ((f32[128,16,128]{2,1,0:T(8,128)}), f32[128,16,128]{2,1,0:T(8,128)}, u32[]{:S(2)}, u32[]{:S(2)}) async-start(f32[128,16,128]{2,1,0:T(8,128)} %param.12), calls=%async_computation | async-start | bytes 2097152 | tf_op jit(solution)/shard_map/all_to_all | solution.py:94
  33.4 1.6 copy.23
  35.1 6.4 %scatter_fusion = f32[128,2048]{0,1:T(8,128)S(1)} fusion(f32[128,2048]{0,1:T(8,128)S(1)} %bitcast.75, s32[1024]{0:T(1024)S(1)} %bitcast.85, f32[1024,128]{1,0:T(8,128)S(1)} %bitcast.82), kind=kCustom, calls=%fused_computation | custom fusion | flops 131072 | bytes 1576960 | tf_op jit(solution)/shard_map/scatter-add | solution.py:89
  41.5 1.0 select_reduce_fusion
  42.6 3.6 %convolution_bitcast_fusion = f32[128,16,128]{0,2,1:T(8,128)S(1)} fusion(f32[16,128,128]{2,1,0:T(8,128)S(1)} %copy-done, f32[128,16,128]{0,2,1:T(8,128)S(1)} %bitcast.76, f32[16,128]{1,0:T(8,128)S(1)} %bitcast_divide_fusion, f32[16,128]{1,0:T(8,128)S(1)} %copy-done.7, s32[16,128]{1,0:T(8,128)S(1)} %copy-done.5, s32[16,128]{1,0:T(8,128)S(1)} %copy-done.6), kind=kOutput, calls=%fused_computation.34 | convolution fusion | flops 404488192 | bytes 3178496 | tf_op jit(solution)/shard_map/jlk,lji->kji/dot_general | solution.py:54
  46.1 1.4 copy.25
  47.5 12.6 %all-to-all-done = f32[128,16,128]{2,1,0:T(8,128)} async-done(((f32[128,16,128]{2,1,0:T(8,128)}), f32[128,16,128]{2,1,0:T(8,128)}, u32[]{:S(2)}, u32[]{:S(2)}) %all-to-all-start) | async-done | bytes 1048608 | tf_op jit(solution)/shard_map/all_to_all | solution.py:94
  60.1 4.2 %all-to-all-start.2 = ((f32[128,16,128]{2,1,0:T(8,128)}), f32[128,16,128]{2,1,0:T(8,128)}, u32[]{:S(2)}, u32[]{:S(2)}) async-start(f32[128,16,128]{2,1,0:T(8,128)} %copy.25), calls=%async_computation.2 | async-start | bytes 2097152 | tf_op jit(solution)/shard_map/all_to_all | solution.py:93
  64.3 1.3 copy.22
  65.9 25.7 %all-to-all-done.2 = f32[128,16,128]{2,1,0:T(8,128)} async-done(((f32[128,16,128]{2,1,0:T(8,128)}), f32[128,16,128]{2,1,0:T(8,128)}, u32[]{:S(2)}, u32[]{:S(2)}) %all-to-all-start.2) | async-done | bytes 1048608 | tf_op jit(solution)/shard_map/all_to_all | solution.py:93
  91.6 1.3 copy.26
  95.2 2.1 %slice_maximum_fusion.3 = (f32[2,8,256,1]{3,2,1,0:T(8,128)}, f32[2,8,256,1]{3,2,1,0:T(8,128)S(1)}) fusion(f32[1,8,256,128]{3,2,1,0:T(8,128)S(1)} %subtract_bitcast_fusion, f32[1,8,256,128]{3,2,1,0:T(8,128)S(1)} %bitcast.67), kind=kLoop, calls=%fused_computation.24 | loop fusion | flops 8192 | bytes 2129920 | tf_op jit(solution)/shard_map/stack | solution.py:99
  97.2 2.2 %copy.27 = f32[2,8,256,1]{2,1,3,0:T(8,128)S(1)} copy(f32[2,8,256,1]{3,2,1,0:T(8,128)} %get-tuple-element.31) | data formatting | bytes 32768 | tf_op jit(solution)/shard_map/slice | solution.py:14
  99.4 1.3 collective-permute-start
  101.3 4.0 %collective-permute-start.1 = (f32[2,8,256,1]{2,1,3,0:T(8,128)S(1)}, f32[2,8,256,1]{2,1,3,0:T(8,128)S(1)}, u32[]{:S(2)}, u32[]{:S(2)}) collective-permute-start(f32[2,8,256,1]{2,1,3,0:T(8,128)S(1)} %copy.28), channel_id=1, source_target_pairs={{16,0},{32,16},{48,32},{64,48},{80,64},{96,80},{112,96},{128,112},... | collective-permute-start | bytes 49160 | tf_op jit(solution)/shard_map/ppermute | solution.py:19
  105.5 2.0 %copy.29 = f32[2,8,256,1]{3,2,1,0:T(8,128)} copy(f32[2,8,256,1]{2,1,3,0:T(8,128)S(1)} %collective-permute-done) | data formatting | bytes 32768 | tf_op jit(solution)/shard_map/ppermute | solution.py:17
  107.5 2.0 %copy.30 = f32[2,8,256,1]{3,2,1,0:T(8,128)} copy(f32[2,8,256,1]{2,1,3,0:T(8,128)S(1)} %collective-permute-done.1) | data formatting | bytes 32768 | tf_op jit(solution)/shard_map/ppermute | solution.py:19
  109.5 3.9 %fusion.1 = f32[2,8,256,130]{3,2,1,0:T(8,128)S(1)} fusion(f32[1,8,256,128]{3,2,1,0:T(8,128)S(1)} %bitcast.68, f32[2,8,256,1]{3,2,1,0:T(8,128)} %copy.30, f32[1,8,256,128]{3,2,1,0:T(8,128)S(1)} %copy-done.4, f32[2,8,256,1]{3,2,1,0:T(8,128)} %copy.29), kind=kLoop, calls=%fused_computation.6 | loop fusion | flops 1597440 | bytes 4259840 | tf_op jit(solution)/shard_map/concatenate | solution.py:15
  113.4 0.8 maximum_bitcast_fusion.3
  114.9 0.9 fusion.17
  115.9 2.7 %slice_maximum_fusion.2 = (f32[2,8,256,1]{3,2,1,0:T(8,128)}, f32[2,8,256,1]{3,2,1,0:T(8,128)}) fusion(f32[1,8,256,128]{3,2,1,0:T(8,128)S(1)} %fusion.17, f32[1,8,256,128]{3,2,1,0:T(8,128)S(1)} %bitcast.69), kind=kLoop, calls=%fused_computation.22 | loop fusion | flops 8192 | bytes 2129920 | tf_op jit(solution)/shard_map/stack | solution.py:99
  118.6 2.2 %copy.31 = f32[2,8,256,1]{2,1,3,0:T(8,128)S(1)} copy(f32[2,8,256,1]{3,2,1,0:T(8,128)} %get-tuple-element.27) | data formatting | bytes 32768 | tf_op jit(solution)/shard_map/slice | solution.py:14
  120.8 2.2 %copy.32 = f32[2,8,256,1]{2,1,3,0:T(8,128)S(1)} copy(f32[2,8,256,1]{3,2,1,0:T(8,128)} %get-tuple-element.28) | data formatting | bytes 32768 | tf_op jit(solution)/shard_map/slice | solution.py:13
  123.0 5.0 %collective-permute-start.3 = (f32[2,8,256,1]{2,1,3,0:T(8,128)S(1)}, f32[2,8,256,1]{2,1,3,0:T(8,128)S(1)}, u32[]{:S(2)}, u32[]{:S(2)}) collective-permute-start(f32[2,8,256,1]{2,1,3,0:T(8,128)S(1)} %copy.32), channel_id=1, source_target_pairs={{16,0},{32,16},{48,32},{64,48},{80,64},{96,80},{112,96},{128,112},... | collective-permute-start | bytes 49160 | tf_op jit(solution)/shard_map/ppermute | solution.py:19
  128.1 2.0 %copy.33 = f32[2,8,256,1]{3,2,1,0:T(8,128)} copy(f32[2,8,256,1]{2,1,3,0:T(8,128)S(1)} %collective-permute-done.2) | data formatting | bytes 32768 | tf_op jit(solution)/shard_map/ppermute | solution.py:17
  130.0 2.0 %copy.34 = f32[2,8,256,1]{3,2,1,0:T(8,128)} copy(f32[2,8,256,1]{2,1,3,0:T(8,128)S(1)} %collective-permute-done.3) | data formatting | bytes 32768 | tf_op jit(solution)/shard_map/ppermute | solution.py:19
  132.0 3.9 %fusion.3 = f32[2,8,256,130]{3,2,1,0:T(8,128)S(1)} fusion(f32[1,8,256,128]{3,2,1,0:T(8,128)S(1)} %bitcast.70, f32[2,8,256,1]{3,2,1,0:T(8,128)} %copy.34, f32[1,8,256,128]{3,2,1,0:T(8,128)S(1)} %fusion.17, f32[2,8,256,1]{3,2,1,0:T(8,128)} %copy.33), kind=kLoop, calls=%fused_computation.8 | loop fusion | flops 1597440 | bytes 4259840 | tf_op jit(solution)/shard_map/concatenate | solution.py:15
  135.9 0.8 maximum_bitcast_fusion.2
  137.5 0.9 fusion.14
  138.4 2.7 %slice_maximum_fusion.1 = (f32[2,8,256,1]{3,2,1,0:T(8,128)}, f32[2,8,256,1]{3,2,1,0:T(8,128)}) fusion(f32[1,8,256,128]{3,2,1,0:T(8,128)S(1)} %fusion.14, f32[1,8,256,128]{3,2,1,0:T(8,128)S(1)} %bitcast.71), kind=kLoop, calls=%fused_computation.20 | loop fusion | flops 8192 | bytes 2129920 | tf_op jit(solution)/shard_map/stack | solution.py:99
  141.1 2.2 %copy.35 = f32[2,8,256,1]{2,1,3,0:T(8,128)S(1)} copy(f32[2,8,256,1]{3,2,1,0:T(8,128)} %get-tuple-element.23) | data formatting | bytes 32768 | tf_op jit(solution)/shard_map/slice | solution.py:14
  143.4 2.2 %copy.36 = f32[2,8,256,1]{2,1,3,0:T(8,128)S(1)} copy(f32[2,8,256,1]{3,2,1,0:T(8,128)} %get-tuple-element.24) | data formatting | bytes 32768 | tf_op jit(solution)/shard_map/slice | solution.py:13
  145.6 5.1 %collective-permute-start.5 = (f32[2,8,256,1]{2,1,3,0:T(8,128)S(1)}, f32[2,8,256,1]{2,1,3,0:T(8,128)S(1)}, u32[]{:S(2)}, u32[]{:S(2)}) collective-permute-start(f32[2,8,256,1]{2,1,3,0:T(8,128)S(1)} %copy.36), channel_id=1, source_target_pairs={{16,0},{32,16},{48,32},{64,48},{80,64},{96,80},{112,96},{128,112},... | collective-permute-start | bytes 49160 | tf_op jit(solution)/shard_map/ppermute | solution.py:19
  150.6 2.0 %copy.37 = f32[2,8,256,1]{3,2,1,0:T(8,128)} copy(f32[2,8,256,1]{2,1,3,0:T(8,128)S(1)} %collective-permute-done.4) | data formatting | bytes 32768 | tf_op jit(solution)/shard_map/ppermute | solution.py:17
  152.6 2.0 %copy.38 = f32[2,8,256,1]{3,2,1,0:T(8,128)} copy(f32[2,8,256,1]{2,1,3,0:T(8,128)S(1)} %collective-permute-done.5) | data formatting | bytes 32768 | tf_op jit(solution)/shard_map/ppermute | solution.py:19
  154.6 3.9 %fusion.5 = f32[2,8,256,130]{3,2,1,0:T(8,128)S(1)} fusion(f32[1,8,256,128]{3,2,1,0:T(8,128)S(1)} %bitcast.72, f32[2,8,256,1]{3,2,1,0:T(8,128)} %copy.38, f32[1,8,256,128]{3,2,1,0:T(8,128)S(1)} %fusion.14, f32[2,8,256,1]{3,2,1,0:T(8,128)} %copy.37), kind=kLoop, calls=%fused_computation.10 | loop fusion | flops 1597440 | bytes 4259840 | tf_op jit(solution)/shard_map/concatenate | solution.py:15
  160.1 0.9 fusion.11
  161.0 2.7 %slice_maximum_fusion = (f32[2,8,256,1]{3,2,1,0:T(8,128)}, f32[2,8,256,1]{3,2,1,0:T(8,128)}) fusion(f32[1,8,256,128]{3,2,1,0:T(8,128)S(1)} %fusion.11, f32[1,8,256,128]{3,2,1,0:T(8,128)S(1)} %bitcast.73), kind=kLoop, calls=%fused_computation.18 | loop fusion | flops 8192 | bytes 2129920 | tf_op jit(solution)/shard_map/stack | solution.py:99
  163.7 2.2 %copy.39 = f32[2,8,256,1]{2,1,3,0:T(8,128)S(1)} copy(f32[2,8,256,1]{3,2,1,0:T(8,128)} %get-tuple-element.19) | data formatting | bytes 32768 | tf_op jit(solution)/shard_map/slice | solution.py:14
  165.9 2.2 %copy.40 = f32[2,8,256,1]{2,1,3,0:T(8,128)S(1)} copy(f32[2,8,256,1]{3,2,1,0:T(8,128)} %get-tuple-element.20) | data formatting | bytes 32768 | tf_op jit(solution)/shard_map/slice | solution.py:13
  168.1 4.8 %collective-permute-start.7 = (f32[2,8,256,1]{2,1,3,0:T(8,128)S(1)}, f32[2,8,256,1]{2,1,3,0:T(8,128)S(1)}, u32[]{:S(2)}, u32[]{:S(2)}) collective-permute-start(f32[2,8,256,1]{2,1,3,0:T(8,128)S(1)} %copy.40), channel_id=1, source_target_pairs={{16,0},{32,16},{48,32},{64,48},{80,64},{96,80},{112,96},{128,112},... | collective-permute-start | bytes 49160 | tf_op jit(solution)/shard_map/ppermute | solution.py:19
  173.0 2.0 %copy.41 = f32[2,8,256,1]{3,2,1,0:T(8,128)} copy(f32[2,8,256,1]{2,1,3,0:T(8,128)S(1)} %collective-permute-done.6) | data formatting | bytes 32768 | tf_op jit(solution)/shard_map/ppermute | solution.py:17
  174.9 2.0 %copy.42 = f32[2,8,256,1]{3,2,1,0:T(8,128)} copy(f32[2,8,256,1]{2,1,3,0:T(8,128)S(1)} %collective-permute-done.7) | data formatting | bytes 32768 | tf_op jit(solution)/shard_map/ppermute | solution.py:19
  176.9 3.9 %fusion.7 = f32[2,8,256,130]{3,2,1,0:T(8,128)S(1)} fusion(f32[1,8,256,128]{3,2,1,0:T(8,128)S(1)} %bitcast.74, f32[2,8,256,1]{3,2,1,0:T(8,128)} %copy.42, f32[1,8,256,128]{3,2,1,0:T(8,128)S(1)} %fusion.11, f32[2,8,256,1]{3,2,1,0:T(8,128)} %copy.41), kind=kLoop, calls=%fused_computation.12 | loop fusion | flops 1597440 | bytes 4259840 | tf_op jit(solution)/shard_map/concatenate | solution.py:15
  182.4 1.9 %fusion.8 = f32[8,256,128]{2,1,0:T(8,128)} fusion(f32[8,256,129]{2,1,0:T(8,128)S(1)} %get-tuple-element.18, f32[8,256,129]{2,1,0:T(8,128)S(1)} %get-tuple-element.17, f32[8,256,130]{2,1,0:T(8,128)S(1)} %get-tuple-element.7, f32[8,256,129]{2,1,0:T(8,128)S(1)} %bitcast.81, f32[8,256,130]{2,1,0:T(8,128)S(1)} %get-tuple-element.5), kind=kLoop, calls=%fused_computation.36 | loop fusion | flops 1835008 | bytes 6316032 | tf_op jit(solution)/shard_map/sub | solution.py:42
  (46 shorter events, 8.1 us)
Async XLA Ops:
  0.0 42.6 %copy-start = (f32[16,128,128]{2,1,0:T(8,128)S(1)}, f32[16,128,128]{2,1,0:T(8,128)}, u32[]{:S(2)}) copy-start(f32[16,128,128]{2,1,0:T(8,128)} %param.14) | copy-start | bytes 3145732
  0.9 32.5 %copy-start.8 = (s32[1,16,64]{2,1,0:T(8,128)S(1)}, s32[1,16,64]{2,1,0:T(8,128)}, u32[]{:S(2)}) copy-start(s32[1,16,64]{2,1,0:T(8,128)} %param.21) | copy-start | bytes 12292
  29.1 31.0 %all-to-all-start = ((f32[128,16,128]{2,1,0:T(8,128)}), f32[128,16,128]{2,1,0:T(8,128)}, u32[]{:S(2)}, u32[]{:S(2)}) async-start(f32[128,16,128]{2,1,0:T(8,128)} %param.12), calls=%async_computation | async-start | bytes 2097152 | tf_op jit(solution)/shard_map/all_to_all | solution.py:94
  35.0 6.5 %copy-start.5 = (s32[16,128]{1,0:T(8,128)S(1)}, s32[16,128]{1,0:T(8,128)}, u32[]{:S(2)}) copy-start(s32[16,128]{1,0:T(8,128)} %param.17) | copy-start | bytes 24580
  35.0 6.5 %copy-start.6 = (s32[16,128]{1,0:T(8,128)S(1)}, s32[16,128]{1,0:T(8,128)}, u32[]{:S(2)}) copy-start(s32[16,128]{1,0:T(8,128)} %param.16) | copy-start | bytes 24580
  35.0 7.5 %copy-start.7 = (f32[16,128]{1,0:T(8,128)S(1)}, f32[16,128]{1,0:T(8,128)}, u32[]{:S(2)}) copy-start(f32[16,128]{1,0:T(8,128)} %param.15) | copy-start | bytes 24580
  60.1 31.5 %all-to-all-start.2 = ((f32[128,16,128]{2,1,0:T(8,128)}), f32[128,16,128]{2,1,0:T(8,128)}, u32[]{:S(2)}, u32[]{:S(2)}) async-start(f32[128,16,128]{2,1,0:T(8,128)} %copy.25), calls=%async_computation.2 | async-start | bytes 2097152 | tf_op jit(solution)/shard_map/all_to_all | solution.py:93
  93.9 1.2 copy-start.2
  94.6 2.7 %copy-start.3 = (f32[1,8,256,128]{3,2,1,0:T(8,128)}, f32[1,8,256,128]{3,2,1,0:T(8,128)S(1)}, u32[]{:S(2)}) copy-start(f32[1,8,256,128]{3,2,1,0:T(8,128)S(1)} %subtract_bitcast_fusion) | copy-start | bytes 3145732
  99.4 6.1 %collective-permute-start = (f32[2,8,256,1]{2,1,3,0:T(8,128)S(1)}, f32[2,8,256,1]{2,1,3,0:T(8,128)S(1)}, u32[]{:S(2)}, u32[]{:S(2)}) collective-permute-start(f32[2,8,256,1]{2,1,3,0:T(8,128)S(1)} %copy.27), channel_id=1, source_target_pairs={{0,16},{16,32},{32,48},{48,64},{64,80},{80,96},{96,112},{112,128},... | collective-permute-start | bytes 49160 | tf_op jit(solution)/shard_map/ppermute | solution.py:17
  101.3 8.2 %copy-start.4 = (f32[1,8,256,128]{3,2,1,0:T(8,128)S(1)}, f32[1,8,256,128]{3,2,1,0:T(8,128)}, u32[]{:S(2)}) copy-start(f32[1,8,256,128]{3,2,1,0:T(8,128)} %copy-done.3) | copy-start | bytes 3145732
  101.3 6.2 %collective-permute-start.1 = (f32[2,8,256,1]{2,1,3,0:T(8,128)S(1)}, f32[2,8,256,1]{2,1,3,0:T(8,128)S(1)}, u32[]{:S(2)}, u32[]{:S(2)}) collective-permute-start(f32[2,8,256,1]{2,1,3,0:T(8,128)S(1)} %copy.28), channel_id=1, source_target_pairs={{16,0},{32,16},{48,32},{64,48},{80,64},{96,80},{112,96},{128,112},... | collective-permute-start | bytes 49160 | tf_op jit(solution)/shard_map/ppermute | solution.py:19
  120.8 7.3 %collective-permute-start.2 = (f32[2,8,256,1]{2,1,3,0:T(8,128)S(1)}, f32[2,8,256,1]{2,1,3,0:T(8,128)S(1)}, u32[]{:S(2)}, u32[]{:S(2)}) collective-permute-start(f32[2,8,256,1]{2,1,3,0:T(8,128)S(1)} %copy.31), channel_id=1, source_target_pairs={{0,16},{16,32},{32,48},{48,64},{64,80},{80,96},{96,112},{112,128},... | collective-permute-start | bytes 49160 | tf_op jit(solution)/shard_map/ppermute | solution.py:17
  123.0 7.0 %collective-permute-start.3 = (f32[2,8,256,1]{2,1,3,0:T(8,128)S(1)}, f32[2,8,256,1]{2,1,3,0:T(8,128)S(1)}, u32[]{:S(2)}, u32[]{:S(2)}) collective-permute-start(f32[2,8,256,1]{2,1,3,0:T(8,128)S(1)} %copy.32), channel_id=1, source_target_pairs={{16,0},{32,16},{48,32},{64,48},{80,64},{96,80},{112,96},{128,112},... | collective-permute-start | bytes 49160 | tf_op jit(solution)/shard_map/ppermute | solution.py:19
  143.3 7.3 %collective-permute-start.4 = (f32[2,8,256,1]{2,1,3,0:T(8,128)S(1)}, f32[2,8,256,1]{2,1,3,0:T(8,128)S(1)}, u32[]{:S(2)}, u32[]{:S(2)}) collective-permute-start(f32[2,8,256,1]{2,1,3,0:T(8,128)S(1)} %copy.35), channel_id=1, source_target_pairs={{0,16},{16,32},{32,48},{48,64},{64,80},{80,96},{96,112},{112,128},... | collective-permute-start | bytes 49160 | tf_op jit(solution)/shard_map/ppermute | solution.py:17
  145.6 7.0 %collective-permute-start.5 = (f32[2,8,256,1]{2,1,3,0:T(8,128)S(1)}, f32[2,8,256,1]{2,1,3,0:T(8,128)S(1)}, u32[]{:S(2)}, u32[]{:S(2)}) collective-permute-start(f32[2,8,256,1]{2,1,3,0:T(8,128)S(1)} %copy.36), channel_id=1, source_target_pairs={{16,0},{32,16},{48,32},{64,48},{80,64},{96,80},{112,96},{128,112},... | collective-permute-start | bytes 49160 | tf_op jit(solution)/shard_map/ppermute | solution.py:19
  165.9 7.1 %collective-permute-start.6 = (f32[2,8,256,1]{2,1,3,0:T(8,128)S(1)}, f32[2,8,256,1]{2,1,3,0:T(8,128)S(1)}, u32[]{:S(2)}, u32[]{:S(2)}) collective-permute-start(f32[2,8,256,1]{2,1,3,0:T(8,128)S(1)} %copy.39), channel_id=1, source_target_pairs={{0,16},{16,32},{32,48},{48,64},{64,80},{80,96},{96,112},{112,128},... | collective-permute-start | bytes 49160 | tf_op jit(solution)/shard_map/ppermute | solution.py:17
  168.1 6.8 %collective-permute-start.7 = (f32[2,8,256,1]{2,1,3,0:T(8,128)S(1)}, f32[2,8,256,1]{2,1,3,0:T(8,128)S(1)}, u32[]{:S(2)}, u32[]{:S(2)}) collective-permute-start(f32[2,8,256,1]{2,1,3,0:T(8,128)S(1)} %copy.40), channel_id=1, source_target_pairs={{16,0},{32,16},{48,32},{64,48},{80,64},{96,80},{112,96},{128,112},... | collective-permute-start | bytes 49160 | tf_op jit(solution)/shard_map/ppermute | solution.py:19
  182.4 1.9 %copy-start.1 = (f32[16,128,128]{2,1,0:T(8,128)S(1)}, f32[16,128,128]{2,1,0:T(8,128)}, u32[]{:S(2)}) copy-start(f32[16,128,128]{2,1,0:T(8,128)} %param.14) | copy-start | bytes 3145732
where the time goes:
time: 185 us; the launch traced here: 184 us
  other arithmetic  44.7 us (24%)
  local copies, waits for them, and re-layouts  41.4 us (22%)
  waiting for transfers between devices  38.6 us (21%)
  starting transfers between devices  28.8 us (16%)
  blocking collectives  27 us (15%)
  matrix products  3.56 us (2%)
    all_to_all x1, blocking collectives, per_device(): lax.all_to_all(partial_value, 'band', split_axis=1, concat_axis=1, tiled=...  27 us
    all_to_all x1, waiting for transfers between devices, per_device(): lax.all_to_all(mixed, 'band', split_axis=0, concat_axis=1, tiled=True)  25.7 us
    ppermute x4, starting transfers between devices, with_halo(): lax.ppermute(head, axis, [((i + 1) % count, i) for i in range(count)])  18.9 us
    concatenate x4, other arithmetic, with_halo(): jnp.concatenate([lax.ppermute(tail, axis, [(i, (i + 1) % count) for i in...  15.6 us
    another operation x8, other arithmetic, per_device(): extended = with_halo(jnp.stack([result, courant_x]), (('region', 3),), 1)  13.5 us
    all_to_all x1, waiting for transfers between devices, per_device(): lax.all_to_all(courant_y, 'band', split_axis=0, concat_axis=1, tiled=True)  12.6 us
    slice x4, local copies, waits for them, and re-layouts, with_halo(): lax.slice_in_dim(cells, cells.shape[dim] - width, cells.shape[dim], axis=...  8.79 us
    ppermute x4, local copies, waits for them, and re-layouts, with_halo(): lax.ppermute(head, axis, [((i + 1) % count, i) for i in range(count)])  7.95 us
  transfers between devices with their start and end apart: 10, of which 3 were waited for; matrix products, arithmetic and copies ran while one was open for 17% of the time, Pallas kernels for 0%

commit v1 on v0

v1 whole, which is shorter than its diff:
```python
import jax
import jax.numpy as jnp
from jax import lax
from jax.sharding import PartitionSpec as P

YSTEPS = 2
XSTEPS = 4


def neighbours(head, tail, axis):
    count = lax.axis_size(axis)
    from_prev = lax.ppermute(tail, axis, [(i, (i + 1) % count) for i in range(count)])
    from_next = lax.ppermute(head, axis, [((i + 1) % count, i) for i in range(count)])
    return from_prev, from_next


def shrink_sweep(tracer, courant, dim):
    n = tracer.shape[dim]

    def cut(field, lo, hi):
        return lax.slice_in_dim(field, lo, hi, axis=dim)

    up = jnp.maximum(cut(courant, 1, n - 1), 0.0)
    low = jnp.minimum(cut(courant, 0, n - 2), 0.0)
    return (
        (1.0 - up + low) * cut(tracer, 1, n - 1)
        + up * cut(tracer, 2, n)
        - low * cut(tracer, 0, n - 2)
    )


def vertical_mix(field, diffusion_inverse, conv_weight, cloud_base, cloud_top):
    levels = jnp.arange(field.shape[0], dtype=jnp.int32)[:, None, None]
    inside = ((levels >= cloud_base[None]) & (levels <= cloud_top[None])).astype(jnp.float32)
    cloud_depth = (cloud_top - cloud_base + 1).astype(jnp.float32)
    column_mean = jnp.sum(inside * field, axis=0) / cloud_depth
    convected = field + conv_weight[None] * inside * (column_mean[None] - field)
    return jnp.einsum("jlk,lji->kji", diffusion_inverse, convected, precision=lax.Precision.HIGHEST)


def per_device(
    adjoint_in,
    courant_y,
    courant_x,
    diffusion_inverse,
    conv_weight,
    cloud_base,
    cloud_top,
    sound_count,
    xco2_adjoint,
    kernel,
    sound_cols,
):
    levels, lat_rows, lon_cells = adjoint_in.shape
    slot_count = kernel.shape[2]
    slot_index = jnp.arange(slot_count, dtype=jnp.int32)
    live_slot = slot_index[None, None, :] < sound_count[:, :, None]
    partial_value = jnp.where(live_slot, xco2_adjoint, 0.0)[..., None] * kernel
    arrived = lax.all_to_all(partial_value, "band", split_axis=1, concat_axis=1, tiled=True)
    flat_cols = sound_cols.reshape(-1)
    update = arrived.reshape(-1, levels).T
    column = adjoint_in.reshape(levels, lat_rows * lon_cells)
    forced = column.at[:, flat_cols].add(update).reshape(adjoint_in.shape)
    mixed = vertical_mix(forced, diffusion_inverse, conv_weight, cloud_base, cloud_top)

    band = lax.axis_index("band")
    last_band = lax.axis_size("band") - 1
    cy_prev, cy_next = neighbours(courant_y[:, :2], courant_y[:, -2:], "band")
    cy = jnp.concatenate([cy_prev, courant_y, cy_next], axis=1)
    row = jnp.arange(lat_rows + 4, dtype=jnp.int32) - 2 + band * lat_rows
    n_lat = lat_rows * (last_band + 1)
    cy = jnp.where(((row >= 0) & (row < n_lat - 1))[None, :, None], cy, 0.0)
    m_prev, m_next = neighbours(mixed[:, :2], mixed[:, -2:], "band")
    m_prev = jnp.where(band > 0, m_prev, 0.0)
    m_next = jnp.where(band < last_band, m_next, 0.0)
    tracer = jnp.concatenate([m_prev, mixed, m_next], axis=1)
    tracer = shrink_sweep(tracer, cy, 1)
    tracer = shrink_sweep(tracer, cy[:, 1:-1], 1)

    slab = lax.all_to_all(tracer, "band", split_axis=0, concat_axis=1, tiled=True)
    cx_prev, cx_next = neighbours(courant_x[:, :, :XSTEPS], courant_x[:, :, -XSTEPS:], "region")
    cx = jnp.concatenate([cx_prev, courant_x, cx_next], axis=2)
    s_prev, s_next = neighbours(slab[:, :, :XSTEPS], slab[:, :, -XSTEPS:], "region")
    result = jnp.concatenate([s_prev, slab, s_next], axis=2)
    for step in range(XSTEPS):
        result = shrink_sweep(result, cx[:, :, step : cx.shape[2] - step], 2)
    return result


def solution(mesh):
    in_specs = (
        P(None, "band", "region"),
        P(None, "band", "region"),
        P("band", None, "region"),
        P("band", None, None),
        P("band", "region"),
        P("band", "region"),
        P("band", "region"),
        P("region", "band"),
        P("region", "band", None),
        P("region", "band", None, None),
        P("region", "band", None),
    )
    out_specs = P("band", None, "region")
    return jax.shard_map(
        per_device, mesh=mesh, in_specs=in_specs, out_specs=out_specs, check_vma=False
    )
```

time: 185 us -> 110 us (0.59)
  blocking collectives: 27 us -> 0 us
  local copies, waits for them, and re-layouts: 41.4 us -> 16.1 us
  other arithmetic: 44.7 us -> 26.8 us
  waiting for transfers between devices: 38.6 us -> 34.7 us
  starting transfers between devices: 28.8 us -> 26.7 us
    all_to_all x1 -> x0, blocking collectives: 27 us -> none  [per_device(): lax.all_to_all(partial_value, 'band', split_axis=1, concat_axis=1, tiled=...]
    slice x14 -> x6, local copies, waits for them, and re-layouts: 19.3 us -> 3.35 us  [the longest x1 1.66 us: per_device(): courant_x[:, :, -XSTEPS:]]
    another operation x8 -> x0, other arithmetic: 13.5 us -> none  [per_device(): extended = with_halo(jnp.stack([result, courant_x]), (('region', 3),), 1)]
    all_to_all x2, waiting for transfers between devices: 38.3 us -> 27.4 us  [the longest x1 15.4 us: per_device(): lax.all_to_all(tracer, 'band', split_axis=0, concat_axis=1, tiled=True)]
    ppermute x8 -> x4, local copies, waits for them, and re-layouts: 15.8 us -> 5.41 us  [the longest x2 2.72 us: neighbours(): lax.ppermute(tail, axis, [(i, (i + 1) % count) for i in range(count)])]
    concatenate x4 -> x2, other arithmetic: 15.6 us -> 5.46 us  [the longest x1 2.73 us: per_device(): cx = jnp.concatenate([cx_prev, courant_x, cx_next], axis=2)]
    ppermute x8, starting transfers between devices: 20.3 us -> 12.2 us  [the longest x4 9.27 us: neighbours(): lax.ppermute(head, axis, [((i + 1) % count, i) for i in range(count)])]
    ppermute x8, waiting for transfers between devices: 0.29 us -> 7.26 us  [the longest x4 4.61 us: neighbours(): lax.ppermute(tail, axis, [(i, (i + 1) % count) for i in range(count)])]
  transfers between devices with their start and end apart: 10 -> 10, of which waited for: 3 -> 5; matrix products, arithmetic and copies ran while one was open for 17% -> 26% of each run, Pallas kernels for 0% -> 0%
where the time goes in v1:
time: 110 us; the launch traced here: 109 us
  waiting for transfers between devices  34.7 us (32%)
  other arithmetic  26.8 us (24%)
  starting transfers between devices  26.7 us (24%)
  local copies, waits for them, and re-layouts  16.1 us (15%)
  matrix products  4.56 us (4%)
    all_to_all x1, waiting for transfers between devices, per_device(): lax.all_to_all(tracer, 'band', split_axis=0, concat_axis=1, tiled=True)  15.4 us
    all_to_all x1, waiting for transfers between devices, per_device(): lax.all_to_all(partial_value, 'band', split_axis=1, concat_axis=1, tiled=...  12 us
    all_to_all x1, starting transfers between devices, per_device(): lax.all_to_all(partial_value, 'band', split_axis=1, concat_axis=1, tiled=...  10.1 us
    ppermute x4, starting transfers between devices, neighbours(): lax.ppermute(head, axis, [((i + 1) % count, i) for i in range(count)])  9.27 us
    sub x6, other arithmetic, shrink_sweep(): (1.0 - up + low) * cut(tracer, 1, n - 1) + up * cut(tracer, 2, n)  9.23 us
    scatter-add x1, other arithmetic, per_device(): forced = column.at[:, flat_cols].add(update).reshape(adjoint_in.shape)  6.82 us
    unnamed x24, local copies, waits for them, and re-layouts  5.76 us
    ppermute x4, waiting for transfers between devices, neighbours(): lax.ppermute(tail, axis, [(i, (i + 1) % count) for i in range(count)])  4.61 us
  transfers between devices with their start and end apart: 10, of which 5 were waited for; matrix products, arithmetic and copies ran while one was open for 26% of the time, Pallas kernels for 0%

profile of v1, /device:TPU:1, one launch (start us, length us, event | category | flops | bytes accessed | tf_op | source)
XLA Modules:
  0.0 109.0 jit_solution(16841061970721969536)
XLA Ops:
  0.0 0.9 select_bitcast_fusion
  0.9 2.0 %bitcast_multiply_fusion = f32[1,16,64,128]{3,2,0,1:T(8,128)} fusion(f32[1,16,64,128]{3,2,1,0:T(8,128)} %param.20, f32[16,64]{1,0:T(8,128)S(1)} %select_bitcast_fusion), kind=kLoop, calls=%fused_computation.63 | loop fusion | flops 131072 | bytes 1052672 | tf_op jit(solution)/shard_map/mul | solution.py:58
  3.0 10.1 %all-to-all-start = ((f32[1,16,64,128]{3,2,0,1:T(8,128)}), f32[1,16,64,128]{3,2,0,1:T(8,128)}, u32[]{:S(2)}, u32[]{:S(2)}) async-start(f32[1,16,64,128]{3,2,0,1:T(8,128)} %bitcast_multiply_fusion), calls=%async_computation | async-start | bytes 1048576 | tf_op jit(solution)/shard_map/all_to_all | solution.py:59
  13.1 0.4 copy.33
  13.5 0.7 fusion.31
  14.2 1.6 %collective-permute-start.2 = (f32[128,2,128]{0,2,1:T(8,128)}, f32[128,2,128]{0,2,1:T(8,128)S(1)}, u32[]{:S(2)}, u32[]{:S(2)}) collective-permute-start(f32[128,2,128]{0,2,1:T(8,128)} %get-tuple-element.9), channel_id=1, source_target_pairs={{0,1},{1,2},{2,3},{3,4},{4,5},{5,6},{6,7},{7,8},{8,9},{9,10},{10,1... | collective-permute-start | bytes 393224 | tf_op jit(solution)/shard_map/ppermute | solution.py:12
  15.8 0.1 reshape.98
  15.9 1.6 %copy.36 = f32[128,16,128]{0,2,1:T(8,128)S(1)} copy(f32[128,16,128]{2,1,0:T(8,128)} %param.11) | data formatting | bytes 2097152 | tf_op args[0]
  17.5 0.5 compare_and_fusion
  18.0 0.6 compare_select_fusion
  18.6 12.0 %all-to-all-done = f32[1,16,64,128]{3,2,0,1:T(8,128)} async-done(((f32[1,16,64,128]{3,2,0,1:T(8,128)}), f32[1,16,64,128]{3,2,0,1:T(8,128)}, u32[]{:S(2)}, u32[]{:S(2)}) %all-to-all-start) | async-done | bytes 524320 | tf_op jit(solution)/shard_map/all_to_all | solution.py:59
  30.6 6.8 %scatter_fusion = f32[128,2048]{0,1:T(8,128)S(1)} fusion(f32[128,2048]{0,1:T(8,128)S(1)} %bitcast.20, s32[1024]{0:T(1024)} %bitcast.27, f32[1024,128]{1,0:T(8,128)} %bitcast.5), kind=kCustom, calls=%fused_computation | custom fusion | flops 131072 | bytes 1576960 | tf_op jit(solution)/shard_map/scatter-add | solution.py:63
  37.4 1.0 select_reduce_fusion
  38.5 4.6 %convolution_bitcast_fusion = f32[128,16,128]{0,2,1:T(8,128)S(1)} fusion(f32[16,128,128]{2,1,0:T(8,128)S(1)} %copy-done, f32[128,16,128]{0,2,1:T(8,128)S(1)} %bitcast.21, f32[16,128]{1,0:T(8,128)S(1)} %bitcast_divide_fusion, f32[16,128]{1,0:T(8,128)} %param.15, s32[16,128]{1,0:T(8,128)S(1)} %copy-done.6, s32[16,128]{1,0:T(8,128)S(1)} %copy-done.7), kind=kOutput, calls=%fused_computation.27 | convolution fusion | flops 404488192 | bytes 3178496 | tf_op jit(solution)/shard_map/jlk,lji->kji/dot_general | solution.py:38
  43.1 0.0 collective-permute-start.4
  43.1 0.2 maximum_select_fusion
  43.3 0.5 collective-permute-start.5
  43.8 1.3 %collective-permute-done.4 = f32[128,2,128]{0,2,1:T(8,128)S(1)} collective-permute-done((f32[128,2,128]{0,2,1:T(8,128)S(1)}, f32[128,2,128]{0,2,1:T(8,128)S(1)}, u32[]{:S(2)}, u32[]{:S(2)}) %collective-permute-start.4) | collective-permute-done | bytes 131104 | tf_op jit(solution)/shard_map/ppermute | solution.py:12
  45.0 2.6 %collective-permute-done.5 = f32[128,2,128]{0,2,1:T(8,128)S(1)} collective-permute-done((f32[128,2,128]{0,2,1:T(8,128)S(1)}, f32[128,2,128]{0,2,1:T(8,128)S(1)}, u32[]{:S(2)}, u32[]{:S(2)}) %collective-permute-start.5) | collective-permute-done | bytes 131104 | tf_op jit(solution)/shard_map/ppermute | solution.py:13
  47.7 0.4 fusion.9
  48.0 0.3 fusion.14
  48.4 0.0 copy-start.1
  48.4 1.4 %copy.38 = f32[128,16,128]{2,1,0:T(8,128)} copy(f32[128,16,128]{0,2,1:T(8,128)S(1)} %fusion.14) | data formatting | bytes 2097152 | tf_op jit(solution)/shard_map/sub | solution.py:26
  49.8 4.4 %all-to-all-start.1 = ((f32[128,16,128]{2,1,0:T(8,128)}), f32[128,16,128]{2,1,0:T(8,128)S(1)}, u32[]{:S(2)}, u32[]{:S(2)}) async-start(f32[128,16,128]{2,1,0:T(8,128)} %copy.38), calls=%async_computation.1 | async-start | bytes 2097152 | tf_op jit(solution)/shard_map/all_to_all | solution.py:80
  54.2 1.7 %fusion.29 = (f32[8,256,4]{2,1,0:T(8,128)}, f32[8,256,4]{2,1,0:T(8,128)}) fusion(f32[8,256,128]{2,1,0:T(8,128)S(1)} %copy-done.1), kind=kLoop, calls=%fused_computation.77 | loop fusion | bytes 131072 | tf_op jit(solution)/shard_map/slice | solution.py:81
  55.8 1.5 %copy.44 = f32[8,256,4]{1,0,2:T(8,128)S(1)} copy(f32[8,256,4]{2,1,0:T(8,128)} %get-tuple-element.5) | data formatting | bytes 65536
  57.4 1.3 %collective-permute-start = (f32[8,256,4]{1,0,2:T(8,128)S(1)}, f32[8,256,4]{1,0,2:T(8,128)S(1)}, u32[]{:S(2)}, u32[]{:S(2)}) collective-permute-start(f32[8,256,4]{1,0,2:T(8,128)S(1)} %copy.44), channel_id=1, source_target_pairs={{0,16},{16,32},{32,48},{48,64},{64,80},{80,96},{96,112},{112,128},... | collective-permute-start | bytes 98312 | tf_op jit(solution)/shard_map/ppermute | solution.py:12
  58.6 1.5 %copy.45 = f32[8,256,4]{1,0,2:T(8,128)S(1)} copy(f32[8,256,4]{2,1,0:T(8,128)} %get-tuple-element.6) | data formatting | bytes 65536
  60.2 3.8 %collective-permute-start.1 = (f32[8,256,4]{1,0,2:T(8,128)S(1)}, f32[8,256,4]{1,0,2:T(8,128)S(1)}, u32[]{:S(2)}, u32[]{:S(2)}) collective-permute-start(f32[8,256,4]{1,0,2:T(8,128)S(1)} %copy.45), channel_id=1, source_target_pairs={{16,0},{32,16},{48,32},{64,48},{80,64},{96,80},{112,96},{128,112},... | collective-permute-start | bytes 98312 | tf_op jit(solution)/shard_map/ppermute | solution.py:13
  64.0 1.4 %copy.29 = f32[8,256,4]{2,1,0:T(8,128)} copy(f32[8,256,4]{1,0,2:T(8,128)S(1)} %collective-permute-done) | data formatting | bytes 65536 | tf_op jit(solution)/shard_map/ppermute | solution.py:12
  65.4 1.4 %copy.32 = f32[8,256,4]{2,1,0:T(8,128)} copy(f32[8,256,4]{1,0,2:T(8,128)S(1)} %collective-permute-done.1) | data formatting | bytes 65536 | tf_op jit(solution)/shard_map/ppermute | solution.py:13
  66.7 15.4 %all-to-all-done.1 = f32[128,16,128]{2,1,0:T(8,128)S(1)} async-done(((f32[128,16,128]{2,1,0:T(8,128)}), f32[128,16,128]{2,1,0:T(8,128)S(1)}, u32[]{:S(2)}, u32[]{:S(2)}) %all-to-all-start.1) | async-done | bytes 1048608 | tf_op jit(solution)/shard_map/all_to_all | solution.py:80
  82.2 0.1 copy.39
  82.2 0.3 fusion.30
  82.6 0.6 copy-done.4
  83.2 0.3 copy.40
  83.5 0.3 copy.41
  83.9 5.0 %collective-permute-start.7 = (f32[8,256,4]{1,0,2:T(8,128)S(1)}, f32[8,256,4]{1,0,2:T(8,128)S(1)}, u32[]{:S(2)}, u32[]{:S(2)}) collective-permute-start(f32[8,256,4]{1,0,2:T(8,128)S(1)} %copy.41), channel_id=1, source_target_pairs={{16,0},{32,16},{48,32},{64,48},{80,64},{96,80},{112,96},{128,112},... | collective-permute-start | bytes 98312 | tf_op jit(solution)/shard_map/ppermute | solution.py:13
  88.9 2.7 %pad_maximum_fusion.1 = f32[8,256,136]{2,1,0:T(8,128)S(1)} fusion(f32[8,256,4]{2,1,0:T(8,128)} %copy.32, f32[8,256,128]{2,1,0:T(8,128)} %param.13, f32[8,256,4]{2,1,0:T(8,128)} %copy.29), kind=kLoop, calls=%fused_computation.25 | loop fusion | flops 557056 | bytes 2228224 | tf_op jit(solution)/shard_map/concatenate | solution.py:82
  91.6 3.3 %collective-permute-done.6 = f32[8,256,4]{1,0,2:T(8,128)S(1)} collective-permute-done((f32[8,256,4]{1,0,2:T(8,128)S(1)}, f32[8,256,4]{1,0,2:T(8,128)S(1)}, u32[]{:S(2)}, u32[]{:S(2)}) %collective-permute-start.6) | collective-permute-done | bytes 32800 | tf_op jit(solution)/shard_map/ppermute | solution.py:12
  95.0 1.4 %copy.42 = f32[8,256,4]{2,1,0:T(8,128)} copy(f32[8,256,4]{1,0,2:T(8,128)S(1)} %collective-permute-done.6) | data formatting | bytes 65536 | tf_op jit(solution)/shard_map/ppermute | solution.py:12
  96.3 1.3 %copy.43 = f32[8,256,4]{2,1,0:T(8,128)} copy(f32[8,256,4]{1,0,2:T(8,128)S(1)} %collective-permute-done.7) | data formatting | bytes 65536 | tf_op jit(solution)/shard_map/ppermute | solution.py:13
  97.7 2.7 %pad_maximum_fusion.2 = f32[8,256,136]{2,1,0:T(8,128)S(1)} fusion(f32[8,256,4]{2,1,0:T(8,128)} %copy.43, f32[8,256,128]{2,1,0:T(8,128)} %bitcast.23, f32[8,256,4]{2,1,0:T(8,128)} %copy.42), kind=kLoop, calls=%fused_computation.26 | loop fusion | flops 557056 | bytes 2228224 | tf_op jit(solution)/shard_map/concatenate | solution.py:84
  100.4 1.7 %fusion.4 = f32[8,256,134]{2,1,0:T(8,128)S(1)} fusion(f32[8,256,136]{2,1,0:T(8,128)S(1)} %pad_maximum_fusion.2, f32[8,256,136]{2,1,0:T(8,128)S(1)} %pad_maximum_fusion.1), kind=kLoop, calls=%fused_computation.12 | loop fusion | flops 2469888 | bytes 6586368 | tf_op jit(solution)/shard_map/sub | solution.py:26
  102.1 0.0 copy-start.2
  102.1 2.2 %fusion.2 = f32[8,256,132]{2,1,0:T(8,128)S(1)} fusion(f32[8,256,134]{2,1,0:T(8,128)S(1)} %fusion.4, f32[8,256,136]{2,1,0:T(8,128)S(1)} %pad_maximum_fusion.1), kind=kLoop, calls=%fused_computation.7 | loop fusion | flops 2433024 | bytes 6488064 | tf_op jit(solution)/shard_map/sub | solution.py:26
  104.4 2.5 %fusion = f32[8,256,130]{2,1,0:T(8,128)S(1)} fusion(f32[8,256,132]{2,1,0:T(8,128)S(1)} %fusion.2, f32[8,256,128]{2,1,0:T(8,128)S(1)} %copy-done.2, f32[8,256,4]{2,1,0:T(8,128)S(1)} %copy-done.3, f32[8,256,136]{2,1,0:T(8,128)S(1)} %pad_maximum_fusion.1), kind=kLoop, calls=%fused_computation.2 | loop fusion | flops 2662400 | bytes 6406144 | tf_op jit(solution)/shard_map/sub | solution.py:26
  106.9 2.1 %fusion.12 = f32[8,256,128]{2,1,0:T(8,128)} fusion(f32[8,256,130]{2,1,0:T(8,128)S(1)} %fusion, f32[8,256,128]{2,1,0:T(8,128)S(1)} %copy-done.2, f32[8,256,4]{2,1,0:T(8,128)S(1)} %copy-done.3), kind=kLoop, calls=%fused_computation.41 | loop fusion | flops 2621440 | bytes 5275648 | tf_op jit(solution)/shard_map/sub | solution.py:26
  (28 shorter events, 0.1 us)
Async XLA Ops:
  0.0 38.4 %copy-start = (f32[16,128,128]{2,1,0:T(8,128)S(1)}, f32[16,128,128]{2,1,0:T(8,128)}, u32[]{:S(2)}) copy-start(f32[16,128,128]{2,1,0:T(8,128)} %param.14) | copy-start | bytes 3145732
  0.0 13.1 %copy-start.5 = (f32[128,16,128]{2,1,0:T(8,128)S(1)}, f32[128,16,128]{2,1,0:T(8,128)}, u32[]{:S(2)}) copy-start(f32[128,16,128]{2,1,0:T(8,128)} %param.12) | copy-start | bytes 3145732
  3.0 12.8 %copy-start.8 = (s32[1,16,64]{2,1,0:T(8,128)S(1)}, s32[1,16,64]{2,1,0:T(8,128)}, u32[]{:S(2)}) copy-start(s32[1,16,64]{2,1,0:T(8,128)} %param.21) | copy-start | bytes 12292
  3.0 27.6 %all-to-all-start = ((f32[1,16,64,128]{3,2,0,1:T(8,128)}), f32[1,16,64,128]{3,2,0,1:T(8,128)}, u32[]{:S(2)}, u32[]{:S(2)}) async-start(f32[1,16,64,128]{3,2,0,1:T(8,128)} %bitcast_multiply_fusion), calls=%async_computation | async-start | bytes 1048576 | tf_op jit(solution)/shard_map/all_to_all | solution.py:59
  14.2 28.9 %collective-permute-start.2 = (f32[128,2,128]{0,2,1:T(8,128)}, f32[128,2,128]{0,2,1:T(8,128)S(1)}, u32[]{:S(2)}, u32[]{:S(2)}) collective-permute-start(f32[128,2,128]{0,2,1:T(8,128)} %get-tuple-element.9), channel_id=1, source_target_pairs={{0,1},{1,2},{2,3},{3,4},{4,5},{5,6},{6,7},{7,8},{8,9},{9,10},{10,1... | collective-permute-start | bytes 393224 | tf_op jit(solution)/shard_map/ppermute | solution.py:12
  15.8 27.3 %collective-permute-start.3 = (f32[128,2,128]{0,2,1:T(8,128)S(1)}, f32[128,2,128]{0,2,1:T(8,128)S(1)}, u32[]{:S(2)}, u32[]{:S(2)}) collective-permute-start(f32[128,2,128]{0,2,1:T(8,128)S(1)} %get-tuple-element.10), channel_id=1, source_target_pairs={{1,0},{2,1},{3,2},{4,3},{5,4},{6,5},{7,6},{8,7},{9,8},{10,9},{11,1... | collective-permute-start | bytes 393224 | tf_op jit(solution)/shard_map/ppermute | solution.py:13
  30.6 6.8 %copy-start.6 = (s32[16,128]{1,0:T(8,128)S(1)}, s32[16,128]{1,0:T(8,128)}, u32[]{:S(2)}) copy-start(s32[16,128]{1,0:T(8,128)} %param.17) | copy-start | bytes 24580
  30.6 6.8 %copy-start.7 = (s32[16,128]{1,0:T(8,128)S(1)}, s32[16,128]{1,0:T(8,128)}, u32[]{:S(2)}) copy-start(s32[16,128]{1,0:T(8,128)} %param.16) | copy-start | bytes 24580
  38.4 4.7 %copy-start.9 = (pred[20]{0:T(512)(128)(4,1)S(1)}, pred[20]{0:T(512)(128)(4,1)}, u32[]{:S(2)}) copy-start(pred[20]{0:T(512)(128)(4,1)} %compare_and_fusion) | copy-start | bytes 64
  43.1 2.0 %collective-permute-start.4 = (f32[128,2,128]{0,2,1:T(8,128)S(1)}, f32[128,2,128]{0,2,1:T(8,128)S(1)}, u32[]{:S(2)}, u32[]{:S(2)}) collective-permute-start(f32[128,2,128]{0,2,1:T(8,128)S(1)} %get-tuple-element.11), channel_id=1, source_target_pairs={{0,1},{1,2},{2,3},{3,4},{4,5},{5,6},{6,7},{7,8},{8,9},{9,10},{10,1... | collective-permute-start | bytes 393224 | tf_op jit(solution)/shard_map/ppermute | solution.py:12
  43.3 4.4 %collective-permute-start.5 = (f32[128,2,128]{0,2,1:T(8,128)S(1)}, f32[128,2,128]{0,2,1:T(8,128)S(1)}, u32[]{:S(2)}, u32[]{:S(2)}) collective-permute-start(f32[128,2,128]{0,2,1:T(8,128)S(1)} %get-tuple-element.12), channel_id=1, source_target_pairs={{1,0},{2,1},{3,2},{4,3},{5,4},{6,5},{7,6},{8,7},{9,8},{10,9},{11,1... | collective-permute-start | bytes 393224 | tf_op jit(solution)/shard_map/ppermute | solution.py:13
  48.4 5.8 %copy-start.1 = (f32[8,256,128]{2,1,0:T(8,128)S(1)}, f32[8,256,128]{2,1,0:T(8,128)}, u32[]{:S(2)}) copy-start(f32[8,256,128]{2,1,0:T(8,128)} %param.13) | copy-start | bytes 3145732
  49.8 32.4 %all-to-all-start.1 = ((f32[128,16,128]{2,1,0:T(8,128)}), f32[128,16,128]{2,1,0:T(8,128)S(1)}, u32[]{:S(2)}, u32[]{:S(2)}) async-start(f32[128,16,128]{2,1,0:T(8,128)} %copy.38), calls=%async_computation.1 | async-start | bytes 2097152 | tf_op jit(solution)/shard_map/all_to_all | solution.py:80
  57.4 6.6 %collective-permute-start = (f32[8,256,4]{1,0,2:T(8,128)S(1)}, f32[8,256,4]{1,0,2:T(8,128)S(1)}, u32[]{:S(2)}, u32[]{:S(2)}) collective-permute-start(f32[8,256,4]{1,0,2:T(8,128)S(1)} %copy.44), channel_id=1, source_target_pairs={{0,16},{16,32},{32,48},{48,64},{64,80},{80,96},{96,112},{112,128},... | collective-permute-start | bytes 98312 | tf_op jit(solution)/shard_map/ppermute | solution.py:12
  60.2 5.2 %collective-permute-start.1 = (f32[8,256,4]{1,0,2:T(8,128)S(1)}, f32[8,256,4]{1,0,2:T(8,128)S(1)}, u32[]{:S(2)}, u32[]{:S(2)}) collective-permute-start(f32[8,256,4]{1,0,2:T(8,128)S(1)} %copy.45), channel_id=1, source_target_pairs={{16,0},{32,16},{48,32},{64,48},{80,64},{96,80},{112,96},{128,112},... | collective-permute-start | bytes 98312 | tf_op jit(solution)/shard_map/ppermute | solution.py:13
  82.2 1.0 copy-start.4
  83.9 12.4 %collective-permute-start.7 = (f32[8,256,4]{1,0,2:T(8,128)S(1)}, f32[8,256,4]{1,0,2:T(8,128)S(1)}, u32[]{:S(2)}, u32[]{:S(2)}) collective-permute-start(f32[8,256,4]{1,0,2:T(8,128)S(1)} %copy.41), channel_id=1, source_target_pairs={{16,0},{32,16},{48,32},{64,48},{80,64},{96,80},{112,96},{128,112},... | collective-permute-start | bytes 98312 | tf_op jit(solution)/shard_map/ppermute | solution.py:13
  88.9 6.1 %collective-permute-start.6 = (f32[8,256,4]{1,0,2:T(8,128)S(1)}, f32[8,256,4]{1,0,2:T(8,128)S(1)}, u32[]{:S(2)}, u32[]{:S(2)}) collective-permute-start(f32[8,256,4]{1,0,2:T(8,128)S(1)} %copy.40), channel_id=1, source_target_pairs={{0,16},{16,32},{32,48},{48,64},{64,80},{80,96},{96,112},{112,128},... | collective-permute-start | bytes 98312 | tf_op jit(solution)/shard_map/ppermute | solution.py:12
  102.1 2.3 %copy-start.2 = (f32[8,256,128]{2,1,0:T(8,128)S(1)}, f32[8,256,128]{2,1,0:T(8,128)}, u32[]{:S(2)}) copy-start(f32[8,256,128]{2,1,0:T(8,128)} %param.13) | copy-start | bytes 3145732
  102.1 2.3 %copy-start.3 = (f32[8,256,4]{2,1,0:T(8,128)S(1)}, f32[8,256,4]{2,1,0:T(8,128)}, u32[]{:S(2)}) copy-start(f32[8,256,4]{2,1,0:T(8,128)} %copy.29) | copy-start | bytes 98308

commit v2 on v1

v2 whole, which is shorter than its diff:
```python
import jax
import jax.numpy as jnp
from jax import lax
from jax.experimental import pallas as pl
from jax.experimental.pallas import tpu as pltpu
from jax.sharding import PartitionSpec as P


XSTEPS = 4
LEV = 128
ROWS = 16
LON = 128
BANDS = 16
SLAB = 8
STRIP = 16
HALVES = 2
GROUP = 4
CHUNK = 4
WIDE = ROWS + 4

f32 = jnp.float32
bf16 = jnp.bfloat16


def split(x):
    hi = x.astype(bf16)
    return hi, (x - hi.astype(f32)).astype(bf16)


def lane_iota(shape):
    return lax.broadcasted_iota(jnp.int32, shape, len(shape) - 1)


def turned(x, shift):
    shift %= LON
    return pltpu.roll(x, shift, x.ndim - 1) if shift else x


def pack_strips(tile_of):
    left, right = [], []
    for half in range(HALVES):
        west = east = None
        for g in range(ROWS // HALVES):
            tile = tile_of(half * (ROWS // HALVES) + g)
            here = lane_iota(tile.shape) // STRIP == g
            to_west = turned(tile, STRIP * g + XSTEPS)
            to_east = turned(tile, STRIP * g + STRIP - XSTEPS)
            west = to_west if west is None else jnp.where(here, to_west, west)
            east = to_east if east is None else jnp.where(here, to_east, east)
        left.append(west)
        right.append(east)
    return left, right


def scale_kernel(count_hbm, value_hbm, kern_hbm, out_hbm, count, value, kern, sem, kern_sem, out_sem):
    small = [
        pltpu.make_async_copy(count_hbm, count, sem.at[0]),
        pltpu.make_async_copy(value_hbm, value, sem.at[1]),
    ]
    spans = [pl.ds(c * GROUP, GROUP) for c in range(BANDS // GROUP)]
    loads = [pltpu.make_async_copy(kern_hbm.at[0, spans[c]], kern.at[spans[c]], kern_sem.at[c]) for c in range(len(spans))]
    stores = [pltpu.make_async_copy(kern.at[spans[c]], out_hbm.at[spans[c]], out_sem.at[c]) for c in range(len(spans))]
    for copy in small + loads:
        copy.start()
    for copy in small:
        copy.wait()
    factor = value[0].T
    live = lax.broadcasted_iota(jnp.int32, factor.shape, 0) < count[...]
    factor = jnp.where(live, factor, 0.0)
    for c in range(len(spans)):
        loads[c].wait()
        for band in range(c * GROUP, c * GROUP + GROUP):
            kern[band] = kern[band] * factor[:, band : band + 1]
        stores[c].start()
    for copy in stores:
        copy.wait()


def prepare_kernel(field_hbm, cy_hbm, diff_hbm, field_out, cy_out, diff_out, field, cy, diff, parts, sem, out_sem):
    loads = [
        pltpu.make_async_copy(diff_hbm, diff, sem.at[0]),
        pltpu.make_async_copy(field_hbm, field, sem.at[1]),
        pltpu.make_async_copy(cy_hbm, cy, sem.at[2]),
    ]
    for copy in loads:
        copy.start()
    loads[0].wait()
    for row in range(ROWS):
        hi, lo = split(diff[row].T)
        parts[row, 0] = hi
        parts[row, 1] = lo
    store = pltpu.make_async_copy(parts, diff_out, out_sem)
    store.start()
    loads[1].wait()
    for row in range(ROWS):
        field_out[row] = field[:, row, :]
    loads[2].wait()
    for row in range(ROWS):
        cy_out[row] = cy[:, row, :]
    store.wait()


def faces_kernel(cx_ref, cx_out, left_out, right_out):
    def source(s, carry):
        def tile_of(row):
            tile = cx_ref[:, pl.ds(s * ROWS + row, 1), :].reshape(SLAB, LON)
            cx_out[s * ROWS + row] = tile
            return tile

        left, right = pack_strips(tile_of)
        for half in range(HALVES):
            left_out[s, half] = left[half]
            right_out[s, half] = right[half]
        return carry

    lax.fori_loop(0, BANDS, source, 0)


def fill_halo(left, right, west, east):
    spot = lane_iota(left.shape) % STRIP
    left = jnp.where(spot < XSTEPS, turned(west, XSTEPS - STRIP + XSTEPS), left)
    right = jnp.where(spot >= STRIP - XSTEPS, turned(east, STRIP - 2 * XSTEPS), right)
    return left, right


def stencil_of(courant):
    up = jnp.maximum(courant, 0.0)
    low = turned(jnp.minimum(courant, 0.0), 1)
    return 1.0 - up + low, up, low


def zonal_sweep(value, keep, up, low):
    return keep * value + up * turned(value, -1) - low * turned(value, 1)


def sides_kernel(left_ref, right_ref, west_ref, east_ref, coef_out):
    def source(s, carry):
        for half in range(HALVES):
            strips = fill_halo(left_ref[s, half], right_ref[s, half], west_ref[s, half], east_ref[s, half])
            for side in range(2):
                for k, value in enumerate(stencil_of(strips[side])):
                    coef_out[s, half, side, k] = value
        return carry

    lax.fori_loop(0, BANDS, source, 0)


def mix_kernel(
    kern_ref, cols_ref, field_ref, cy_ref, before_ref, after_ref, diff_hbm, conv_hbm, base_hbm, top_hbm,
    block_out,
    parts, onehot, mixed, once, diff_buf, conv_ref, base_ref, top_ref, diff_sem, sem,
):
    def diff_copy(g):
        span = pl.ds(g * GROUP, GROUP)
        return pltpu.make_async_copy(diff_hbm.at[span], diff_buf.at[span], diff_sem.at[g])

    small = [
        pltpu.make_async_copy(conv_hbm, conv_ref, sem.at[0]),
        pltpu.make_async_copy(base_hbm, base_ref, sem.at[1]),
        pltpu.make_async_copy(top_hbm, top_ref, sem.at[2]),
    ]
    for copy in small + [diff_copy(g) for g in range(ROWS // GROUP)]:
        copy.start()
    for c in range(8):
        span = slice(c * 128, c * 128 + 128)
        hi, lo = split(kern_ref[span, :])
        parts[span, :LEV] = hi
        parts[span, LEV:] = lo

    for copy in small:
        copy.wait()
    level = lax.broadcasted_iota(jnp.int32, (LEV, LON), 0)

    def group(g, carry):
        cols = cols_ref[...] - g * (GROUP * LON)
        for r in range(0, GROUP * LON, 32):
            cell = lax.broadcasted_iota(jnp.int32, (32, cols.shape[1]), 0) + r
            onehot[pl.ds(r, 32), :] = jnp.where(cell == cols, 1.0, 0.0).astype(bf16)
        both = jnp.dot(onehot[...], parts[...], preferred_element_type=f32)
        added = both[:, :LEV] + both[:, LEV:]
        diff_copy(g).wait()
        for q in range(GROUP):
            row = g * GROUP + q
            forced = field_ref[row] + added[q * LON : (q + 1) * LON].T
            base = base_ref[pl.ds(row, 1), :]
            top = top_ref[pl.ds(row, 1), :]
            inside = jnp.where((level >= base) & (level <= top), 1.0, 0.0)
            mean = jnp.sum(inside * forced, axis=0, keepdims=True) / (top - base + 1).astype(f32)
            convected = forced + conv_ref[pl.ds(row, 1), :] * inside * (mean - forced)
            hi, lo = split(convected)
            d_hi = diff_buf[row, 0]
            d_lo = diff_buf[row, 1]
            mixed[row] = (
                jnp.dot(d_hi, lo, preferred_element_type=f32)
                + jnp.dot(d_lo, hi, preferred_element_type=f32)
                + jnp.dot(d_hi, hi, preferred_element_type=f32)
            )
        return carry

    lax.fori_loop(0, ROWS // GROUP, group, 0)
    open_face = jnp.where(lax.axis_index("band") == BANDS - 1, 0.0, 1.0)

    def face(row):
        if row < 0:
            return before_ref[row + 2]
        if row == ROWS:
            return after_ref[0]
        return cy_ref[row] * open_face if row == ROWS - 1 else cy_ref[row]

    def partial_sweep(value, first, last, row):
        own = value(row) if first <= row <= last else None
        terms = []
        if own is not None or row - 1 >= first:
            low = jnp.minimum(face(row - 1), 0.0) if row > -2 else None
        if own is not None:
            terms.append((1.0 - jnp.maximum(face(row), 0.0) + low) * own)
        if first <= row + 1 <= last:
            terms.append(jnp.maximum(face(row), 0.0) * value(row + 1))
        if first <= row - 1 <= last:
            terms.append(-(low * value(row - 1)))
        return sum(terms[1:], terms[0])

    for row in range(-1, ROWS + 1):
        once[row + 1] = partial_sweep(lambda r: mixed[r], 0, ROWS - 1, row)
    for row in range(-2, ROWS + 2):
        value = partial_sweep(lambda r: once[r + 1], -1, ROWS, row)
        block_out[:, row + 2] = value.reshape(BANDS, SLAB, LON)


def summed(rows_ref, s, row):
    value = rows_ref[s, row + 2]
    if row < 2:
        value += jnp.where(s > 0, rows_ref[jnp.maximum(s - 1, 0), row + ROWS + 2], 0.0)
    if row >= ROWS - 2:
        value += jnp.where(s < BANDS - 1, rows_ref[jnp.minimum(s + 1, BANDS - 1), row - ROWS + 2], 0.0)
    return value


def pack_kernel(rows_ref, left_out, right_out):
    def sources(i, carry):
        for k in range(CHUNK):
            s = i * CHUNK + k
            left, right = pack_strips(lambda row: summed(rows_ref, s, row))
            for half in range(HALVES):
                left_out[s, half] = left[half]
                right_out[s, half] = right[half]
        return carry

    lax.fori_loop(0, BANDS // CHUNK, sources, 0)


def zonal_kernel(rows_ref, cx_ref, out_ref, keep_buf, up_buf, low_buf, first, second):
    tiles = CHUNK * ROWS

    def sources(i, carry):
        for t in range(tiles):
            first[t] = summed(rows_ref, i * CHUNK + t // ROWS, t % ROWS)
            keep_buf[t], up_buf[t], low_buf[t] = stencil_of(cx_ref[i * tiles + t])
        old, new = first, second
        for step in range(XSTEPS):
            for t in range(tiles):
                value = zonal_sweep(old[t], keep_buf[t], up_buf[t], low_buf[t])
                if step == XSTEPS - 1:
                    out_ref[i * tiles + t] = value
                else:
                    new[t] = value
            old, new = new, old
        return carry

    lax.fori_loop(0, BANDS // CHUNK, sources, 0)


def merge_kernel(inner_ref, left_ref, right_ref, west_ref, east_ref, coef_ref, out_ref, sides, left_buf, right_buf):
    count = BANDS * HALVES
    for n in range(count):
        s, half = n // HALVES, n % HALVES
        left_buf[n], right_buf[n] = fill_halo(
            left_ref[s, half], right_ref[s, half], west_ref[s, half], east_ref[s, half]
        )
    for _ in range(XSTEPS):
        for n in range(count):
            s, half = n // HALVES, n % HALVES
            for side, buf in enumerate((left_buf, right_buf)):
                buf[n] = zonal_sweep(buf[n], *(coef_ref[s, half, side, k] for k in range(3)))
    spot = lane_iota((SLAB, LON)) % STRIP
    for n in range(count):
        sides[n] = jnp.where(spot < XSTEPS, turned(right_buf[n], -2 * XSTEPS), left_buf[n])
    lane = lane_iota((SLAB, LON))
    outer = (lane < XSTEPS) | (lane >= LON - XSTEPS)

    def sources(i, carry):
        for k in range(HALVES):
            packed = sides[i * HALVES + k]
            for g in range(ROWS // HALVES):
                lat = i * ROWS + k * (ROWS // HALVES) + g
                out_ref[:, pl.ds(lat, 1), :] = jnp.where(
                    outer, turned(packed, -STRIP * g - XSTEPS), inner_ref[lat]
                ).reshape(SLAB, 1, LON)
        return carry

    lax.fori_loop(0, BANDS, sources, 0)


def call(body, outs, args, scratch=(), hbm_in=(), hbm_out=(), vmem=16):
    def place(k, far):
        return pl.BlockSpec(memory_space=pltpu.HBM if k in far else pltpu.VMEM)

    args = [pltpu.with_memory_space_constraint(x, pltpu.HBM) if k in hbm_in else x for k, x in enumerate(args)]
    return pl.pallas_call(
        body,
        out_shape=[
            (pltpu.HBM if k in hbm_out else jax.ShapeDtypeStruct)(shape, kind) for k, (shape, kind) in enumerate(outs)
        ],
        in_specs=[place(k, hbm_in) for k in range(len(args))],
        out_specs=[place(k, hbm_out) for k in range(len(outs))],
        scratch_shapes=list(scratch),
        compiler_params=pltpu.CompilerParams(vmem_limit_bytes=vmem << 20),
    )(*args)


def ring_pair(up_value, down_value, axis, wrap):
    n = lax.axis_size(axis)
    up = [(i, (i + 1) % n) for i in range(n if wrap else n - 1)]
    from_prev = lax.ppermute(up_value, axis, up)
    from_next = lax.ppermute(down_value, axis, [(b, a) for a, b in up])
    return from_prev, from_next


def swap_bands(blocks):
    return lax.all_to_all(blocks, "band", split_axis=0, concat_axis=0, tiled=True)


def step_adjoint(
    adjoint_in, courant_y, courant_x, diffusion_inverse, conv_weight, cloud_base, cloud_top,
    sound_count, xco2_adjoint, kernel, sound_cols,
):
    slots = kernel.shape[2]
    dma = pltpu.SemaphoreType.DMA
    (kern,) = call(
        scale_kernel,
        [(kernel.shape[1:], f32)],
        (sound_count, xco2_adjoint, kernel),
        (
            pltpu.VMEM(sound_count.shape, jnp.int32),
            pltpu.VMEM(xco2_adjoint.shape, f32),
            pltpu.VMEM(kernel.shape[1:], f32),
            dma((2,)),
            dma((BANDS // GROUP,)),
            dma((BANDS // GROUP,)),
        ),
        hbm_in=(0, 1, 2),
        hbm_out=(0,),
    )
    kern = swap_bands(kern)

    grid = (ROWS, LEV, LON)
    field, cy, diff = call(
        prepare_kernel,
        [(grid, f32), (grid, f32), ((ROWS, 2, LEV, LEV), bf16)],
        (adjoint_in, courant_y, diffusion_inverse),
        (
            pltpu.VMEM(adjoint_in.shape, f32),
            pltpu.VMEM(courant_y.shape, f32),
            pltpu.VMEM(diffusion_inverse.shape, f32),
            pltpu.VMEM((ROWS, 2, LEV, LEV), bf16),
            dma((3,)),
            dma,
        ),
        hbm_in=(0, 1, 2),
        hbm_out=(2,),
    )
    cy_before, cy_after = ring_pair(cy[ROWS - 2 :], cy[:1], "band", False)

    (rows,) = call(
        mix_kernel,
        [((BANDS, WIDE, SLAB, LON), f32)],
        (
            kern.reshape(BANDS * slots, LEV),
            sound_cols.reshape(1, BANDS * slots),
            field,
            cy,
            cy_before,
            cy_after,
            diff,
            conv_weight,
            cloud_base,
            cloud_top,
        ),
        (
            pltpu.VMEM((BANDS * slots, 2 * LEV), bf16),
            pltpu.VMEM((GROUP * LON, BANDS * slots), bf16),
            pltpu.VMEM(grid, f32),
            pltpu.VMEM((ROWS + 2, LEV, LON), f32),
            pltpu.VMEM((ROWS, 2, LEV, LEV), bf16),
            pltpu.VMEM((ROWS, LON), f32),
            pltpu.VMEM((ROWS, LON), jnp.int32),
            pltpu.VMEM((ROWS, LON), jnp.int32),
            dma((ROWS // GROUP,)),
            dma((3,)),
        ),
        hbm_in=(6, 7, 8, 9),
    )
    rows = swap_bands(rows)

    strips = (BANDS, HALVES, SLAB, LON)
    tiles = (BANDS * ROWS, SLAB, LON)
    cx, cx_left, cx_right = call(faces_kernel, [(tiles, f32), (strips, f32), (strips, f32)], (courant_x,))
    cx_west, cx_east = ring_pair(cx_right, cx_left, "region", True)
    (coef,) = call(
        sides_kernel,
        [((BANDS, HALVES, 2, 3, SLAB, LON), f32)],
        (cx_left, cx_right, cx_west, cx_east),
    )
    left, right = call(pack_kernel, [(strips, f32), (strips, f32)], (rows,))
    west, east = ring_pair(right, left, "region", True)
    chunk = pltpu.VMEM((CHUNK * ROWS, SLAB, LON), f32)
    (inner,) = call(zonal_kernel, [(tiles, f32)], (rows, cx), (chunk,) * 5)
    flat = pltpu.VMEM((BANDS * HALVES, SLAB, LON), f32)
    return call(
        merge_kernel,
        [((SLAB, BANDS * ROWS, LON), f32)],
        (inner, left, right, west, east, coef),
        (flat,) * 3,
    )[0]


def solution(mesh):
    in_specs = (
        P(None, "band", "region"),
        P(None, "band", "region"),
        P("band", None, "region"),
        P("band", None, None),
        P("band", "region"),
        P("band", "region"),
        P("band", "region"),
        P("region", "band"),
        P("region", "band", None),
        P("region", "band", None, None),
        P("region", "band", None),
    )
    out_specs = P("band", None, "region")
    return jax.shard_map(step_adjoint, mesh=mesh, in_specs=in_specs, out_specs=out_specs, check_vma=False)
```

time: 110 us -> 89.6 us (0.81)
  other arithmetic: 26.8 us -> 0 us
  Pallas kernels: 0 us -> 24.2 us
  local copies, waits for them, and re-layouts: 16.1 us -> 0.1 us
  matrix products: 4.56 us -> 0 us
  starting transfers between devices: 26.7 us -> 29.8 us
    pallas_call x0 -> x8, Pallas kernels: none -> 24.2 us  [call(): pl.pallas_call(body, out_shape=[(pltpu.HBM if k in hbm_out else jax.Shape...]
    sub x6 -> x0, other arithmetic: 9.23 us -> none  [shrink_sweep(): (1.0 - up + low) * cut(tracer, 1, n - 1) + up * cut(tracer, 2, n)]
    scatter-add x1 -> x0, other arithmetic: 6.82 us -> none  [per_device(): forced = column.at[:, flat_cols].add(update).reshape(adjoint_in.shape)]
    unnamed x24 -> x4, local copies, waits for them, and re-layouts: 5.76 us -> 0.01 us
    concatenate x2 -> x0, other arithmetic: 5.46 us -> none  [the longest x1 2.73 us: per_device(): cx = jnp.concatenate([cx_prev, courant_x, cx_next], axis=2)]
    ppermute x4 -> x0, local copies, waits for them, and re-layouts: 5.41 us -> none  [the longest x2 2.72 us: neighbours(): lax.ppermute(tail, axis, [(i, (i + 1) % count) for i in range(count)])]
    dot_general x1 -> x0, matrix products: 4.56 us -> none  [vertical_mix(): jnp.einsum('jlk,lji->kji', diffusion_inverse, convected, precision=lax.Pr...]
    slice x6 -> x2, local copies, waits for them, and re-layouts: 3.35 us -> 0.02 us  [step_adjoint(): cy_before, cy_after = ring_pair(cy[ROWS - 2:], cy[:1], 'band', False)]
  transfers between devices with their start and end apart: 10 -> 8, of which waited for: 5 -> 3; matrix products, arithmetic and copies ran while one was open for 26% -> 0% of each run, Pallas kernels for 0% -> 13%
where the time goes in v2:
time: 89.6 us; the launch traced here: 89.2 us
  waiting for transfers between devices  35 us (39%)
  starting transfers between devices  29.8 us (33%)
  Pallas kernels  24.2 us (27%)
    all_to_all x2, waiting for transfers between devices, swap_bands(): lax.all_to_all(blocks, 'band', split_axis=0, concat_axis=0, tiled=True)  28.5 us
    pallas_call x8, Pallas kernels, call(): pl.pallas_call(body, out_shape=[(pltpu.HBM if k in hbm_out else jax.Shape...  24.2 us
    all_to_all x2, starting transfers between devices, swap_bands(): lax.all_to_all(blocks, 'band', split_axis=0, concat_axis=0, tiled=True)  14.3 us
    ppermute x3, starting transfers between devices, ring_pair(): from_next = lax.ppermute(down_value, axis, [(b, a) for a, b in up])  9.45 us
    ppermute x3, waiting for transfers between devices, ring_pair(): from_next = lax.ppermute(down_value, axis, [(b, a) for a, b in up])  6.47 us
    ppermute x3, starting transfers between devices, ring_pair(): from_prev = lax.ppermute(up_value, axis, up)  6.04 us
  transfers between devices with their start and end apart: 8, of which 3 were waited for; matrix products, arithmetic and copies ran while one was open for 0% of the time, Pallas kernels for 13%

profile of v2, /device:TPU:1, one launch (start us, length us, event | category | flops | bytes accessed | tf_op | source)
XLA Modules:
  0.0 89.2 jit_solution(16918126983845322371)
XLA Ops:
  0.0 2.1 %shard_map.109 = f32[16,64,128]{2,1,0:T(8,128)} custom-call(s32[1,16]{1,0:T(1,128)} %count_hbm.1, f32[1,16,64]{2,1,0:T(8,128)} %value_hbm.1, f32[1,16,64,128]{3,2,1,0:T(8,128)} %kern_hbm.1), custom_call_target="tpu_custom_call" | custom-call | tf_op jit(solution)/shard_map/pallas_call | solution.py:309
  2.1 10.0 %all-to-all-start = ((f32[16,64,128]{2,1,0:T(8,128)}), f32[16,64,128]{2,1,0:T(8,128)S(1)}, u32[]{:S(2)}, u32[]{:S(2)}) async-start(f32[16,64,128]{2,1,0:T(8,128)} %shard_map.109), calls=%async_computation | async-start | bytes 1048576 | tf_op jit(solution)/shard_map/all_to_all | solution.py:330
  12.1 0.0 copy-start.1
  12.1 2.7 %shard_map.110 = (f32[16,128,128]{2,1,0:T(8,128)S(1)}, f32[16,128,128]{2,1,0:T(8,128)S(1)}, bf16[16,2,128,128]{3,2,1,0:T(8,128)(2,1)}) custom-call(f32[128,16,128]{2,1,0:T(8,128)} %field_hbm.1, f32[128,16,128]{2,1,0:T(8,128)} %cy_hbm.1, f32[16,128,128]{2,1,0:T(8,128)} %diff_hbm.1), custom_call_target="tpu_custom_call" | custom-call | tf_op jit(solution)/shard_map/pallas_call | solution.py:309
  14.9 3.5 %collective-permute-start = (f32[2,128,128]{2,1,0:T(8,128)S(1)}, f32[2,128,128]{2,1,0:T(8,128)S(1)}, u32[]{:S(2)}, u32[]{:S(2)}) collective-permute-start(f32[2,128,128]{2,1,0:T(8,128)S(1)} %slice.6), channel_id=1, source_target_pairs={{0,1},{1,2},{2,3},{3,4},{4,5},{5,6},{6,7},{7,8},{8,9},{9,10},{10,1... | collective-permute-start | bytes 393224 | tf_op jit(solution)/shard_map/ppermute | solution.py:324
  18.4 1.9 %collective-permute-start.1 = (f32[1,128,128]{2,1,0:T(8,128)S(1)}, f32[1,128,128]{2,1,0:T(8,128)S(1)}, u32[]{:S(2)}, u32[]{:S(2)}) collective-permute-start(f32[1,128,128]{2,1,0:T(8,128)S(1)} %slice.7), channel_id=1, source_target_pairs={{1,0},{2,1},{3,2},{4,3},{5,4},{6,5},{7,6},{8,7},{9,8},{10,9},{11,1... | collective-permute-start | bytes 196616 | tf_op jit(solution)/shard_map/ppermute | solution.py:325
  20.4 0.0 copy-done.1
  20.4 0.1 reshape.7.cols_ref
  20.4 6.5 %collective-permute-done.1.after_ref = f32[1,128,128]{2,1,0:T(8,128)S(1)} collective-permute-done((f32[1,128,128]{2,1,0:T(8,128)S(1)}, f32[1,128,128]{2,1,0:T(8,128)S(1)}, u32[]{:S(2)}, u32[]{:S(2)}) %collective-permute-start.1) | collective-permute-done | bytes 65568 | tf_op jit(solution)/shard_map/ppermute | solution.py:325
  26.9 0.0 collective-permute-done.before_ref
  26.9 2.6 %all-to-all-done = f32[16,64,128]{2,1,0:T(8,128)S(1)} async-done(((f32[16,64,128]{2,1,0:T(8,128)}), f32[16,64,128]{2,1,0:T(8,128)S(1)}, u32[]{:S(2)}, u32[]{:S(2)}) %all-to-all-start) | async-done | bytes 524320 | tf_op jit(solution)/shard_map/all_to_all | solution.py:330
  29.5 6.8 %shard_map.111 = f32[16,20,8,128]{3,2,1,0:T(8,128)} custom-call(f32[1024,128]{1,0:T(8,128)S(1)} %bitcast.1, s32[1,1024]{1,0:T(1,128)S(1)} %reshape.7.cols_ref, f32[16,128,128]{2,1,0:T(8,128)S(1)} %get-tuple-element.13.field_ref, f32[16,128,128]{2,1,0:T(8,128)S(1)} %get-tuple-element.14.cy_ref, f32[2,128,128]{2,1,0:T(8,128)S(1)} %collective-permute-done.before_ref, ...), custom_call_target="tpu_custom_call" | custom-call | tf_op jit(solution)/shard_map/pallas_call | solution.py:309
  36.3 0.0 copy-start
  36.3 4.4 %all-to-all-start.1 = ((f32[16,20,8,128]{3,2,1,0:T(8,128)}), f32[16,20,8,128]{3,2,1,0:T(8,128)S(1)}, u32[]{:S(2)}, u32[]{:S(2)}) async-start(f32[16,20,8,128]{3,2,1,0:T(8,128)} %shard_map.111), calls=%async_computation.1 | async-start | bytes 2621440 | tf_op jit(solution)/shard_map/all_to_all | solution.py:330
  40.7 0.0 copy-done
  40.7 2.4 %shard_map.112 = (f32[256,8,128]{2,1,0:T(8,128)S(1)}, f32[16,2,8,128]{3,2,1,0:T(8,128)S(1)}, f32[16,2,8,128]{3,2,1,0:T(8,128)}) custom-call(f32[8,256,128]{2,1,0:T(8,128)S(1)} %copy-done), custom_call_target="tpu_custom_call" | custom-call | tf_op jit(solution)/shard_map/pallas_call | solution.py:309
  43.1 1.2 %collective-permute-start.4 = (f32[16,2,8,128]{3,2,1,0:T(8,128)}, f32[16,2,8,128]{3,2,1,0:T(8,128)S(1)}, u32[]{:S(2)}, u32[]{:S(2)}) collective-permute-start(f32[16,2,8,128]{3,2,1,0:T(8,128)} %get-tuple-element.20.right_ref), channel_id=1, source_target_pairs={{0,16},{16,32},{32,48},{48,64},{64,80},{80,96},{96,112},{112,128},... | collective-permute-start | bytes 393224 | tf_op jit(solution)/shard_map/ppermute | solution.py:324
  44.3 3.7 %collective-permute-start.5 = (f32[16,2,8,128]{3,2,1,0:T(8,128)S(1)}, f32[16,2,8,128]{3,2,1,0:T(8,128)S(1)}, u32[]{:S(2)}, u32[]{:S(2)}) collective-permute-start(f32[16,2,8,128]{3,2,1,0:T(8,128)S(1)} %get-tuple-element.19.left_ref), channel_id=1, source_target_pairs={{16,0},{32,16},{48,32},{64,48},{80,64},{96,80},{112,96},{128,112},... | collective-permute-start | bytes 393224 | tf_op jit(solution)/shard_map/ppermute | solution.py:325
  48.0 25.9 %all-to-all-done.1.rows_ref = f32[16,20,8,128]{3,2,1,0:T(8,128)S(1)} async-done(((f32[16,20,8,128]{3,2,1,0:T(8,128)}), f32[16,20,8,128]{3,2,1,0:T(8,128)S(1)}, u32[]{:S(2)}, u32[]{:S(2)}) %all-to-all-start.1) | async-done | bytes 1310752 | tf_op jit(solution)/shard_map/all_to_all | solution.py:330
  73.9 0.8 shard_map.114
  74.7 1.3 %collective-permute-start.2 = (f32[16,2,8,128]{3,2,1,0:T(8,128)S(1)}, f32[16,2,8,128]{3,2,1,0:T(8,128)S(1)}, u32[]{:S(2)}, u32[]{:S(2)}) collective-permute-start(f32[16,2,8,128]{3,2,1,0:T(8,128)S(1)} %get-tuple-element.18.right_ref), channel_id=1, source_target_pairs={{0,16},{16,32},{32,48},{48,64},{64,80},{80,96},{96,112},{112,128},... | collective-permute-start | bytes 393224 | tf_op jit(solution)/shard_map/ppermute | solution.py:324
  76.0 3.8 %collective-permute-start.3 = (f32[16,2,8,128]{3,2,1,0:T(8,128)S(1)}, f32[16,2,8,128]{3,2,1,0:T(8,128)S(1)}, u32[]{:S(2)}, u32[]{:S(2)}) collective-permute-start(f32[16,2,8,128]{3,2,1,0:T(8,128)S(1)} %get-tuple-element.17.left_ref), channel_id=1, source_target_pairs={{16,0},{32,16},{48,32},{64,48},{80,64},{96,80},{112,96},{128,112},... | collective-permute-start | bytes 393224 | tf_op jit(solution)/shard_map/ppermute | solution.py:325
  79.8 0.0 collective-permute-done.4.west_ref
  79.8 0.0 collective-permute-done.5.east_ref
  79.8 3.2 %shard_map.115.coef_ref = f32[16,2,2,3,8,128]{5,4,3,2,1,0:T(8,128)S(1)} custom-call(f32[16,2,8,128]{3,2,1,0:T(8,128)S(1)} %get-tuple-element.19.left_ref, f32[16,2,8,128]{3,2,1,0:T(8,128)} %get-tuple-element.20.right_ref, f32[16,2,8,128]{3,2,1,0:T(8,128)S(1)} %collective-permute-done.4.west_ref, f32[16,2,8,128]{3,2,1,0:T(8,128)S(1)} %collective-permute-done.5.east_ref), custom_call_target="tpu_custom_call" | custom-call | tf_op jit(solution)/shard_map/pallas_call | solution.py:309
  83.0 2.7 %shard_map.113.inner_ref = f32[256,8,128]{2,1,0:T(8,128)S(1)} custom-call(f32[16,20,8,128]{3,2,1,0:T(8,128)S(1)} %all-to-all-done.1.rows_ref, f32[256,8,128]{2,1,0:T(8,128)S(1)} %get-tuple-element.16.cx_ref), custom_call_target="tpu_custom_call" | custom-call | tf_op jit(solution)/shard_map/pallas_call | solution.py:309
  85.8 0.0 collective-permute-done.2.west_ref
  85.8 0.0 collective-permute-done.3.east_ref
  85.8 3.5 %shard_map.116 = f32[8,256,128]{2,1,0:T(8,128)} custom-call(f32[256,8,128]{2,1,0:T(8,128)S(1)} %shard_map.113.inner_ref, f32[16,2,8,128]{3,2,1,0:T(8,128)S(1)} %get-tuple-element.17.left_ref, f32[16,2,8,128]{3,2,1,0:T(8,128)S(1)} %get-tuple-element.18.right_ref, f32[16,2,8,128]{3,2,1,0:T(8,128)S(1)} %collective-permute-done.2.west_ref, ...), custom_call_target="tpu_custom_call" | custom-call | tf_op jit(solution)/shard_map/pallas_call | solution.py:309
  (2 shorter events, 0.0 us)
Async XLA Ops:
  2.1 27.4 %all-to-all-start = ((f32[16,64,128]{2,1,0:T(8,128)}), f32[16,64,128]{2,1,0:T(8,128)S(1)}, u32[]{:S(2)}, u32[]{:S(2)}) async-start(f32[16,64,128]{2,1,0:T(8,128)} %shard_map.109), calls=%async_computation | async-start | bytes 1048576 | tf_op jit(solution)/shard_map/all_to_all | solution.py:330
  12.1 8.2 %copy-start.1 = (s32[1,16,64]{2,1,0:T(8,128)S(1)}, s32[1,16,64]{2,1,0:T(8,128)}, u32[]{:S(2)}) copy-start(s32[1,16,64]{2,1,0:T(8,128)} %param.21) | copy-start | bytes 12292
  14.9 12.1 %collective-permute-start = (f32[2,128,128]{2,1,0:T(8,128)S(1)}, f32[2,128,128]{2,1,0:T(8,128)S(1)}, u32[]{:S(2)}, u32[]{:S(2)}) collective-permute-start(f32[2,128,128]{2,1,0:T(8,128)S(1)} %slice.6), channel_id=1, source_target_pairs={{0,1},{1,2},{2,3},{3,4},{4,5},{5,6},{6,7},{7,8},{8,9},{9,10},{10,1... | collective-permute-start | bytes 393224 | tf_op jit(solution)/shard_map/ppermute | solution.py:324
  18.4 8.5 %collective-permute-start.1 = (f32[1,128,128]{2,1,0:T(8,128)S(1)}, f32[1,128,128]{2,1,0:T(8,128)S(1)}, u32[]{:S(2)}, u32[]{:S(2)}) collective-permute-start(f32[1,128,128]{2,1,0:T(8,128)S(1)} %slice.7), channel_id=1, source_target_pairs={{1,0},{2,1},{3,2},{4,3},{5,4},{6,5},{7,6},{8,7},{9,8},{10,9},{11,1... | collective-permute-start | bytes 196616 | tf_op jit(solution)/shard_map/ppermute | solution.py:325
  36.3 4.4 %copy-start = (f32[8,256,128]{2,1,0:T(8,128)S(1)}, f32[8,256,128]{2,1,0:T(8,128)}, u32[]{:S(2)}) copy-start(f32[8,256,128]{2,1,0:T(8,128)} %cx_ref.1) | copy-start | bytes 3145732
  36.3 37.6 %all-to-all-start.1 = ((f32[16,20,8,128]{3,2,1,0:T(8,128)}), f32[16,20,8,128]{3,2,1,0:T(8,128)S(1)}, u32[]{:S(2)}, u32[]{:S(2)}) async-start(f32[16,20,8,128]{3,2,1,0:T(8,128)} %shard_map.111), calls=%async_computation.1 | async-start | bytes 2621440 | tf_op jit(solution)/shard_map/all_to_all | solution.py:330
  43.1 36.8 %collective-permute-start.4 = (f32[16,2,8,128]{3,2,1,0:T(8,128)}, f32[16,2,8,128]{3,2,1,0:T(8,128)S(1)}, u32[]{:S(2)}, u32[]{:S(2)}) collective-permute-start(f32[16,2,8,128]{3,2,1,0:T(8,128)} %get-tuple-element.20.right_ref), channel_id=1, source_target_pairs={{0,16},{16,32},{32,48},{48,64},{64,80},{80,96},{96,112},{112,128},... | collective-permute-start | bytes 393224 | tf_op jit(solution)/shard_map/ppermute | solution.py:324
  44.3 35.6 %collective-permute-start.5 = (f32[16,2,8,128]{3,2,1,0:T(8,128)S(1)}, f32[16,2,8,128]{3,2,1,0:T(8,128)S(1)}, u32[]{:S(2)}, u32[]{:S(2)}) collective-permute-start(f32[16,2,8,128]{3,2,1,0:T(8,128)S(1)} %get-tuple-element.19.left_ref), channel_id=1, source_target_pairs={{16,0},{32,16},{48,32},{64,48},{80,64},{96,80},{112,96},{128,112},... | collective-permute-start | bytes 393224 | tf_op jit(solution)/shard_map/ppermute | solution.py:325
  74.7 11.0 %collective-permute-start.2 = (f32[16,2,8,128]{3,2,1,0:T(8,128)S(1)}, f32[16,2,8,128]{3,2,1,0:T(8,128)S(1)}, u32[]{:S(2)}, u32[]{:S(2)}) collective-permute-start(f32[16,2,8,128]{3,2,1,0:T(8,128)S(1)} %get-tuple-element.18.right_ref), channel_id=1, source_target_pairs={{0,16},{16,32},{32,48},{48,64},{64,80},{80,96},{96,112},{112,128},... | collective-permute-start | bytes 393224 | tf_op jit(solution)/shard_map/ppermute | solution.py:324
  76.0 9.7 %collective-permute-start.3 = (f32[16,2,8,128]{3,2,1,0:T(8,128)S(1)}, f32[16,2,8,128]{3,2,1,0:T(8,128)S(1)}, u32[]{:S(2)}, u32[]{:S(2)}) collective-permute-start(f32[16,2,8,128]{3,2,1,0:T(8,128)S(1)} %get-tuple-element.17.left_ref), channel_id=1, source_target_pairs={{16,0},{32,16},{48,32},{64,48},{80,64},{96,80},{112,96},{128,112},... | collective-permute-start | bytes 393224 | tf_op jit(solution)/shard_map/ppermute | solution.py:325

commit v3 on v2

--- a/solution.py
+++ b/solution.py
@@ -16,6 +16,9 @@
 HALVES = 2
 GROUP = 4
 CHUNK = 4
+CORES = 2
+CHIPS = BANDS // CORES
+ORDER = (4, 3, 5, 2, 6, 1, 7)
 WIDE = ROWS + 4
 
 f32 = jnp.float32
@@ -147,8 +150,8 @@
 
 def mix_kernel(
     kern_ref, cols_ref, field_ref, cy_ref, before_ref, after_ref, diff_hbm, conv_hbm, base_hbm, top_hbm,
-    block_out,
-    parts, onehot, mixed, once, diff_buf, conv_ref, base_ref, top_ref, diff_sem, sem,
+    keep_out, give_out,
+    parts, onehot, mixed, once, twice, diff_buf, conv_ref, base_ref, top_ref, diff_sem, sem,
 ):
     def diff_copy(g):
         span = pl.ds(g * GROUP, GROUP)
@@ -224,42 +227,59 @@
         once[row + 1] = partial_sweep(lambda r: mixed[r], 0, ROWS - 1, row)
     for row in range(-2, ROWS + 2):
         value = partial_sweep(lambda r: once[r + 1], -1, ROWS, row)
-        block_out[:, row + 2] = value.reshape(BANDS, SLAB, LON)
-
-
-def summed(rows_ref, s, row):
-    value = rows_ref[s, row + 2]
-    if row < 2:
-        value += jnp.where(s > 0, rows_ref[jnp.maximum(s - 1, 0), row + ROWS + 2], 0.0)
-    if row >= ROWS - 2:
-        value += jnp.where(s < BANDS - 1, rows_ref[jnp.minimum(s + 1, BANDS - 1), row - ROWS + 2], 0.0)
-    return value
-
-
-def pack_kernel(rows_ref, left_out, right_out):
-    def sources(i, carry):
+        twice[row + 2] = value
+    z, core = lax.axis_index("band") // CORES, lax.axis_index("band") % CORES
+    for t in range(CHIPS):
+        pair = CORES * ((z + t) % CHIPS)
+        for row in range(WIDE):
+            keep_out[t, row] = twice[row, pl.ds(pl.multiple_of((pair + core) * SLAB, SLAB), SLAB)]
+            give_out[t, row] = twice[row, pl.ds(pl.multiple_of((pair + 1 - core) * SLAB, SLAB), SLAB)]
+
+
+def join_kernel(keep_ref, got_ref, *outs):
+    core = lax.axis_index("band") % CORES
+    for t in range(CHIPS):
+        outs[t][core] = keep_ref[t]
+        outs[t][1 - core] = got_ref[t]
+
+
+def pack_kernel(*refs):
+    moved, (own_out, left_out, right_out) = refs[:CHIPS], refs[CHIPS:]
+    z = lax.axis_index("band") // CORES
+    sources = [
+        (moved[t], core, CORES * ((z - t) % CHIPS) + core) for t in range(CHIPS) for core in range(CORES)
+    ]
+    for ref, core, s in sources:
+        own_out[pl.ds(s * ROWS, ROWS)] = ref[core, 2 : ROWS + 2]
+    for ref, core, s in sources:
+        south = pl.ds(jnp.maximum(s - 1, 0) * ROWS + ROWS - 2, 2)
+        own_out[south] += jnp.where(s > 0, ref[core, 0:2], 0.0)
+        north = pl.ds(jnp.minimum(s + 1, BANDS - 1) * ROWS, 2)
+        own_out[north] += jnp.where(s < BANDS - 1, ref[core, ROWS + 2 :], 0.0)
+
+    def pack(i, carry):
         for k in range(CHUNK):
             s = i * CHUNK + k
-            left, right = pack_strips(lambda row: summed(rows_ref, s, row))
+            left, right = pack_strips(lambda row: own_out[s * ROWS + row])
             for half in range(HALVES):
                 left_out[s, half] = left[half]
                 right_out[s, half] = right[half]
         return carry
 
-    lax.fori_loop(0, BANDS // CHUNK, sources, 0)
-
-
-def zonal_kernel(rows_ref, cx_ref, out_ref, keep_buf, up_buf, low_buf, first, second):
+    lax.fori_loop(0, BANDS // CHUNK, pack, 0)
+
+
+def zonal_kernel(own_ref, cx_ref, out_ref, keep_buf, up_buf, low_buf, first, second):
     tiles = CHUNK * ROWS
 
     def sources(i, carry):
         for t in range(tiles):
-            first[t] = summed(rows_ref, i * CHUNK + t // ROWS, t % ROWS)
             keep_buf[t], up_buf[t], low_buf[t] = stencil_of(cx_ref[i * tiles + t])
         old, new = first, second
         for step in range(XSTEPS):
             for t in range(tiles):
-                value = zonal_sweep(old[t], keep_buf[t], up_buf[t], low_buf[t])
+                value = own_ref[i * tiles + t] if step == 0 else old[t]
+                value = zonal_sweep(value, keep_buf[t], up_buf[t], low_buf[t])
                 if step == XSTEPS - 1:
                     out_ref[i * tiles + t] = value
                 else:
@@ -371,9 +391,9 @@
     )
     cy_before, cy_after = ring_pair(cy[ROWS - 2 :], cy[:1], "band", False)
 
-    (rows,) = call(
+    keep, give = call(
         mix_kernel,
-        [((BANDS, WIDE, SLAB, LON), f32)],
+        [((CHIPS, WIDE, SLAB, LON), f32)] * 2,
         (
             kern.reshape(BANDS * slots, LEV),
             sound_cols.reshape(1, BANDS * slots),
@@ -391,6 +411,7 @@
             pltpu.VMEM((GROUP * LON, BANDS * slots), bf16),
             pltpu.VMEM(grid, f32),
             pltpu.VMEM((ROWS + 2, LEV, LON), f32),
+            pltpu.VMEM((WIDE, LEV, LON), f32),
             pltpu.VMEM((ROWS, 2, LEV, LEV), bf16),
             pltpu.VMEM((ROWS, LON), f32),
             pltpu.VMEM((ROWS, LON), jnp.int32),
@@ -400,7 +421,10 @@
         ),
         hbm_in=(6, 7, 8, 9),
     )
-    rows = swap_bands(rows)
+    got = lax.ppermute(give, "band", [(i, i ^ 1) for i in range(BANDS)])
+    moved = list(call(join_kernel, [((CORES, WIDE, SLAB, LON), f32)] * CHIPS, (keep, got)))
+    for t in ORDER:
+        moved[t] = lax.ppermute(moved[t], "band", [(i, (i + CORES * t) % BANDS) for i in range(BANDS)])
 
     strips = (BANDS, HALVES, SLAB, LON)
     tiles = (BANDS * ROWS, SLAB, LON)
@@ -411,10 +435,10 @@
         [((BANDS, HALVES, 2, 3, SLAB, LON), f32)],
         (cx_left, cx_right, cx_west, cx_east),
     )
-    left, right = call(pack_kernel, [(strips, f32), (strips, f32)], (rows,))
+    own, left, right = call(pack_kernel, [(tiles, f32), (strips, f32), (strips, f32)], tuple(moved))
     west, east = ring_pair(right, left, "region", True)
     chunk = pltpu.VMEM((CHUNK * ROWS, SLAB, LON), f32)
-    (inner,) = call(zonal_kernel, [(tiles, f32)], (rows, cx), (chunk,) * 5)
+    (inner,) = call(zonal_kernel, [(tiles, f32)], (own, cx), (chunk,) * 5)
     flat = pltpu.VMEM((BANDS * HALVES, SLAB, LON), f32)
     return call(
         merge_kernel,

time: 89.6 us -> 89.4 us (level)
  starting transfers between devices: 29.8 us -> 41.3 us
  waiting for transfers between devices: 35 us -> 25.1 us
  Pallas kernels: 24.2 us -> 22.3 us
    all_to_all x2 -> x1, waiting for transfers between devices: 28.5 us -> 2.6 us  [swap_bands(): lax.all_to_all(blocks, 'band', split_axis=0, concat_axis=0, tiled=True)]
    ppermute x0 -> x8, waiting for transfers between devices: none -> 16.1 us  [the longest x7 14 us: step_adjoint(): lax.ppermute(moved[t], 'band', [(i, (i + CORES * t) % BANDS) for i in ran...]
    ppermute x0 -> x8, starting transfers between devices: none -> 14.5 us  [the longest x7 14.4 us: step_adjoint(): lax.ppermute(moved[t], 'band', [(i, (i + CORES * t) % BANDS) for i in ran...]
    all_to_all x2 -> x1, starting transfers between devices: 14.3 us -> 9.98 us  [swap_bands(): lax.all_to_all(blocks, 'band', split_axis=0, concat_axis=0, tiled=True)]
    pallas_call x8 -> x9, Pallas kernels: 24.2 us -> 22.3 us  [call(): pl.pallas_call(body, out_shape=[(pltpu.HBM if k in hbm_out else jax.Shape...]
    ppermute x3, starting transfers between devices: 9.45 us -> 10.6 us  [ring_pair(): from_next = lax.ppermute(down_value, axis, [(b, a) for a, b in up])]
  transfers between devices with their start and end apart: 8 -> 15, of which waited for: 3 -> 7; matrix products, arithmetic and copies ran while one was open for 0% -> 0% of each run, Pallas kernels for 13% -> 12%
where the time goes in v3:
time: 89.4 us; the launch traced here: 89 us
  starting transfers between devices  41.3 us (46%)
  waiting for transfers between devices  25.1 us (28%)
  Pallas kernels  22.3 us (25%)
    pallas_call x9, Pallas kernels, call(): pl.pallas_call(body, out_shape=[(pltpu.HBM if k in hbm_out else jax.Shape...  22.3 us
    ppermute x7, starting transfers between devices, step_adjoint(): lax.ppermute(moved[t], 'band', [(i, (i + CORES * t) % BANDS) for i in ran...  14.4 us
    ppermute x7, waiting for transfers between devices, step_adjoint(): lax.ppermute(moved[t], 'band', [(i, (i + CORES * t) % BANDS) for i in ran...  14 us
    ppermute x3, starting transfers between devices, ring_pair(): from_next = lax.ppermute(down_value, axis, [(b, a) for a, b in up])  10.6 us
    all_to_all x1, starting transfers between devices, swap_bands(): lax.all_to_all(blocks, 'band', split_axis=0, concat_axis=0, tiled=True)  9.98 us
    ppermute x3, waiting for transfers between devices, ring_pair(): from_next = lax.ppermute(down_value, axis, [(b, a) for a, b in up])  6.48 us
    ppermute x3, starting transfers between devices, ring_pair(): from_prev = lax.ppermute(up_value, axis, up)  6.11 us
    all_to_all x1, waiting for transfers between devices, swap_bands(): lax.all_to_all(blocks, 'band', split_axis=0, concat_axis=0, tiled=True)  2.6 us
  transfers between devices with their start and end apart: 15, of which 7 were waited for; matrix products, arithmetic and copies ran while one was open for 0% of the time, Pallas kernels for 12%

profile of v3, /device:TPU:1, one launch (start us, length us, event | category | flops | bytes accessed | tf_op | source)
XLA Modules:
  0.0 89.0 jit_solution(7165964119427156350)
XLA Ops:
  0.0 2.1 %shard_map.109 = f32[16,64,128]{2,1,0:T(8,128)} custom-call(s32[1,16]{1,0:T(1,128)} %count_hbm.1, f32[1,16,64]{2,1,0:T(8,128)} %value_hbm.1, f32[1,16,64,128]{3,2,1,0:T(8,128)} %kern_hbm.1), custom_call_target="tpu_custom_call" | custom-call | tf_op jit(solution)/shard_map/pallas_call | solution.py:329
  2.2 10.0 %all-to-all-start = ((f32[16,64,128]{2,1,0:T(8,128)}), f32[16,64,128]{2,1,0:T(8,128)S(1)}, u32[]{:S(2)}, u32[]{:S(2)}) async-start(f32[16,64,128]{2,1,0:T(8,128)} %shard_map.109), calls=%async_computation | async-start | bytes 1048576 | tf_op jit(solution)/shard_map/all_to_all | solution.py:350
  12.1 2.7 %shard_map.110 = (f32[16,128,128]{2,1,0:T(8,128)S(1)}, f32[16,128,128]{2,1,0:T(8,128)S(1)}, bf16[16,2,128,128]{3,2,1,0:T(8,128)(2,1)}) custom-call(f32[128,16,128]{2,1,0:T(8,128)} %field_hbm.1, f32[128,16,128]{2,1,0:T(8,128)} %cy_hbm.1, f32[16,128,128]{2,1,0:T(8,128)} %diff_hbm.1), custom_call_target="tpu_custom_call" | custom-call | tf_op jit(solution)/shard_map/pallas_call | solution.py:329
  14.9 0.0 copy-start.1
  14.9 3.5 %collective-permute-start = (f32[2,128,128]{2,1,0:T(8,128)S(1)}, f32[2,128,128]{2,1,0:T(8,128)S(1)}, u32[]{:S(2)}, u32[]{:S(2)}) collective-permute-start(f32[2,128,128]{2,1,0:T(8,128)S(1)} %slice.6), channel_id=1, source_target_pairs={{0,1},{1,2},{2,3},{3,4},{4,5},{5,6},{6,7},{7,8},{8,9},{9,10},{10,1... | collective-permute-start | bytes 393224 | tf_op jit(solution)/shard_map/ppermute | solution.py:344
  18.4 1.9 %collective-permute-start.1 = (f32[1,128,128]{2,1,0:T(8,128)S(1)}, f32[1,128,128]{2,1,0:T(8,128)S(1)}, u32[]{:S(2)}, u32[]{:S(2)}) collective-permute-start(f32[1,128,128]{2,1,0:T(8,128)S(1)} %slice.7), channel_id=1, source_target_pairs={{1,0},{2,1},{3,2},{4,3},{5,4},{6,5},{7,6},{8,7},{9,8},{10,9},{11,1... | collective-permute-start | bytes 196616 | tf_op jit(solution)/shard_map/ppermute | solution.py:345
  20.4 0.0 copy-done.1
  20.4 0.1 reshape.7.cols_ref
  20.4 6.5 %collective-permute-done.1.after_ref = f32[1,128,128]{2,1,0:T(8,128)S(1)} collective-permute-done((f32[1,128,128]{2,1,0:T(8,128)S(1)}, f32[1,128,128]{2,1,0:T(8,128)S(1)}, u32[]{:S(2)}, u32[]{:S(2)}) %collective-permute-start.1) | collective-permute-done | bytes 65568 | tf_op jit(solution)/shard_map/ppermute | solution.py:345
  26.9 0.0 collective-permute-done.before_ref
  26.9 2.6 %all-to-all-done = f32[16,64,128]{2,1,0:T(8,128)S(1)} async-done(((f32[16,64,128]{2,1,0:T(8,128)}), f32[16,64,128]{2,1,0:T(8,128)S(1)}, u32[]{:S(2)}, u32[]{:S(2)}) %all-to-all-start) | async-done | bytes 524320 | tf_op jit(solution)/shard_map/all_to_all | solution.py:350
  29.5 6.1 %shard_map.111 = (f32[8,20,8,128]{3,2,1,0:T(8,128)S(1)}, f32[8,20,8,128]{3,2,1,0:T(8,128)S(1)}) custom-call(f32[1024,128]{1,0:T(8,128)S(1)} %bitcast.1, s32[1,1024]{1,0:T(1,128)S(1)} %reshape.7.cols_ref, f32[16,128,128]{2,1,0:T(8,128)S(1)} %get-tuple-element.24.field_ref, f32[16,128,128]{2,1,0:T(8,128)S(1)} %get-tuple-element.25.cy_ref, ...), custom_call_target="tpu_custom_call" | custom-call | tf_op jit(solution)/shard_map/pallas_call | solution.py:329
  35.6 0.0 copy-start
  35.6 0.1 collective-permute-start.2
  35.7 2.1 %collective-permute-done.2.got_ref = f32[8,20,8,128]{3,2,1,0:T(8,128)S(1)} collective-permute-done((f32[8,20,8,128]{3,2,1,0:T(8,128)S(1)}, f32[8,20,8,128]{3,2,1,0:T(8,128)S(1)}, u32[]{:S(2)}, u32[]{:S(2)}) %collective-permute-start.2) | collective-permute-done | bytes 655392 | tf_op jit(solution)/shard_map/ppermute | solution.py:424
  37.8 0.1 shard_map.112
  37.9 0.1 collective-permute-start.3
  38.0 1.5 %collective-permute-start.4 = (f32[2,20,8,128]{3,2,1,0:T(8,128)S(1)}, f32[2,20,8,128]{3,2,1,0:T(8,128)S(1)}, u32[]{:S(2)}, u32[]{:S(2)}) collective-permute-start(f32[2,20,8,128]{3,2,1,0:T(8,128)S(1)} %get-tuple-element.31), channel_id=1, source_target_pairs={{0,4},{1,5},{2,6},{3,7},{4,8},{5,9},{6,10},{7,11},{8,12},{9,13},{1... | collective-permute-start | bytes 491528 | tf_op jit(solution)/shard_map/ppermute | solution.py:427
  39.5 2.2 %collective-permute-start.5 = (f32[2,20,8,128]{3,2,1,0:T(8,128)S(1)}, f32[2,20,8,128]{3,2,1,0:T(8,128)S(1)}, u32[]{:S(2)}, u32[]{:S(2)}) collective-permute-start(f32[2,20,8,128]{3,2,1,0:T(8,128)S(1)} %get-tuple-element.32), channel_id=1, source_target_pairs={{0,6},{1,7},{2,8},{3,9},{4,10},{5,11},{6,12},{7,13},{8,14},{9,15},... | collective-permute-start | bytes 491528 | tf_op jit(solution)/shard_map/ppermute | solution.py:427
  41.7 1.9 %collective-permute-start.6 = (f32[2,20,8,128]{3,2,1,0:T(8,128)S(1)}, f32[2,20,8,128]{3,2,1,0:T(8,128)S(1)}, u32[]{:S(2)}, u32[]{:S(2)}) collective-permute-start(f32[2,20,8,128]{3,2,1,0:T(8,128)S(1)} %get-tuple-element.33), channel_id=1, source_target_pairs={{0,8},{1,9},{2,10},{3,11},{4,12},{5,13},{6,14},{7,15},{8,0},{9,1},... | collective-permute-start | bytes 491528 | tf_op jit(solution)/shard_map/ppermute | solution.py:427
  43.6 2.5 %collective-permute-start.7 = (f32[2,20,8,128]{3,2,1,0:T(8,128)S(1)}, f32[2,20,8,128]{3,2,1,0:T(8,128)S(1)}, u32[]{:S(2)}, u32[]{:S(2)}) collective-permute-start(f32[2,20,8,128]{3,2,1,0:T(8,128)S(1)} %get-tuple-element.34), channel_id=1, source_target_pairs={{0,10},{1,11},{2,12},{3,13},{4,14},{5,15},{6,0},{7,1},{8,2},{9,3},... | collective-permute-start | bytes 491528 | tf_op jit(solution)/shard_map/ppermute | solution.py:427
  46.2 0.0 collective-permute-done.3.refs_1_
  46.2 3.3 %collective-permute-start.8 = (f32[2,20,8,128]{3,2,1,0:T(8,128)S(1)}, f32[2,20,8,128]{3,2,1,0:T(8,128)S(1)}, u32[]{:S(2)}, u32[]{:S(2)}) collective-permute-start(f32[2,20,8,128]{3,2,1,0:T(8,128)S(1)} %get-tuple-element.35), channel_id=1, source_target_pairs={{0,12},{1,13},{2,14},{3,15},{4,0},{5,1},{6,2},{7,3},{8,4},{9,5},{1... | collective-permute-start | bytes 491528 | tf_op jit(solution)/shard_map/ppermute | solution.py:427
  49.5 0.0 collective-permute-done.4.refs_2_
  49.5 2.9 %collective-permute-start.9 = (f32[2,20,8,128]{3,2,1,0:T(8,128)S(1)}, f32[2,20,8,128]{3,2,1,0:T(8,128)S(1)}, u32[]{:S(2)}, u32[]{:S(2)}) collective-permute-start(f32[2,20,8,128]{3,2,1,0:T(8,128)S(1)} %get-tuple-element.36), channel_id=1, source_target_pairs={{0,14},{1,15},{2,0},{3,1},{4,2},{5,3},{6,4},{7,5},{8,6},{9,7},{10,... | collective-permute-start | bytes 491528 | tf_op jit(solution)/shard_map/ppermute | solution.py:427
  52.4 0.0 copy-done
  52.4 1.7 %shard_map.114 = (f32[256,8,128]{2,1,0:T(8,128)S(1)}, f32[16,2,8,128]{3,2,1,0:T(8,128)S(1)}, f32[16,2,8,128]{3,2,1,0:T(8,128)S(1)}) custom-call(f32[8,256,128]{2,1,0:T(8,128)S(1)} %copy-done), custom_call_target="tpu_custom_call" | custom-call | tf_op jit(solution)/shard_map/pallas_call | solution.py:329
  54.1 9.0 %collective-permute-done.5.refs_3_ = f32[2,20,8,128]{3,2,1,0:T(8,128)S(1)} collective-permute-done((f32[2,20,8,128]{3,2,1,0:T(8,128)S(1)}, f32[2,20,8,128]{3,2,1,0:T(8,128)S(1)}, u32[]{:S(2)}, u32[]{:S(2)}) %collective-permute-start.5) | collective-permute-done | bytes 163872 | tf_op jit(solution)/shard_map/ppermute | solution.py:427
  63.1 1.1 %collective-permute-start.12 = (f32[16,2,8,128]{3,2,1,0:T(8,128)S(1)}, f32[16,2,8,128]{3,2,1,0:T(8,128)S(1)}, u32[]{:S(2)}, u32[]{:S(2)}) collective-permute-start(f32[16,2,8,128]{3,2,1,0:T(8,128)S(1)} %get-tuple-element.42.right_ref), channel_id=1, source_target_pairs={{0,16},{16,32},{32,48},{48,64},{64,80},{80,96},{96,112},{112,128},... | collective-permute-start | bytes 393224 | tf_op jit(solution)/shard_map/ppermute | solution.py:344
  64.2 2.3 %collective-permute-done.6.refs_4_ = f32[2,20,8,128]{3,2,1,0:T(8,128)S(1)} collective-permute-done((f32[2,20,8,128]{3,2,1,0:T(8,128)S(1)}, f32[2,20,8,128]{3,2,1,0:T(8,128)S(1)}, u32[]{:S(2)}, u32[]{:S(2)}) %collective-permute-start.6) | collective-permute-done | bytes 163872 | tf_op jit(solution)/shard_map/ppermute | solution.py:427
  66.6 4.9 %collective-permute-start.13 = (f32[16,2,8,128]{3,2,1,0:T(8,128)S(1)}, f32[16,2,8,128]{3,2,1,0:T(8,128)S(1)}, u32[]{:S(2)}, u32[]{:S(2)}) collective-permute-start(f32[16,2,8,128]{3,2,1,0:T(8,128)S(1)} %get-tuple-element.41.left_ref), channel_id=1, source_target_pairs={{16,0},{32,16},{48,32},{64,48},{80,64},{96,80},{112,96},{128,112},... | collective-permute-start | bytes 393224 | tf_op jit(solution)/shard_map/ppermute | solution.py:345
  71.5 0.0 collective-permute-done.7.refs_5_
  71.5 1.2 %collective-permute-done.8.refs_6_ = f32[2,20,8,128]{3,2,1,0:T(8,128)S(1)} collective-permute-done((f32[2,20,8,128]{3,2,1,0:T(8,128)S(1)}, f32[2,20,8,128]{3,2,1,0:T(8,128)S(1)}, u32[]{:S(2)}, u32[]{:S(2)}) %collective-permute-start.8) | collective-permute-done | bytes 163872 | tf_op jit(solution)/shard_map/ppermute | solution.py:427
  72.7 1.4 %collective-permute-done.9.refs_7_ = f32[2,20,8,128]{3,2,1,0:T(8,128)S(1)} collective-permute-done((f32[2,20,8,128]{3,2,1,0:T(8,128)S(1)}, f32[2,20,8,128]{3,2,1,0:T(8,128)S(1)}, u32[]{:S(2)}, u32[]{:S(2)}) %collective-permute-start.9) | collective-permute-done | bytes 163872 | tf_op jit(solution)/shard_map/ppermute | solution.py:427
  74.1 1.0 %shard_map.113 = (f32[256,8,128]{2,1,0:T(8,128)S(1)}, f32[16,2,8,128]{3,2,1,0:T(8,128)S(1)}, f32[16,2,8,128]{3,2,1,0:T(8,128)S(1)}) custom-call(f32[2,20,8,128]{3,2,1,0:T(8,128)S(1)} %get-tuple-element.29.refs_0_, f32[2,20,8,128]{3,2,1,0:T(8,128)S(1)} %collective-permute-done.3.refs_1_, f32[2,20,8,128]{3,2,1,0:T(8,128)S(1)} %collective-permute-done.4.refs_2_, ...), custom_call_target="tpu_custom_call" | custom-call | tf_op jit(solution)/shard_map/pallas_call | solution.py:329
  75.2 1.5 %collective-permute-start.10 = (f32[16,2,8,128]{3,2,1,0:T(8,128)S(1)}, f32[16,2,8,128]{3,2,1,0:T(8,128)S(1)}, u32[]{:S(2)}, u32[]{:S(2)}) collective-permute-start(f32[16,2,8,128]{3,2,1,0:T(8,128)S(1)} %get-tuple-element.40.right_ref), channel_id=1, source_target_pairs={{0,16},{16,32},{32,48},{48,64},{64,80},{80,96},{96,112},{112,128},... | collective-permute-start | bytes 393224 | tf_op jit(solution)/shard_map/ppermute | solution.py:344
  76.6 3.8 %collective-permute-start.11 = (f32[16,2,8,128]{3,2,1,0:T(8,128)S(1)}, f32[16,2,8,128]{3,2,1,0:T(8,128)S(1)}, u32[]{:S(2)}, u32[]{:S(2)}) collective-permute-start(f32[16,2,8,128]{3,2,1,0:T(8,128)S(1)} %get-tuple-element.39.left_ref), channel_id=1, source_target_pairs={{16,0},{32,16},{48,32},{64,48},{80,64},{96,80},{112,96},{128,112},... | collective-permute-start | bytes 393224 | tf_op jit(solution)/shard_map/ppermute | solution.py:345
  80.4 0.0 collective-permute-done.12.west_ref
  80.4 0.0 collective-permute-done.13.east_ref
  80.4 2.3 %shard_map.116.coef_ref = f32[16,2,2,3,8,128]{5,4,3,2,1,0:T(8,128)S(1)} custom-call(f32[16,2,8,128]{3,2,1,0:T(8,128)S(1)} %get-tuple-element.41.left_ref, f32[16,2,8,128]{3,2,1,0:T(8,128)S(1)} %get-tuple-element.42.right_ref, f32[16,2,8,128]{3,2,1,0:T(8,128)S(1)} %collective-permute-done.12.west_ref, f32[16,2,8,128]{3,2,1,0:T(8,128)S(1)} %collective-permute-done.13.east_ref), custom_call_target="tpu_custom_call" | custom-call | tf_op jit(solution)/shard_map/pallas_call | solution.py:329
  82.7 2.7 %shard_map.115.inner_ref = f32[256,8,128]{2,1,0:T(8,128)S(1)} custom-call(f32[256,8,128]{2,1,0:T(8,128)S(1)} %get-tuple-element.37.own_ref, f32[256,8,128]{2,1,0:T(8,128)S(1)} %get-tuple-element.38.cx_ref), custom_call_target="tpu_custom_call" | custom-call | tf_op jit(solution)/shard_map/pallas_call | solution.py:329
  85.5 0.0 collective-permute-done.10.west_ref
  85.5 0.0 collective-permute-done.11.east_ref
  85.5 3.5 %shard_map.117 = f32[8,256,128]{2,1,0:T(8,128)} custom-call(f32[256,8,128]{2,1,0:T(8,128)S(1)} %shard_map.115.inner_ref, f32[16,2,8,128]{3,2,1,0:T(8,128)S(1)} %get-tuple-element.39.left_ref, f32[16,2,8,128]{3,2,1,0:T(8,128)S(1)} %get-tuple-element.40.right_ref, f32[16,2,8,128]{3,2,1,0:T(8,128)S(1)} %collective-permute-done.10.west_ref, ...), custom_call_target="tpu_custom_call" | custom-call | tf_op jit(solution)/shard_map/pallas_call | solution.py:329
  (2 shorter events, 0.0 us)
Async XLA Ops:
  2.2 27.4 %all-to-all-start = ((f32[16,64,128]{2,1,0:T(8,128)}), f32[16,64,128]{2,1,0:T(8,128)S(1)}, u32[]{:S(2)}, u32[]{:S(2)}) async-start(f32[16,64,128]{2,1,0:T(8,128)} %shard_map.109), calls=%async_computation | async-start | bytes 1048576 | tf_op jit(solution)/shard_map/all_to_all | solution.py:350
  14.9 5.5 %copy-start.1 = (s32[1,16,64]{2,1,0:T(8,128)S(1)}, s32[1,16,64]{2,1,0:T(8,128)}, u32[]{:S(2)}) copy-start(s32[1,16,64]{2,1,0:T(8,128)} %param.21) | copy-start | bytes 12292
  14.9 12.1 %collective-permute-start = (f32[2,128,128]{2,1,0:T(8,128)S(1)}, f32[2,128,128]{2,1,0:T(8,128)S(1)}, u32[]{:S(2)}, u32[]{:S(2)}) collective-permute-start(f32[2,128,128]{2,1,0:T(8,128)S(1)} %slice.6), channel_id=1, source_target_pairs={{0,1},{1,2},{2,3},{3,4},{4,5},{5,6},{6,7},{7,8},{8,9},{9,10},{10,1... | collective-permute-start | bytes 393224 | tf_op jit(solution)/shard_map/ppermute | solution.py:344
  18.4 8.5 %collective-permute-start.1 = (f32[1,128,128]{2,1,0:T(8,128)S(1)}, f32[1,128,128]{2,1,0:T(8,128)S(1)}, u32[]{:S(2)}, u32[]{:S(2)}) collective-permute-start(f32[1,128,128]{2,1,0:T(8,128)S(1)} %slice.7), channel_id=1, source_target_pairs={{1,0},{2,1},{3,2},{4,3},{5,4},{6,5},{7,6},{8,7},{9,8},{10,9},{11,1... | collective-permute-start | bytes 196616 | tf_op jit(solution)/shard_map/ppermute | solution.py:345
  35.6 16.8 %copy-start = (f32[8,256,128]{2,1,0:T(8,128)S(1)}, f32[8,256,128]{2,1,0:T(8,128)}, u32[]{:S(2)}) copy-start(f32[8,256,128]{2,1,0:T(8,128)} %cx_ref.1) | copy-start | bytes 3145732
  35.6 2.2 %collective-permute-start.2 = (f32[8,20,8,128]{3,2,1,0:T(8,128)S(1)}, f32[8,20,8,128]{3,2,1,0:T(8,128)S(1)}, u32[]{:S(2)}, u32[]{:S(2)}) collective-permute-start(f32[8,20,8,128]{3,2,1,0:T(8,128)S(1)} %get-tuple-element.28), channel_id=1, source_target_pairs={{0,1},{1,0},{2,3},{3,2},{4,5},{5,4},{6,7},{7,6},{8,9},{9,8},{10,11... | collective-permute-start | bytes 1966088 | tf_op jit(solution)/shard_map/ppermute | solution.py:424
  37.9 8.3 %collective-permute-start.3 = (f32[2,20,8,128]{3,2,1,0:T(8,128)S(1)}, f32[2,20,8,128]{3,2,1,0:T(8,128)S(1)}, u32[]{:S(2)}, u32[]{:S(2)}) collective-permute-start(f32[2,20,8,128]{3,2,1,0:T(8,128)S(1)} %get-tuple-element.30), channel_id=1, source_target_pairs={{0,2},{1,3},{2,4},{3,5},{4,6},{5,7},{6,8},{7,9},{8,10},{9,11},{10,... | collective-permute-start | bytes 491528 | tf_op jit(solution)/shard_map/ppermute | solution.py:427
  38.0 11.5 %collective-permute-start.4 = (f32[2,20,8,128]{3,2,1,0:T(8,128)S(1)}, f32[2,20,8,128]{3,2,1,0:T(8,128)S(1)}, u32[]{:S(2)}, u32[]{:S(2)}) collective-permute-start(f32[2,20,8,128]{3,2,1,0:T(8,128)S(1)} %get-tuple-element.31), channel_id=1, source_target_pairs={{0,4},{1,5},{2,6},{3,7},{4,8},{5,9},{6,10},{7,11},{8,12},{9,13},{1... | collective-permute-start | bytes 491528 | tf_op jit(solution)/shard_map/ppermute | solution.py:427
  39.5 23.6 %collective-permute-start.5 = (f32[2,20,8,128]{3,2,1,0:T(8,128)S(1)}, f32[2,20,8,128]{3,2,1,0:T(8,128)S(1)}, u32[]{:S(2)}, u32[]{:S(2)}) collective-permute-start(f32[2,20,8,128]{3,2,1,0:T(8,128)S(1)} %get-tuple-element.32), channel_id=1, source_target_pairs={{0,6},{1,7},{2,8},{3,9},{4,10},{5,11},{6,12},{7,13},{8,14},{9,15},... | collective-permute-start | bytes 491528 | tf_op jit(solution)/shard_map/ppermute | solution.py:427
  41.7 24.8 %collective-permute-start.6 = (f32[2,20,8,128]{3,2,1,0:T(8,128)S(1)}, f32[2,20,8,128]{3,2,1,0:T(8,128)S(1)}, u32[]{:S(2)}, u32[]{:S(2)}) collective-permute-start(f32[2,20,8,128]{3,2,1,0:T(8,128)S(1)} %get-tuple-element.33), channel_id=1, source_target_pairs={{0,8},{1,9},{2,10},{3,11},{4,12},{5,13},{6,14},{7,15},{8,0},{9,1},... | collective-permute-start | bytes 491528 | tf_op jit(solution)/shard_map/ppermute | solution.py:427
  43.6 27.8 %collective-permute-start.7 = (f32[2,20,8,128]{3,2,1,0:T(8,128)S(1)}, f32[2,20,8,128]{3,2,1,0:T(8,128)S(1)}, u32[]{:S(2)}, u32[]{:S(2)}) collective-permute-start(f32[2,20,8,128]{3,2,1,0:T(8,128)S(1)} %get-tuple-element.34), channel_id=1, source_target_pairs={{0,10},{1,11},{2,12},{3,13},{4,14},{5,15},{6,0},{7,1},{8,2},{9,3},... | collective-permute-start | bytes 491528 | tf_op jit(solution)/shard_map/ppermute | solution.py:427
  46.2 26.6 %collective-permute-start.8 = (f32[2,20,8,128]{3,2,1,0:T(8,128)S(1)}, f32[2,20,8,128]{3,2,1,0:T(8,128)S(1)}, u32[]{:S(2)}, u32[]{:S(2)}) collective-permute-start(f32[2,20,8,128]{3,2,1,0:T(8,128)S(1)} %get-tuple-element.35), channel_id=1, source_target_pairs={{0,12},{1,13},{2,14},{3,15},{4,0},{5,1},{6,2},{7,3},{8,4},{9,5},{1... | collective-permute-start | bytes 491528 | tf_op jit(solution)/shard_map/ppermute | solution.py:427
  49.5 24.6 %collective-permute-start.9 = (f32[2,20,8,128]{3,2,1,0:T(8,128)S(1)}, f32[2,20,8,128]{3,2,1,0:T(8,128)S(1)}, u32[]{:S(2)}, u32[]{:S(2)}) collective-permute-start(f32[2,20,8,128]{3,2,1,0:T(8,128)S(1)} %get-tuple-element.36), channel_id=1, source_target_pairs={{0,14},{1,15},{2,0},{3,1},{4,2},{5,3},{6,4},{7,5},{8,6},{9,7},{10,... | collective-permute-start | bytes 491528 | tf_op jit(solution)/shard_map/ppermute | solution.py:427
  63.1 17.3 %collective-permute-start.12 = (f32[16,2,8,128]{3,2,1,0:T(8,128)S(1)}, f32[16,2,8,128]{3,2,1,0:T(8,128)S(1)}, u32[]{:S(2)}, u32[]{:S(2)}) collective-permute-start(f32[16,2,8,128]{3,2,1,0:T(8,128)S(1)} %get-tuple-element.42.right_ref), channel_id=1, source_target_pairs={{0,16},{16,32},{32,48},{48,64},{64,80},{80,96},{96,112},{112,128},... | collective-permute-start | bytes 393224 | tf_op jit(solution)/shard_map/ppermute | solution.py:344
  66.6 13.9 %collective-permute-start.13 = (f32[16,2,8,128]{3,2,1,0:T(8,128)S(1)}, f32[16,2,8,128]{3,2,1,0:T(8,128)S(1)}, u32[]{:S(2)}, u32[]{:S(2)}) collective-permute-start(f32[16,2,8,128]{3,2,1,0:T(8,128)S(1)} %get-tuple-element.41.left_ref), channel_id=1, source_target_pairs={{16,0},{32,16},{48,32},{64,48},{80,64},{96,80},{112,96},{128,112},... | collective-permute-start | bytes 393224 | tf_op jit(solution)/shard_map/ppermute | solution.py:345
  75.2 10.3 %collective-permute-start.10 = (f32[16,2,8,128]{3,2,1,0:T(8,128)S(1)}, f32[16,2,8,128]{3,2,1,0:T(8,128)S(1)}, u32[]{:S(2)}, u32[]{:S(2)}) collective-permute-start(f32[16,2,8,128]{3,2,1,0:T(8,128)S(1)} %get-tuple-element.40.right_ref), channel_id=1, source_target_pairs={{0,16},{16,32},{32,48},{48,64},{64,80},{80,96},{96,112},{112,128},... | collective-permute-start | bytes 393224 | tf_op jit(solution)/shard_map/ppermute | solution.py:344
  76.6 8.8 %collective-permute-start.11 = (f32[16,2,8,128]{3,2,1,0:T(8,128)S(1)}, f32[16,2,8,128]{3,2,1,0:T(8,128)S(1)}, u32[]{:S(2)}, u32[]{:S(2)}) collective-permute-start(f32[16,2,8,128]{3,2,1,0:T(8,128)S(1)} %get-tuple-element.39.left_ref), channel_id=1, source_target_pairs={{16,0},{32,16},{48,32},{64,48},{80,64},{96,80},{112,96},{128,112},... | collective-permute-start | bytes 393224 | tf_op jit(solution)/shard_map/ppermute | solution.py:345

commit v4 on v3

--- a/solution.py
+++ b/solution.py
@@ -18,7 +18,8 @@
 CHUNK = 4
 CORES = 2
 CHIPS = BANDS // CORES
-ORDER = (4, 3, 5, 2, 6, 1, 7)
+FAR = CHIPS // 2
+NEAR = (0, 3, 5, 2, 6, 1, 7)
 WIDE = ROWS + 4
 
 f32 = jnp.float32
@@ -55,14 +56,13 @@
     return left, right
 
 
-def scale_kernel(count_hbm, value_hbm, kern_hbm, out_hbm, count, value, kern, sem, kern_sem, out_sem):
+def scale_kernel(count_hbm, value_hbm, kern_hbm, out_ref, count, value, kern, sem, kern_sem):
     small = [
         pltpu.make_async_copy(count_hbm, count, sem.at[0]),
         pltpu.make_async_copy(value_hbm, value, sem.at[1]),
     ]
     spans = [pl.ds(c * GROUP, GROUP) for c in range(BANDS // GROUP)]
     loads = [pltpu.make_async_copy(kern_hbm.at[0, spans[c]], kern.at[spans[c]], kern_sem.at[c]) for c in range(len(spans))]
-    stores = [pltpu.make_async_copy(kern.at[spans[c]], out_hbm.at[spans[c]], out_sem.at[c]) for c in range(len(spans))]
     for copy in small + loads:
         copy.start()
     for copy in small:
@@ -73,10 +73,7 @@
     for c in range(len(spans)):
         loads[c].wait()
         for band in range(c * GROUP, c * GROUP + GROUP):
-            kern[band] = kern[band] * factor[:, band : band + 1]
-        stores[c].start()
-    for copy in stores:
-        copy.wait()
+            out_ref[band] = kern[band] * factor[:, band : band + 1]
 
 
 def prepare_kernel(field_hbm, cy_hbm, diff_hbm, field_out, cy_out, diff_out, field, cy, diff, parts, sem, out_sem):
@@ -90,8 +87,8 @@
     loads[0].wait()
     for row in range(ROWS):
         hi, lo = split(diff[row].T)
-        parts[row, 0] = hi
-        parts[row, 1] = lo
+        parts[row, :, :LEV] = hi
+        parts[row, :, LEV:] = lo
     store = pltpu.make_async_copy(parts, diff_out, out_sem)
     store.start()
     loads[1].wait()
@@ -103,20 +100,24 @@
     store.wait()
 
 
-def faces_kernel(cx_ref, cx_out, left_out, right_out):
-    def source(s, carry):
-        def tile_of(row):
-            tile = cx_ref[:, pl.ds(s * ROWS + row, 1), :].reshape(SLAB, LON)
-            cx_out[s * ROWS + row] = tile
-            return tile
-
-        left, right = pack_strips(tile_of)
-        for half in range(HALVES):
-            left_out[s, half] = left[half]
-            right_out[s, half] = right[half]
+def faces_kernel(cx_ref, cx_out, low_out, left_out, right_out):
+    def sources(i, carry):
+        for k in range(2):
+            s = i * 2 + k
+
+            def tile_of(row):
+                tile = cx_ref[:, pl.ds(s * ROWS + row, 1), :].reshape(SLAB, LON)
+                cx_out[s * ROWS + row] = tile
+                low_out[s * ROWS + row] = turned(jnp.minimum(tile, 0.0), 1)
+                return tile
+
+            left, right = pack_strips(tile_of)
+            for half in range(HALVES):
+                left_out[s, half] = left[half]
+                right_out[s, half] = right[half]
         return carry
 
-    lax.fori_loop(0, BANDS, source, 0)
+    lax.fori_loop(0, BANDS // 2, sources, 0)
 
 
 def fill_halo(left, right, west, east):
@@ -137,20 +138,22 @@
 
 
 def sides_kernel(left_ref, right_ref, west_ref, east_ref, coef_out):
-    def source(s, carry):
-        for half in range(HALVES):
-            strips = fill_halo(left_ref[s, half], right_ref[s, half], west_ref[s, half], east_ref[s, half])
-            for side in range(2):
-                for k, value in enumerate(stencil_of(strips[side])):
-                    coef_out[s, half, side, k] = value
+    def sources(i, carry):
+        for k in range(CHUNK):
+            s = i * CHUNK + k
+            for half in range(HALVES):
+                strips = fill_halo(left_ref[s, half], right_ref[s, half], west_ref[s, half], east_ref[s, half])
+                for side in range(2):
+                    for n, value in enumerate(stencil_of(strips[side])):
+                        coef_out[s, half, side, n] = value
         return carry
 
-    lax.fori_loop(0, BANDS, source, 0)
+    lax.fori_loop(0, BANDS // CHUNK, sources, 0)
 
 
 def mix_kernel(
     kern_ref, cols_ref, field_ref, cy_ref, before_ref, after_ref, diff_hbm, conv_hbm, base_hbm, top_hbm,
-    keep_out, give_out,
+    keep_out, give_out, far_out,
     parts, onehot, mixed, once, twice, diff_buf, conv_ref, base_ref, top_ref, diff_sem, sem,
 ):
     def diff_copy(g):
@@ -174,33 +177,29 @@
         copy.wait()
     level = lax.broadcasted_iota(jnp.int32, (LEV, LON), 0)
 
-    def group(g, carry):
-        cols = cols_ref[...] - g * (GROUP * LON)
-        for r in range(0, GROUP * LON, 32):
-            cell = lax.broadcasted_iota(jnp.int32, (32, cols.shape[1]), 0) + r
-            onehot[pl.ds(r, 32), :] = jnp.where(cell == cols, 1.0, 0.0).astype(bf16)
-        both = jnp.dot(onehot[...], parts[...], preferred_element_type=f32)
+    for g in range(ROWS // GROUP):
+        cols = cols_ref[...]
+        for q in range(GROUP):
+            here = jnp.where(cols // LON == g * GROUP + q, cols % LON, -1).astype(f32).astype(bf16)
+            for r in range(0, LON, 32):
+                cell = lax.broadcasted_iota(jnp.int32, (32, cols.shape[1]), 0) + r
+                match = cell.astype(f32).astype(bf16) == here
+                onehot[g, q * LON + r : q * LON + r + 32, :] = jnp.where(match, jnp.ones((), bf16), jnp.zeros((), bf16))
+        both = jnp.dot(onehot[g], parts[...], preferred_element_type=f32)
         added = both[:, :LEV] + both[:, LEV:]
         diff_copy(g).wait()
         for q in range(GROUP):
             row = g * GROUP + q
             forced = field_ref[row] + added[q * LON : (q + 1) * LON].T
-            base = base_ref[pl.ds(row, 1), :]
-            top = top_ref[pl.ds(row, 1), :]
+            base = base_ref[row : row + 1, :]
+            top = top_ref[row : row + 1, :]
             inside = jnp.where((level >= base) & (level <= top), 1.0, 0.0)
             mean = jnp.sum(inside * forced, axis=0, keepdims=True) / (top - base + 1).astype(f32)
-            convected = forced + conv_ref[pl.ds(row, 1), :] * inside * (mean - forced)
+            convected = forced + conv_ref[row : row + 1, :] * inside * (mean - forced)
             hi, lo = split(convected)
-            d_hi = diff_buf[row, 0]
-            d_lo = diff_buf[row, 1]
-            mixed[row] = (
-                jnp.dot(d_hi, lo, preferred_element_type=f32)
-                + jnp.dot(d_lo, hi, preferred_element_type=f32)
-                + jnp.dot(d_hi, hi, preferred_element_type=f32)
-            )
-        return carry
-
-    lax.fori_loop(0, ROWS // GROUP, group, 0)
+            pair = jnp.concatenate([hi, lo], axis=1)
+            both = jnp.dot(diff_buf[row], jnp.concatenate([pair, pair], axis=0), preferred_element_type=f32)
+            mixed[row] = both[:, :LON] + both[:, LON:]
     open_face = jnp.where(lax.axis_index("band") == BANDS - 1, 0.0, 1.0)
 
     def face(row):
@@ -234,28 +233,37 @@
         for row in range(WIDE):
             keep_out[t, row] = twice[row, pl.ds(pl.multiple_of((pair + core) * SLAB, SLAB), SLAB)]
             give_out[t, row] = twice[row, pl.ds(pl.multiple_of((pair + 1 - core) * SLAB, SLAB), SLAB)]
+    far_out[...] = keep_out[FAR]
 
 
 def join_kernel(keep_ref, got_ref, *outs):
     core = lax.axis_index("band") % CORES
-    for t in range(CHIPS):
-        outs[t][core] = keep_ref[t]
-        outs[t][1 - core] = got_ref[t]
+
+    def join(south, north):
+        for out, t in zip(outs[1:], NEAR):
+            out[0 : ROWS + 2] = south[t, 0 : ROWS + 2]
+            out[ROWS + 2 :] = north[t, 2:]
+            out[ROWS : ROWS + 2] += north[t, 0:2]
+            out[ROWS + 2 : ROWS + 4] += south[t, ROWS + 2 :]
+
+    outs[0][...] = got_ref[FAR]
+    pl.when(core == 0)(lambda: join(keep_ref, got_ref))
+    pl.when(core == 1)(lambda: join(got_ref, keep_ref))
 
 
 def pack_kernel(*refs):
-    moved, (own_out, left_out, right_out) = refs[:CHIPS], refs[CHIPS:]
-    z = lax.axis_index("band") // CORES
-    sources = [
-        (moved[t], core, CORES * ((z - t) % CHIPS) + core) for t in range(CHIPS) for core in range(CORES)
-    ]
-    for ref, core, s in sources:
-        own_out[pl.ds(s * ROWS, ROWS)] = ref[core, 2 : ROWS + 2]
-    for ref, core, s in sources:
+    moved, (own_out, left_out, right_out) = refs[: CHIPS + 1], refs[CHIPS + 1 :]
+    z, core = lax.axis_index("band") // CORES, lax.axis_index("band") % CORES
+    far = (z - FAR) % CHIPS * CORES
+    blocks = [(moved[0], far + core, 1), (moved[1], far + 1 - core, 1)]
+    blocks += [(ref, (z - t) % CHIPS * CORES, CORES) for ref, t in zip(moved[2:], NEAR)]
+    for ref, s, n in blocks:
+        own_out[pl.ds(s * ROWS, n * ROWS)] = ref[2 : n * ROWS + 2]
+    for ref, s, n in blocks:
         south = pl.ds(jnp.maximum(s - 1, 0) * ROWS + ROWS - 2, 2)
-        own_out[south] += jnp.where(s > 0, ref[core, 0:2], 0.0)
-        north = pl.ds(jnp.minimum(s + 1, BANDS - 1) * ROWS, 2)
-        own_out[north] += jnp.where(s < BANDS - 1, ref[core, ROWS + 2 :], 0.0)
+        own_out[south] += jnp.where(s > 0, ref[0:2], 0.0)
+        north = pl.ds(jnp.minimum(s + n, BANDS - 1) * ROWS, 2)
+        own_out[north] += jnp.where(s + n < BANDS, ref[n * ROWS + 2 :], 0.0)
 
     def pack(i, carry):
         for k in range(CHUNK):
@@ -269,17 +277,17 @@
     lax.fori_loop(0, BANDS // CHUNK, pack, 0)
 
 
-def zonal_kernel(own_ref, cx_ref, out_ref, keep_buf, up_buf, low_buf, first, second):
+def zonal_kernel(own_ref, cx_ref, low_ref, out_ref, first, second):
     tiles = CHUNK * ROWS
 
     def sources(i, carry):
-        for t in range(tiles):
-            keep_buf[t], up_buf[t], low_buf[t] = stencil_of(cx_ref[i * tiles + t])
         old, new = first, second
         for step in range(XSTEPS):
             for t in range(tiles):
                 value = own_ref[i * tiles + t] if step == 0 else old[t]
-                value = zonal_sweep(value, keep_buf[t], up_buf[t], low_buf[t])
+                up = jnp.maximum(cx_ref[i * tiles + t], 0.0)
+                low = low_ref[i * tiles + t]
+                value = zonal_sweep(value, 1.0 - up + low, up, low)
                 if step == XSTEPS - 1:
                     out_ref[i * tiles + t] = value
                 else:
@@ -290,7 +298,7 @@
     lax.fori_loop(0, BANDS // CHUNK, sources, 0)
 
 
-def merge_kernel(inner_ref, left_ref, right_ref, west_ref, east_ref, coef_ref, out_ref, sides, left_buf, right_buf):
+def merge_kernel(inner_ref, left_ref, right_ref, west_ref, east_ref, coef_ref, out_hbm, sides, left_buf, right_buf, out_ref, sem):
     count = BANDS * HALVES
     for n in range(count):
         s, half = n // HALVES, n % HALVES
@@ -308,17 +316,20 @@
     lane = lane_iota((SLAB, LON))
     outer = (lane < XSTEPS) | (lane >= LON - XSTEPS)
 
-    def sources(i, carry):
-        for k in range(HALVES):
-            packed = sides[i * HALVES + k]
-            for g in range(ROWS // HALVES):
-                lat = i * ROWS + k * (ROWS // HALVES) + g
-                out_ref[:, pl.ds(lat, 1), :] = jnp.where(
-                    outer, turned(packed, -STRIP * g - XSTEPS), inner_ref[lat]
-                ).reshape(SLAB, 1, LON)
-        return carry
-
-    lax.fori_loop(0, BANDS, sources, 0)
+    def store(c):
+        span = pl.ds(c * CHUNK * ROWS, CHUNK * ROWS)
+        return pltpu.make_async_copy(out_ref.at[:, span], out_hbm.at[:, span], sem.at[c])
+
+    for c in range(BANDS // CHUNK):
+        for i in range(c * CHUNK, c * CHUNK + CHUNK):
+            for k in range(HALVES):
+                packed = sides[i * HALVES + k]
+                for g in range(ROWS // HALVES):
+                    lat = i * ROWS + k * (ROWS // HALVES) + g
+                    out_ref[:, lat, :] = jnp.where(outer, turned(packed, -STRIP * g - XSTEPS), inner_ref[lat])
+        store(c).start()
+    for c in range(BANDS // CHUNK):
+        store(c).wait()
 
 
 def call(body, outs, args, scratch=(), hbm_in=(), hbm_out=(), vmem=16):
@@ -366,23 +377,21 @@
             pltpu.VMEM(kernel.shape[1:], f32),
             dma((2,)),
             dma((BANDS // GROUP,)),
-            dma((BANDS // GROUP,)),
         ),
         hbm_in=(0, 1, 2),
-        hbm_out=(0,),
     )
     kern = swap_bands(kern)
 
     grid = (ROWS, LEV, LON)
     field, cy, diff = call(
         prepare_kernel,
-        [(grid, f32), (grid, f32), ((ROWS, 2, LEV, LEV), bf16)],
+        [(grid, f32), (grid, f32), ((ROWS, LEV, 2 * LEV), bf16)],
         (adjoint_in, courant_y, diffusion_inverse),
         (
             pltpu.VMEM(adjoint_in.shape, f32),
             pltpu.VMEM(courant_y.shape, f32),
             pltpu.VMEM(diffusion_inverse.shape, f32),
-            pltpu.VMEM((ROWS, 2, LEV, LEV), bf16),
+            pltpu.VMEM((ROWS, LEV, 2 * LEV), bf16),
             dma((3,)),
             dma,
         ),
@@ -391,9 +400,9 @@
     )
     cy_before, cy_after = ring_pair(cy[ROWS - 2 :], cy[:1], "band", False)
 
-    keep, give = call(
+    keep, give, far = call(
         mix_kernel,
-        [((CHIPS, WIDE, SLAB, LON), f32)] * 2,
+        [((CHIPS, WIDE, SLAB, LON), f32)] * 2 + [((WIDE, SLAB, LON), f32)],
         (
             kern.reshape(BANDS * slots, LEV),
             sound_cols.reshape(1, BANDS * slots),
@@ -408,11 +417,11 @@
         ),
         (
             pltpu.VMEM((BANDS * slots, 2 * LEV), bf16),
-            pltpu.VMEM((GROUP * LON, BANDS * slots), bf16),
+            pltpu.VMEM((ROWS // GROUP, GROUP * LON, BANDS * slots), bf16),
             pltpu.VMEM(grid, f32),
             pltpu.VMEM((ROWS + 2, LEV, LON), f32),
             pltpu.VMEM((WIDE, LEV, LON), f32),
-            pltpu.VMEM((ROWS, 2, LEV, LEV), bf16),
+            pltpu.VMEM((ROWS, LEV, 2 * LEV), bf16),
             pltpu.VMEM((ROWS, LON), f32),
             pltpu.VMEM((ROWS, LON), jnp.int32),
             pltpu.VMEM((ROWS, LON), jnp.int32),
@@ -420,31 +429,42 @@
             dma((3,)),
         ),
         hbm_in=(6, 7, 8, 9),
+        vmem=24,
     )
     got = lax.ppermute(give, "band", [(i, i ^ 1) for i in range(BANDS)])
-    moved = list(call(join_kernel, [((CORES, WIDE, SLAB, LON), f32)] * CHIPS, (keep, got)))
-    for t in ORDER:
-        moved[t] = lax.ppermute(moved[t], "band", [(i, (i + CORES * t) % BANDS) for i in range(BANDS)])
+
+    def move(block, t):
+        return lax.ppermute(block, "band", [(i, (i + CORES * t) % BANDS) for i in range(BANDS)])
+
+    far = move(far, FAR)
+    rest, *near = call(
+        join_kernel,
+        [((WIDE, SLAB, LON), f32)] + [((ROWS + WIDE, SLAB, LON), f32)] * len(NEAR),
+        (keep, got),
+    )
+    near = [near[0]] + [move(block, t) for block, t in zip(near[1:], NEAR[1:])]
+    moved = (far, move(rest, FAR), *near)
 
     strips = (BANDS, HALVES, SLAB, LON)
     tiles = (BANDS * ROWS, SLAB, LON)
-    cx, cx_left, cx_right = call(faces_kernel, [(tiles, f32), (strips, f32), (strips, f32)], (courant_x,))
+    cx, cx_low, cx_left, cx_right = call(faces_kernel, [(tiles, f32), (tiles, f32), (strips, f32), (strips, f32)], (courant_x,))
     cx_west, cx_east = ring_pair(cx_right, cx_left, "region", True)
     (coef,) = call(
         sides_kernel,
         [((BANDS, HALVES, 2, 3, SLAB, LON), f32)],
         (cx_left, cx_right, cx_west, cx_east),
     )
-    own, left, right = call(pack_kernel, [(tiles, f32), (strips, f32), (strips, f32)], tuple(moved))
+    own, left, right = call(pack_kernel, [(tiles, f32), (strips, f32), (strips, f32)], moved)
     west, east = ring_pair(right, left, "region", True)
     chunk = pltpu.VMEM((CHUNK * ROWS, SLAB, LON), f32)
-    (inner,) = call(zonal_kernel, [(tiles, f32)], (own, cx), (chunk,) * 5)
+    (inner,) = call(zonal_kernel, [(tiles, f32)], (own, cx, cx_low), (chunk,) * 2)
     flat = pltpu.VMEM((BANDS * HALVES, SLAB, LON), f32)
     return call(
         merge_kernel,
         [((SLAB, BANDS * ROWS, LON), f32)],
         (inner, left, right, west, east, coef),
-        (flat,) * 3,
+        (flat,) * 3 + (pltpu.VMEM((SLAB, BANDS * ROWS, LON), f32), dma((BANDS // CHUNK,))),
+        hbm_out=(0,),
     )[0]
 
 

time: 89.4 us -> 81.5 us (0.912)
  Pallas kernels: 22.3 us -> 18.7 us
  starting transfers between devices: 41.3 us -> 38 us
  waiting for transfers between devices: 25.1 us -> 23.1 us
    pallas_call x9, Pallas kernels: 22.3 us -> 18.7 us  [call(): pl.pallas_call(body, out_shape=[(pltpu.HBM if k in hbm_out else jax.Shape...]
    ppermute x7 -> x8, waiting for transfers between devices: 14 us -> 11.9 us  [move(): lax.ppermute(block, 'band', [(i, (i + CORES * t) % BANDS) for i in range(...]
    ppermute x7 -> x8, starting transfers between devices: 14.4 us -> 12.5 us  [move(): lax.ppermute(block, 'band', [(i, (i + CORES * t) % BANDS) for i in range(...]
    ppermute x3, starting transfers between devices: 10.6 us -> 9.45 us  [ring_pair(): from_next = lax.ppermute(down_value, axis, [(b, a) for a, b in up])]
  transfers between devices with their start and end apart: 15 -> 16, of which waited for: 7 -> 5; matrix products, arithmetic and copies ran while one was open for 0% -> 0% of each run, Pallas kernels for 12% -> 11%
where the time goes in v4:
time: 81.5 us; the launch traced here: 80.2 us
  starting transfers between devices  38 us (47%)
  waiting for transfers between devices  23.1 us (28%)
  Pallas kernels  18.7 us (23%)
    pallas_call x9, Pallas kernels, call(): pl.pallas_call(body, out_shape=[(pltpu.HBM if k in hbm_out else jax.Shape...  18.7 us
    ppermute x8, starting transfers between devices, move(): lax.ppermute(block, 'band', [(i, (i + CORES * t) % BANDS) for i in range(...  12.5 us
    ppermute x8, waiting for transfers between devices, move(): lax.ppermute(block, 'band', [(i, (i + CORES * t) % BANDS) for i in range(...  11.9 us
    all_to_all x1, starting transfers between devices, swap_bands(): lax.all_to_all(blocks, 'band', split_axis=0, concat_axis=0, tiled=True)  9.98 us
    ppermute x3, starting transfers between devices, ring_pair(): from_next = lax.ppermute(down_value, axis, [(b, a) for a, b in up])  9.45 us
    ppermute x3, waiting for transfers between devices, ring_pair(): from_next = lax.ppermute(down_value, axis, [(b, a) for a, b in up])  6.48 us
    ppermute x3, starting transfers between devices, ring_pair(): from_prev = lax.ppermute(up_value, axis, up)  6.04 us
    all_to_all x1, waiting for transfers between devices, swap_bands(): lax.all_to_all(blocks, 'band', split_axis=0, concat_axis=0, tiled=True)  2.6 us
  transfers between devices with their start and end apart: 16, of which 5 were waited for; matrix products, arithmetic and copies ran while one was open for 0% of the time, Pallas kernels for 11%

profile of v4, /device:TPU:1, one launch (start us, length us, event | category | flops | bytes accessed | tf_op | source)
XLA Modules:
  0.0 80.2 jit_solution(17307583352899509798)
XLA Ops:
  0.0 2.3 %shard_map.109 = f32[16,64,128]{2,1,0:T(8,128)} custom-call(s32[1,16]{1,0:T(1,128)} %count_hbm.1, f32[1,16,64]{2,1,0:T(8,128)} %value_hbm.1, f32[1,16,64,128]{3,2,1,0:T(8,128)} %kern_hbm.1), custom_call_target="tpu_custom_call" | custom-call | tf_op jit(solution)/shard_map/pallas_call | solution.py:340
  2.3 10.0 %all-to-all-start = ((f32[16,64,128]{2,1,0:T(8,128)}), f32[16,64,128]{2,1,0:T(8,128)S(1)}, u32[]{:S(2)}, u32[]{:S(2)}) async-start(f32[16,64,128]{2,1,0:T(8,128)} %shard_map.109), calls=%async_computation | async-start | bytes 1048576 | tf_op jit(solution)/shard_map/all_to_all | solution.py:361
  12.3 2.7 %shard_map.110 = (f32[16,128,128]{2,1,0:T(8,128)S(1)}, f32[16,128,128]{2,1,0:T(8,128)S(1)}, bf16[16,128,256]{2,1,0:T(8,128)(2,1)}) custom-call(f32[128,16,128]{2,1,0:T(8,128)} %field_hbm.1, f32[128,16,128]{2,1,0:T(8,128)} %cy_hbm.1, f32[16,128,128]{2,1,0:T(8,128)} %diff_hbm.1), custom_call_target="tpu_custom_call" | custom-call | tf_op jit(solution)/shard_map/pallas_call | solution.py:340
  15.0 0.0 copy-start.1
  15.0 3.5 %collective-permute-start = (f32[2,128,128]{2,1,0:T(8,128)S(1)}, f32[2,128,128]{2,1,0:T(8,128)S(1)}, u32[]{:S(2)}, u32[]{:S(2)}) collective-permute-start(f32[2,128,128]{2,1,0:T(8,128)S(1)} %slice.6), channel_id=1, source_target_pairs={{0,1},{1,2},{2,3},{3,4},{4,5},{5,6},{6,7},{7,8},{8,9},{9,10},{10,1... | collective-permute-start | bytes 393224 | tf_op jit(solution)/shard_map/ppermute | solution.py:355
  18.5 1.9 %collective-permute-start.1 = (f32[1,128,128]{2,1,0:T(8,128)S(1)}, f32[1,128,128]{2,1,0:T(8,128)S(1)}, u32[]{:S(2)}, u32[]{:S(2)}) collective-permute-start(f32[1,128,128]{2,1,0:T(8,128)S(1)} %slice.7), channel_id=1, source_target_pairs={{1,0},{2,1},{3,2},{4,3},{5,4},{6,5},{7,6},{8,7},{9,8},{10,9},{11,1... | collective-permute-start | bytes 196616 | tf_op jit(solution)/shard_map/ppermute | solution.py:356
  20.5 0.0 copy-done.1
  20.5 0.1 reshape.7.cols_ref
  20.6 6.5 %collective-permute-done.1.after_ref = f32[1,128,128]{2,1,0:T(8,128)S(1)} collective-permute-done((f32[1,128,128]{2,1,0:T(8,128)S(1)}, f32[1,128,128]{2,1,0:T(8,128)S(1)}, u32[]{:S(2)}, u32[]{:S(2)}) %collective-permute-start.1) | collective-permute-done | bytes 65568 | tf_op jit(solution)/shard_map/ppermute | solution.py:356
  27.0 0.0 collective-permute-done.before_ref
  27.0 2.6 %all-to-all-done = f32[16,64,128]{2,1,0:T(8,128)S(1)} async-done(((f32[16,64,128]{2,1,0:T(8,128)}), f32[16,64,128]{2,1,0:T(8,128)S(1)}, u32[]{:S(2)}, u32[]{:S(2)}) %all-to-all-start) | async-done | bytes 524320 | tf_op jit(solution)/shard_map/all_to_all | solution.py:361
  29.6 5.6 %shard_map.111 = (f32[8,20,8,128]{3,2,1,0:T(8,128)S(1)}, f32[8,20,8,128]{3,2,1,0:T(8,128)S(1)}, f32[20,8,128]{2,1,0:T(8,128)S(1)}) custom-call(f32[1024,128]{1,0:T(8,128)S(1)} %bitcast.1, s32[1,1024]{1,0:T(1,128)S(1)} %reshape.7.cols_ref, f32[16,128,128]{2,1,0:T(8,128)S(1)} %get-tuple-element.26.field_ref, f32[16,128,128]{2,1,0:T(8,128)S(1)} %get-tuple-element.27.cy_ref, ...), custom_call_target="tpu_custom_call" | custom-call | tf_op jit(solution)/shard_map/pallas_call | solution.py:340
  35.3 0.0 copy-start
  35.3 0.1 collective-permute-start.3
  35.4 2.1 %collective-permute-done.3.got_ref = f32[8,20,8,128]{3,2,1,0:T(8,128)S(1)} collective-permute-done((f32[8,20,8,128]{3,2,1,0:T(8,128)S(1)}, f32[8,20,8,128]{3,2,1,0:T(8,128)S(1)}, u32[]{:S(2)}, u32[]{:S(2)}) %collective-permute-start.3) | collective-permute-done | bytes 655392 | tf_op jit(solution)/shard_map/ppermute | solution.py:434
  37.5 0.1 shard_map.112
  37.6 0.5 collective-permute-start.10
  38.1 3.2 %collective-permute-start.2 = (f32[20,8,128]{2,1,0:T(8,128)S(1)}, f32[20,8,128]{2,1,0:T(8,128)S(1)}, u32[]{:S(2)}, u32[]{:S(2)}) collective-permute-start(f32[20,8,128]{2,1,0:T(8,128)S(1)} %get-tuple-element.29), channel_id=1, source_target_pairs={{0,8},{1,9},{2,10},{3,11},{4,12},{5,13},{6,14},{7,15},{8,0},{9,1},... | collective-permute-start | bytes 245768 | tf_op jit(solution)/shard_map/ppermute | solution.py:437
  41.3 2.2 %collective-permute-start.4 = (f32[20,8,128]{2,1,0:T(8,128)S(1)}, f32[20,8,128]{2,1,0:T(8,128)S(1)}, u32[]{:S(2)}, u32[]{:S(2)}) collective-permute-start(f32[20,8,128]{2,1,0:T(8,128)S(1)} %get-tuple-element.32), channel_id=1, source_target_pairs={{0,8},{1,9},{2,10},{3,11},{4,12},{5,13},{6,14},{7,15},{8,0},{9,1},... | collective-permute-start | bytes 245768 | tf_op jit(solution)/shard_map/ppermute | solution.py:437
  43.4 0.9 %collective-permute-start.5 = (f32[36,8,128]{2,1,0:T(8,128)S(1)}, f32[36,8,128]{2,1,0:T(8,128)S(1)}, u32[]{:S(2)}, u32[]{:S(2)}) collective-permute-start(f32[36,8,128]{2,1,0:T(8,128)S(1)} %get-tuple-element.34), channel_id=1, source_target_pairs={{0,6},{1,7},{2,8},{3,9},{4,10},{5,11},{6,12},{7,13},{8,14},{9,15},... | collective-permute-start | bytes 442376 | tf_op jit(solution)/shard_map/ppermute | solution.py:437
  44.4 3.5 %collective-permute-start.6 = (f32[36,8,128]{2,1,0:T(8,128)S(1)}, f32[36,8,128]{2,1,0:T(8,128)S(1)}, u32[]{:S(2)}, u32[]{:S(2)}) collective-permute-start(f32[36,8,128]{2,1,0:T(8,128)S(1)} %get-tuple-element.35), channel_id=1, source_target_pairs={{0,10},{1,11},{2,12},{3,13},{4,14},{5,15},{6,0},{7,1},{8,2},{9,3},... | collective-permute-start | bytes 442376 | tf_op jit(solution)/shard_map/ppermute | solution.py:437
  47.9 0.0 collective-permute-done.2.refs_0_
  47.9 0.0 collective-permute-start.7
  47.9 2.5 %collective-permute-done.4.refs_1_ = f32[20,8,128]{2,1,0:T(8,128)S(1)} collective-permute-done((f32[20,8,128]{2,1,0:T(8,128)S(1)}, f32[20,8,128]{2,1,0:T(8,128)S(1)}, u32[]{:S(2)}, u32[]{:S(2)}) %collective-permute-start.4) | collective-permute-done | bytes 81952 | tf_op jit(solution)/shard_map/ppermute | solution.py:437
  50.4 1.6 %collective-permute-start.8 = (f32[36,8,128]{2,1,0:T(8,128)S(1)}, f32[36,8,128]{2,1,0:T(8,128)S(1)}, u32[]{:S(2)}, u32[]{:S(2)}) collective-permute-start(f32[36,8,128]{2,1,0:T(8,128)S(1)} %get-tuple-element.37), channel_id=1, source_target_pairs={{0,12},{1,13},{2,14},{3,15},{4,0},{5,1},{6,2},{7,3},{8,4},{9,5},{1... | collective-permute-start | bytes 442376 | tf_op jit(solution)/shard_map/ppermute | solution.py:437
  52.0 0.0 collective-permute-done.10.refs_8_
  52.0 0.5 collective-permute-start.9
  52.5 0.0 copy-done
  52.5 1.9 %shard_map.114 = (f32[256,8,128]{2,1,0:T(8,128)S(1)}, f32[256,8,128]{2,1,0:T(8,128)S(1)}, f32[16,2,8,128]{3,2,1,0:T(8,128)S(1)}, f32[16,2,8,128]{3,2,1,0:T(8,128)S(1)}) custom-call(f32[8,256,128]{2,1,0:T(8,128)S(1)} %copy-done), custom_call_target="tpu_custom_call" | custom-call | tf_op jit(solution)/shard_map/pallas_call | solution.py:340
  54.4 9.4 %collective-permute-done.5.refs_3_ = f32[36,8,128]{2,1,0:T(8,128)S(1)} collective-permute-done((f32[36,8,128]{2,1,0:T(8,128)S(1)}, f32[36,8,128]{2,1,0:T(8,128)S(1)}, u32[]{:S(2)}, u32[]{:S(2)}) %collective-permute-start.5) | collective-permute-done | bytes 147488 | tf_op jit(solution)/shard_map/ppermute | solution.py:437
  63.8 1.2 %collective-permute-start.13 = (f32[16,2,8,128]{3,2,1,0:T(8,128)S(1)}, f32[16,2,8,128]{3,2,1,0:T(8,128)S(1)}, u32[]{:S(2)}, u32[]{:S(2)}) collective-permute-start(f32[16,2,8,128]{3,2,1,0:T(8,128)S(1)} %get-tuple-element.46.right_ref), channel_id=1, source_target_pairs={{0,16},{16,32},{32,48},{48,64},{64,80},{80,96},{96,112},{112,128},... | collective-permute-start | bytes 393224 | tf_op jit(solution)/shard_map/ppermute | solution.py:355
  65.0 0.0 collective-permute-done.6.refs_4_
  65.0 3.7 %collective-permute-start.14 = (f32[16,2,8,128]{3,2,1,0:T(8,128)S(1)}, f32[16,2,8,128]{3,2,1,0:T(8,128)S(1)}, u32[]{:S(2)}, u32[]{:S(2)}) collective-permute-start(f32[16,2,8,128]{3,2,1,0:T(8,128)S(1)} %get-tuple-element.45.left_ref), channel_id=1, source_target_pairs={{16,0},{32,16},{48,32},{64,48},{80,64},{96,80},{112,96},{128,112},... | collective-permute-start | bytes 393224 | tf_op jit(solution)/shard_map/ppermute | solution.py:356
  68.7 0.0 collective-permute-done.7.refs_5_
  68.7 0.0 collective-permute-done.8.refs_6_
  68.7 0.0 collective-permute-done.9.refs_7_
  68.7 1.0 %shard_map.113 = (f32[256,8,128]{2,1,0:T(8,128)S(1)}, f32[16,2,8,128]{3,2,1,0:T(8,128)S(1)}, f32[16,2,8,128]{3,2,1,0:T(8,128)S(1)}) custom-call(f32[20,8,128]{2,1,0:T(8,128)S(1)} %collective-permute-done.2.refs_0_, f32[20,8,128]{2,1,0:T(8,128)S(1)} %collective-permute-done.4.refs_1_, f32[36,8,128]{2,1,0:T(8,128)S(1)} %get-tuple-element.33.refs_2_, ...), custom_call_target="tpu_custom_call" | custom-call | tf_op jit(solution)/shard_map/pallas_call | solution.py:340
  69.7 1.3 %collective-permute-start.11 = (f32[16,2,8,128]{3,2,1,0:T(8,128)S(1)}, f32[16,2,8,128]{3,2,1,0:T(8,128)S(1)}, u32[]{:S(2)}, u32[]{:S(2)}) collective-permute-start(f32[16,2,8,128]{3,2,1,0:T(8,128)S(1)} %get-tuple-element.44.right_ref), channel_id=1, source_target_pairs={{0,16},{16,32},{32,48},{48,64},{64,80},{80,96},{96,112},{112,128},... | collective-permute-start | bytes 393224 | tf_op jit(solution)/shard_map/ppermute | solution.py:355
  71.0 3.8 %collective-permute-start.12 = (f32[16,2,8,128]{3,2,1,0:T(8,128)S(1)}, f32[16,2,8,128]{3,2,1,0:T(8,128)S(1)}, u32[]{:S(2)}, u32[]{:S(2)}) collective-permute-start(f32[16,2,8,128]{3,2,1,0:T(8,128)S(1)} %get-tuple-element.43.left_ref), channel_id=1, source_target_pairs={{16,0},{32,16},{48,32},{64,48},{80,64},{96,80},{112,96},{128,112},... | collective-permute-start | bytes 393224 | tf_op jit(solution)/shard_map/ppermute | solution.py:356
  74.8 0.0 collective-permute-done.13.west_ref
  74.8 0.0 collective-permute-done.14.east_ref
  74.8 0.6 shard_map.116.coef_ref
  75.5 2.5 %shard_map.115.inner_ref = f32[256,8,128]{2,1,0:T(8,128)S(1)} custom-call(f32[256,8,128]{2,1,0:T(8,128)S(1)} %get-tuple-element.40.own_ref, f32[256,8,128]{2,1,0:T(8,128)S(1)} %get-tuple-element.41.cx_ref, f32[256,8,128]{2,1,0:T(8,128)S(1)} %get-tuple-element.42.low_ref), custom_call_target="tpu_custom_call" | custom-call | tf_op jit(solution)/shard_map/pallas_call | solution.py:340
  77.9 0.0 collective-permute-done.11.west_ref
  77.9 0.0 collective-permute-done.12.east_ref
  78.0 2.1 %shard_map.117 = f32[8,256,128]{2,1,0:T(8,128)} custom-call(f32[256,8,128]{2,1,0:T(8,128)S(1)} %shard_map.115.inner_ref, f32[16,2,8,128]{3,2,1,0:T(8,128)S(1)} %get-tuple-element.43.left_ref, f32[16,2,8,128]{3,2,1,0:T(8,128)S(1)} %get-tuple-element.44.right_ref, f32[16,2,8,128]{3,2,1,0:T(8,128)S(1)} %collective-permute-done.11.west_ref, ...), custom_call_target="tpu_custom_call" | custom-call | tf_op jit(solution)/shard_map/pallas_call | solution.py:340
  (2 shorter events, 0.0 us)
Async XLA Ops:
  2.3 27.4 %all-to-all-start = ((f32[16,64,128]{2,1,0:T(8,128)}), f32[16,64,128]{2,1,0:T(8,128)S(1)}, u32[]{:S(2)}, u32[]{:S(2)}) async-start(f32[16,64,128]{2,1,0:T(8,128)} %shard_map.109), calls=%async_computation | async-start | bytes 1048576 | tf_op jit(solution)/shard_map/all_to_all | solution.py:361
  15.0 5.5 %copy-start.1 = (s32[1,16,64]{2,1,0:T(8,128)S(1)}, s32[1,16,64]{2,1,0:T(8,128)}, u32[]{:S(2)}) copy-start(s32[1,16,64]{2,1,0:T(8,128)} %param.21) | copy-start | bytes 12292
  15.0 12.1 %collective-permute-start = (f32[2,128,128]{2,1,0:T(8,128)S(1)}, f32[2,128,128]{2,1,0:T(8,128)S(1)}, u32[]{:S(2)}, u32[]{:S(2)}) collective-permute-start(f32[2,128,128]{2,1,0:T(8,128)S(1)} %slice.6), channel_id=1, source_target_pairs={{0,1},{1,2},{2,3},{3,4},{4,5},{5,6},{6,7},{7,8},{8,9},{9,10},{10,1... | collective-permute-start | bytes 393224 | tf_op jit(solution)/shard_map/ppermute | solution.py:355
  18.5 8.5 %collective-permute-start.1 = (f32[1,128,128]{2,1,0:T(8,128)S(1)}, f32[1,128,128]{2,1,0:T(8,128)S(1)}, u32[]{:S(2)}, u32[]{:S(2)}) collective-permute-start(f32[1,128,128]{2,1,0:T(8,128)S(1)} %slice.7), channel_id=1, source_target_pairs={{1,0},{2,1},{3,2},{4,3},{5,4},{6,5},{7,6},{8,7},{9,8},{10,9},{11,1... | collective-permute-start | bytes 196616 | tf_op jit(solution)/shard_map/ppermute | solution.py:356
  35.3 17.3 %copy-start = (f32[8,256,128]{2,1,0:T(8,128)S(1)}, f32[8,256,128]{2,1,0:T(8,128)}, u32[]{:S(2)}) copy-start(f32[8,256,128]{2,1,0:T(8,128)} %cx_ref.1) | copy-start | bytes 3145732
  35.3 2.2 %collective-permute-start.3 = (f32[8,20,8,128]{3,2,1,0:T(8,128)S(1)}, f32[8,20,8,128]{3,2,1,0:T(8,128)S(1)}, u32[]{:S(2)}, u32[]{:S(2)}) collective-permute-start(f32[8,20,8,128]{3,2,1,0:T(8,128)S(1)} %get-tuple-element.31), channel_id=1, source_target_pairs={{0,1},{1,0},{2,3},{3,2},{4,5},{5,4},{6,7},{7,6},{8,9},{9,8},{10,11... | collective-permute-start | bytes 1966088 | tf_op jit(solution)/shard_map/ppermute | solution.py:434
  37.6 14.5 %collective-permute-start.10 = (f32[36,8,128]{2,1,0:T(8,128)S(1)}, f32[36,8,128]{2,1,0:T(8,128)S(1)}, u32[]{:S(2)}, u32[]{:S(2)}) collective-permute-start(f32[36,8,128]{2,1,0:T(8,128)S(1)} %get-tuple-element.39), channel_id=1, source_target_pairs={{0,14},{1,15},{2,0},{3,1},{4,2},{5,3},{6,4},{7,5},{8,6},{9,7},{10,... | collective-permute-start | bytes 442376 | tf_op jit(solution)/shard_map/ppermute | solution.py:437
  38.1 9.9 %collective-permute-start.2 = (f32[20,8,128]{2,1,0:T(8,128)S(1)}, f32[20,8,128]{2,1,0:T(8,128)S(1)}, u32[]{:S(2)}, u32[]{:S(2)}) collective-permute-start(f32[20,8,128]{2,1,0:T(8,128)S(1)} %get-tuple-element.29), channel_id=1, source_target_pairs={{0,8},{1,9},{2,10},{3,11},{4,12},{5,13},{6,14},{7,15},{8,0},{9,1},... | collective-permute-start | bytes 245768 | tf_op jit(solution)/shard_map/ppermute | solution.py:437
  41.3 9.1 %collective-permute-start.4 = (f32[20,8,128]{2,1,0:T(8,128)S(1)}, f32[20,8,128]{2,1,0:T(8,128)S(1)}, u32[]{:S(2)}, u32[]{:S(2)}) collective-permute-start(f32[20,8,128]{2,1,0:T(8,128)S(1)} %get-tuple-element.32), channel_id=1, source_target_pairs={{0,8},{1,9},{2,10},{3,11},{4,12},{5,13},{6,14},{7,15},{8,0},{9,1},... | collective-permute-start | bytes 245768 | tf_op jit(solution)/shard_map/ppermute | solution.py:437
  43.4 20.3 %collective-permute-start.5 = (f32[36,8,128]{2,1,0:T(8,128)S(1)}, f32[36,8,128]{2,1,0:T(8,128)S(1)}, u32[]{:S(2)}, u32[]{:S(2)}) collective-permute-start(f32[36,8,128]{2,1,0:T(8,128)S(1)} %get-tuple-element.34), channel_id=1, source_target_pairs={{0,6},{1,7},{2,8},{3,9},{4,10},{5,11},{6,12},{7,13},{8,14},{9,15},... | collective-permute-start | bytes 442376 | tf_op jit(solution)/shard_map/ppermute | solution.py:437
  44.4 20.6 %collective-permute-start.6 = (f32[36,8,128]{2,1,0:T(8,128)S(1)}, f32[36,8,128]{2,1,0:T(8,128)S(1)}, u32[]{:S(2)}, u32[]{:S(2)}) collective-permute-start(f32[36,8,128]{2,1,0:T(8,128)S(1)} %get-tuple-element.35), channel_id=1, source_target_pairs={{0,10},{1,11},{2,12},{3,13},{4,14},{5,15},{6,0},{7,1},{8,2},{9,3},... | collective-permute-start | bytes 442376 | tf_op jit(solution)/shard_map/ppermute | solution.py:437
  47.9 20.8 %collective-permute-start.7 = (f32[36,8,128]{2,1,0:T(8,128)S(1)}, f32[36,8,128]{2,1,0:T(8,128)S(1)}, u32[]{:S(2)}, u32[]{:S(2)}) collective-permute-start(f32[36,8,128]{2,1,0:T(8,128)S(1)} %get-tuple-element.36), channel_id=1, source_target_pairs={{0,4},{1,5},{2,6},{3,7},{4,8},{5,9},{6,10},{7,11},{8,12},{9,13},{1... | collective-permute-start | bytes 442376 | tf_op jit(solution)/shard_map/ppermute | solution.py:437
  50.4 18.3 %collective-permute-start.8 = (f32[36,8,128]{2,1,0:T(8,128)S(1)}, f32[36,8,128]{2,1,0:T(8,128)S(1)}, u32[]{:S(2)}, u32[]{:S(2)}) collective-permute-start(f32[36,8,128]{2,1,0:T(8,128)S(1)} %get-tuple-element.37), channel_id=1, source_target_pairs={{0,12},{1,13},{2,14},{3,15},{4,0},{5,1},{6,2},{7,3},{8,4},{9,5},{1... | collective-permute-start | bytes 442376 | tf_op jit(solution)/shard_map/ppermute | solution.py:437
  52.0 16.7 %collective-permute-start.9 = (f32[36,8,128]{2,1,0:T(8,128)S(1)}, f32[36,8,128]{2,1,0:T(8,128)S(1)}, u32[]{:S(2)}, u32[]{:S(2)}) collective-permute-start(f32[36,8,128]{2,1,0:T(8,128)S(1)} %get-tuple-element.38), channel_id=1, source_target_pairs={{0,2},{1,3},{2,4},{3,5},{4,6},{5,7},{6,8},{7,9},{8,10},{9,11},{10,... | collective-permute-start | bytes 442376 | tf_op jit(solution)/shard_map/ppermute | solution.py:437
  63.8 11.1 %collective-permute-start.13 = (f32[16,2,8,128]{3,2,1,0:T(8,128)S(1)}, f32[16,2,8,128]{3,2,1,0:T(8,128)S(1)}, u32[]{:S(2)}, u32[]{:S(2)}) collective-permute-start(f32[16,2,8,128]{3,2,1,0:T(8,128)S(1)} %get-tuple-element.46.right_ref), channel_id=1, source_target_pairs={{0,16},{16,32},{32,48},{48,64},{64,80},{80,96},{96,112},{112,128},... | collective-permute-start | bytes 393224 | tf_op jit(solution)/shard_map/ppermute | solution.py:355
  65.0 9.9 %collective-permute-start.14 = (f32[16,2,8,128]{3,2,1,0:T(8,128)S(1)}, f32[16,2,8,128]{3,2,1,0:T(8,128)S(1)}, u32[]{:S(2)}, u32[]{:S(2)}) collective-permute-start(f32[16,2,8,128]{3,2,1,0:T(8,128)S(1)} %get-tuple-element.45.left_ref), channel_id=1, source_target_pairs={{16,0},{32,16},{48,32},{64,48},{80,64},{96,80},{112,96},{128,112},... | collective-permute-start | bytes 393224 | tf_op jit(solution)/shard_map/ppermute | solution.py:356
  69.7 8.2 %collective-permute-start.11 = (f32[16,2,8,128]{3,2,1,0:T(8,128)S(1)}, f32[16,2,8,128]{3,2,1,0:T(8,128)S(1)}, u32[]{:S(2)}, u32[]{:S(2)}) collective-permute-start(f32[16,2,8,128]{3,2,1,0:T(8,128)S(1)} %get-tuple-element.44.right_ref), channel_id=1, source_target_pairs={{0,16},{16,32},{32,48},{48,64},{64,80},{80,96},{96,112},{112,128},... | collective-permute-start | bytes 393224 | tf_op jit(solution)/shard_map/ppermute | solution.py:355
  71.0 6.9 %collective-permute-start.12 = (f32[16,2,8,128]{3,2,1,0:T(8,128)S(1)}, f32[16,2,8,128]{3,2,1,0:T(8,128)S(1)}, u32[]{:S(2)}, u32[]{:S(2)}) collective-permute-start(f32[16,2,8,128]{3,2,1,0:T(8,128)S(1)} %get-tuple-element.43.left_ref), channel_id=1, source_target_pairs={{16,0},{32,16},{48,32},{64,48},{80,64},{96,80},{112,96},{128,112},... | collective-permute-start | bytes 393224 | tf_op jit(solution)/shard_map/ppermute | solution.py:356

commit v5 on v4

--- a/solution.py
+++ b/solution.py
@@ -1,3 +1,5 @@
+import functools
+
 import jax
 import jax.numpy as jnp
 from jax import lax
@@ -154,7 +156,7 @@
 def mix_kernel(
     kern_ref, cols_ref, field_ref, cy_ref, before_ref, after_ref, diff_hbm, conv_hbm, base_hbm, top_hbm,
     keep_out, give_out, far_out,
-    parts, onehot, mixed, once, twice, diff_buf, conv_ref, base_ref, top_ref, diff_sem, sem,
+    parts, onehot, added, mixed, diff_buf, conv_ref, base_ref, top_ref, diff_sem, sem,
 ):
     def diff_copy(g):
         span = pl.ds(g * GROUP, GROUP)
@@ -177,20 +179,28 @@
         copy.wait()
     level = lax.broadcasted_iota(jnp.int32, (LEV, LON), 0)
 
-    for g in range(ROWS // GROUP):
+    half = parts.shape[0] // 2
+
+    def spread(g):
         cols = cols_ref[...]
         for q in range(GROUP):
             here = jnp.where(cols // LON == g * GROUP + q, cols % LON, -1).astype(f32).astype(bf16)
             for r in range(0, LON, 32):
                 cell = lax.broadcasted_iota(jnp.int32, (32, cols.shape[1]), 0) + r
                 match = cell.astype(f32).astype(bf16) == here
-                onehot[g, q * LON + r : q * LON + r + 32, :] = jnp.where(match, jnp.ones((), bf16), jnp.zeros((), bf16))
-        both = jnp.dot(onehot[g], parts[...], preferred_element_type=f32)
-        added = both[:, :LEV] + both[:, LEV:]
+                onehot[g, q * LON + r : q * LON + r + 32, :] = jnp.where(
+                    match, jnp.ones((), bf16), jnp.zeros((), bf16)
+                )
+        first = jnp.dot(onehot[g, :, :half], parts[:half], preferred_element_type=f32)
+        second = jnp.dot(onehot[g, :, half:], parts[half:], preferred_element_type=f32)
+        both = first + second
+        added[g] = both[:, :LEV] + both[:, LEV:]
+
+    def column(g):
         diff_copy(g).wait()
         for q in range(GROUP):
             row = g * GROUP + q
-            forced = field_ref[row] + added[q * LON : (q + 1) * LON].T
+            forced = field_ref[row] + added[g, q * LON : (q + 1) * LON].T
             base = base_ref[row : row + 1, :]
             top = top_ref[row : row + 1, :]
             inside = jnp.where((level >= base) & (level <= top), 1.0, 0.0)
@@ -200,40 +210,63 @@
             pair = jnp.concatenate([hi, lo], axis=1)
             both = jnp.dot(diff_buf[row], jnp.concatenate([pair, pair], axis=0), preferred_element_type=f32)
             mixed[row] = both[:, :LON] + both[:, LON:]
+
+    spread(0)
+    for g in range(ROWS // GROUP):
+        if g + 1 < ROWS // GROUP:
+            spread(g + 1)
+        column(g)
+
     open_face = jnp.where(lax.axis_index("band") == BANDS - 1, 0.0, 1.0)
-
-    def face(row):
-        if row < 0:
-            return before_ref[row + 2]
-        if row == ROWS:
-            return after_ref[0]
-        return cy_ref[row] * open_face if row == ROWS - 1 else cy_ref[row]
-
-    def partial_sweep(value, first, last, row):
-        own = value(row) if first <= row <= last else None
-        terms = []
-        if own is not None or row - 1 >= first:
-            low = jnp.minimum(face(row - 1), 0.0) if row > -2 else None
-        if own is not None:
-            terms.append((1.0 - jnp.maximum(face(row), 0.0) + low) * own)
-        if first <= row + 1 <= last:
-            terms.append(jnp.maximum(face(row), 0.0) * value(row + 1))
-        if first <= row - 1 <= last:
-            terms.append(-(low * value(row - 1)))
-        return sum(terms[1:], terms[0])
-
-    for row in range(-1, ROWS + 1):
-        once[row + 1] = partial_sweep(lambda r: mixed[r], 0, ROWS - 1, row)
-    for row in range(-2, ROWS + 2):
-        value = partial_sweep(lambda r: once[r + 1], -1, ROWS, row)
-        twice[row + 2] = value
     z, core = lax.axis_index("band") // CORES, lax.axis_index("band") % CORES
+
+    def meridional(slab, store):
+        span = pl.ds(pl.multiple_of(slab * SLAB, SLAB), SLAB)
+        faces = {}
+
+        def face(row):
+            if row not in faces:
+                if row < 0:
+                    courant = before_ref[row + 2, span]
+                elif row == ROWS:
+                    courant = after_ref[0, span]
+                else:
+                    courant = cy_ref[row, span]
+                if row == ROWS - 1:
+                    courant = courant * open_face
+                faces[row] = jnp.maximum(courant, 0.0), jnp.minimum(courant, 0.0)
+            return faces[row]
+
+        def partial_sweep(values, row):
+            terms = []
+            if row in values:
+                terms.append((1.0 - face(row)[0] + face(row - 1)[1]) * values[row])
+            if row + 1 in values:
+                terms.append(face(row)[0] * values[row + 1])
+            if row - 1 in values:
+                terms.append(-(face(row - 1)[1] * values[row - 1]))
+            return sum(terms[1:], terms[0])
+
+        values = {row: mixed[row, span] for row in range(ROWS)}
+        swept = {-1: partial_sweep(values, -1)}
+        for row in range(ROWS + 4):
+            if row <= ROWS:
+                swept[row] = partial_sweep(values, row)
+            store(row - 2, partial_sweep(swept, row - 2))
+
     for t in range(CHIPS):
         pair = CORES * ((z + t) % CHIPS)
-        for row in range(WIDE):
-            keep_out[t, row] = twice[row, pl.ds(pl.multiple_of((pair + core) * SLAB, SLAB), SLAB)]
-            give_out[t, row] = twice[row, pl.ds(pl.multiple_of((pair + 1 - core) * SLAB, SLAB), SLAB)]
-    far_out[...] = keep_out[FAR]
+
+        def keep(row, value):
+            keep_out[t, row + 2] = value
+            if t == FAR:
+                far_out[row + 2] = value
+
+        def give(row, value):
+            give_out[t, row + 2] = value
+
+        meridional(pair + core, keep)
+        meridional(pair + 1 - core, give)
 
 
 def join_kernel(keep_ref, got_ref, *outs):
@@ -277,16 +310,17 @@
     lax.fori_loop(0, BANDS // CHUNK, pack, 0)
 
 
-def zonal_kernel(own_ref, cx_ref, low_ref, out_ref, first, second):
+def zonal_kernel(part, own_ref, cx_ref, low_ref, out_ref, first, second):
     tiles = CHUNK * ROWS
+    chunks = BANDS // CHUNK // 2
 
     def sources(i, carry):
         old, new = first, second
         for step in range(XSTEPS):
             for t in range(tiles):
-                value = own_ref[i * tiles + t] if step == 0 else old[t]
-                up = jnp.maximum(cx_ref[i * tiles + t], 0.0)
-                low = low_ref[i * tiles + t]
+                value = own_ref[(part * chunks + i) * tiles + t] if step == 0 else old[t]
+                up = jnp.maximum(cx_ref[(part * chunks + i) * tiles + t], 0.0)
+                low = low_ref[(part * chunks + i) * tiles + t]
                 value = zonal_sweep(value, 1.0 - up + low, up, low)
                 if step == XSTEPS - 1:
                     out_ref[i * tiles + t] = value
@@ -295,10 +329,10 @@
             old, new = new, old
         return carry
 
-    lax.fori_loop(0, BANDS // CHUNK, sources, 0)
-
-
-def merge_kernel(inner_ref, left_ref, right_ref, west_ref, east_ref, coef_ref, out_hbm, sides, left_buf, right_buf, out_ref, sem):
+    lax.fori_loop(0, chunks, sources, 0)
+
+
+def merge_kernel(inner_a, inner_b, left_ref, right_ref, west_ref, east_ref, coef_ref, out_hbm, sides, left_buf, right_buf, out_ref, sem):
     count = BANDS * HALVES
     for n in range(count):
         s, half = n // HALVES, n % HALVES
@@ -326,7 +360,8 @@
                 packed = sides[i * HALVES + k]
                 for g in range(ROWS // HALVES):
                     lat = i * ROWS + k * (ROWS // HALVES) + g
-                    out_ref[:, lat, :] = jnp.where(outer, turned(packed, -STRIP * g - XSTEPS), inner_ref[lat])
+                    inner = inner_a[lat] if i < BANDS // 2 else inner_b[lat - BANDS // 2 * ROWS]
+                    out_ref[:, lat, :] = jnp.where(outer, turned(packed, -STRIP * g - XSTEPS), inner)
         store(c).start()
     for c in range(BANDS // CHUNK):
         store(c).wait()
@@ -418,9 +453,8 @@
         (
             pltpu.VMEM((BANDS * slots, 2 * LEV), bf16),
             pltpu.VMEM((ROWS // GROUP, GROUP * LON, BANDS * slots), bf16),
+            pltpu.VMEM((ROWS // GROUP, GROUP * LON, LEV), f32),
             pltpu.VMEM(grid, f32),
-            pltpu.VMEM((ROWS + 2, LEV, LON), f32),
-            pltpu.VMEM((WIDE, LEV, LON), f32),
             pltpu.VMEM((ROWS, LEV, 2 * LEV), bf16),
             pltpu.VMEM((ROWS, LON), f32),
             pltpu.VMEM((ROWS, LON), jnp.int32),
@@ -455,14 +489,23 @@
         (cx_left, cx_right, cx_west, cx_east),
     )
     own, left, right = call(pack_kernel, [(tiles, f32), (strips, f32), (strips, f32)], moved)
-    west, east = ring_pair(right, left, "region", True)
+    regions = lax.axis_size("region")
+    west = lax.ppermute(right, "region", [(i, (i + 1) % regions) for i in range(regions)])
+    east = lax.ppermute(left, "region", [((i + 1) % regions, i) for i in range(regions)])
     chunk = pltpu.VMEM((CHUNK * ROWS, SLAB, LON), f32)
-    (inner,) = call(zonal_kernel, [(tiles, f32)], (own, cx, cx_low), (chunk,) * 2)
+    inner = []
+    for part in range(2):
+        inner += call(
+            functools.partial(zonal_kernel, part),
+            [((BANDS * ROWS // 2, SLAB, LON), f32)],
+            (own, cx, cx_low),
+            (chunk,) * 2,
+        )
     flat = pltpu.VMEM((BANDS * HALVES, SLAB, LON), f32)
     return call(
         merge_kernel,
         [((SLAB, BANDS * ROWS, LON), f32)],
-        (inner, left, right, west, east, coef),
+        (*inner, left, right, west, east, coef),
         (flat,) * 3 + (pltpu.VMEM((SLAB, BANDS * ROWS, LON), f32), dma((BANDS // CHUNK,))),
         hbm_out=(0,),
     )[0]
@@ -483,4 +526,6 @@
         P("region", "band", None),
     )
     out_specs = P("band", None, "region")
-    return jax.shard_map(step_adjoint, mesh=mesh, in_specs=in_specs, out_specs=out_specs, check_vma=False)
+    return jax.shard_map(
+        step_adjoint, mesh=mesh, in_specs=in_specs, out_specs=out_specs, check_vma=False
+    )

time: 81.5 us -> 80.9 us (level)
    ppermute x0 -> x2, starting transfers between devices: none -> 5.09 us  [the longest x1 3.81 us: step_adjoint(): lax.ppermute(left, 'region', [((i + 1) % regions, i) for i in range(regio...]
    ppermute x3 -> x2, starting transfers between devices: 9.45 us -> 5.66 us  [ring_pair(): from_next = lax.ppermute(down_value, axis, [(b, a) for a, b in up])]
    ppermute x3 -> x2, starting transfers between devices: 6.04 us -> 4.75 us  [ring_pair(): from_prev = lax.ppermute(up_value, axis, up)]
    pallas_call x9 -> x10, Pallas kernels: 18.7 us -> 18.1 us  [call(): pl.pallas_call(body, out_shape=[(pltpu.HBM if k in hbm_out else jax.Shape...]
    ppermute x3 -> x2, waiting for transfers between devices: 6.48 us -> 6.48 us  [ring_pair(): from_next = lax.ppermute(down_value, axis, [(b, a) for a, b in up])]
where the time goes in v5:
time: 80.9 us; the launch traced here: 79.6 us
  starting transfers between devices  38 us (47%)
  waiting for transfers between devices  23.1 us (29%)
  Pallas kernels  18.1 us (22%)
    pallas_call x10, Pallas kernels, call(): pl.pallas_call(body, out_shape=[(pltpu.HBM if k in hbm_out else jax.Shape...  18.1 us
    ppermute x8, starting transfers between devices, move(): lax.ppermute(block, 'band', [(i, (i + CORES * t) % BANDS) for i in range(...  12.5 us
    ppermute x8, waiting for transfers between devices, move(): lax.ppermute(block, 'band', [(i, (i + CORES * t) % BANDS) for i in range(...  11.9 us
    all_to_all x1, starting transfers between devices, swap_bands(): lax.all_to_all(blocks, 'band', split_axis=0, concat_axis=0, tiled=True)  9.98 us
    ppermute x2, waiting for transfers between devices, ring_pair(): from_next = lax.ppermute(down_value, axis, [(b, a) for a, b in up])  6.48 us
    ppermute x2, starting transfers between devices, ring_pair(): from_next = lax.ppermute(down_value, axis, [(b, a) for a, b in up])  5.66 us
    ppermute x2, starting transfers between devices, ring_pair(): from_prev = lax.ppermute(up_value, axis, up)  4.75 us
    ppermute x1, starting transfers between devices, step_adjoint(): lax.ppermute(left, 'region', [((i + 1) % regions, i) for i in range(regio...  3.81 us
  transfers between devices with their start and end apart: 16, of which 5 were waited for; matrix products, arithmetic and copies ran while one was open for 0% of the time, Pallas kernels for 11%

profile of v5, /device:TPU:1, one launch (start us, length us, event | category | flops | bytes accessed | tf_op | source)
XLA Modules:
  0.0 79.6 jit_solution(8711463655435798712)
XLA Ops:
  0.0 2.3 %shard_map.109 = f32[16,64,128]{2,1,0:T(8,128)} custom-call(s32[1,16]{1,0:T(1,128)} %count_hbm.1, f32[1,16,64]{2,1,0:T(8,128)} %value_hbm.1, f32[1,16,64,128]{3,2,1,0:T(8,128)} %kern_hbm.1), custom_call_target="tpu_custom_call" | custom-call | tf_op jit(solution)/shard_map/pallas_call | solution.py:375
  2.3 10.0 %all-to-all-start = ((f32[16,64,128]{2,1,0:T(8,128)}), f32[16,64,128]{2,1,0:T(8,128)S(1)}, u32[]{:S(2)}, u32[]{:S(2)}) async-start(f32[16,64,128]{2,1,0:T(8,128)} %shard_map.109), calls=%async_computation | async-start | bytes 1048576 | tf_op jit(solution)/shard_map/all_to_all | solution.py:396
  12.3 2.7 %shard_map.110 = (f32[16,128,128]{2,1,0:T(8,128)S(1)}, f32[16,128,128]{2,1,0:T(8,128)S(1)}, bf16[16,128,256]{2,1,0:T(8,128)(2,1)}) custom-call(f32[128,16,128]{2,1,0:T(8,128)} %field_hbm.1, f32[128,16,128]{2,1,0:T(8,128)} %cy_hbm.1, f32[16,128,128]{2,1,0:T(8,128)} %diff_hbm.1), custom_call_target="tpu_custom_call" | custom-call | tf_op jit(solution)/shard_map/pallas_call | solution.py:375
  15.0 0.0 copy-start.1
  15.0 3.5 %collective-permute-start = (f32[2,128,128]{2,1,0:T(8,128)S(1)}, f32[2,128,128]{2,1,0:T(8,128)S(1)}, u32[]{:S(2)}, u32[]{:S(2)}) collective-permute-start(f32[2,128,128]{2,1,0:T(8,128)S(1)} %slice.6), channel_id=1, source_target_pairs={{0,1},{1,2},{2,3},{3,4},{4,5},{5,6},{6,7},{7,8},{8,9},{9,10},{10,1... | collective-permute-start | bytes 393224 | tf_op jit(solution)/shard_map/ppermute | solution.py:390
  18.5 1.9 %collective-permute-start.1 = (f32[1,128,128]{2,1,0:T(8,128)S(1)}, f32[1,128,128]{2,1,0:T(8,128)S(1)}, u32[]{:S(2)}, u32[]{:S(2)}) collective-permute-start(f32[1,128,128]{2,1,0:T(8,128)S(1)} %slice.7), channel_id=1, source_target_pairs={{1,0},{2,1},{3,2},{4,3},{5,4},{6,5},{7,6},{8,7},{9,8},{10,9},{11,1... | collective-permute-start | bytes 196616 | tf_op jit(solution)/shard_map/ppermute | solution.py:391
  20.5 0.0 copy-done.1
  20.5 0.1 reshape.7.cols_ref
  20.6 6.5 %collective-permute-done.1.after_ref = f32[1,128,128]{2,1,0:T(8,128)S(1)} collective-permute-done((f32[1,128,128]{2,1,0:T(8,128)S(1)}, f32[1,128,128]{2,1,0:T(8,128)S(1)}, u32[]{:S(2)}, u32[]{:S(2)}) %collective-permute-start.1) | collective-permute-done | bytes 65568 | tf_op jit(solution)/shard_map/ppermute | solution.py:391
  27.0 0.0 collective-permute-done.before_ref
  27.0 2.6 %all-to-all-done = f32[16,64,128]{2,1,0:T(8,128)S(1)} async-done(((f32[16,64,128]{2,1,0:T(8,128)}), f32[16,64,128]{2,1,0:T(8,128)S(1)}, u32[]{:S(2)}, u32[]{:S(2)}) %all-to-all-start) | async-done | bytes 524320 | tf_op jit(solution)/shard_map/all_to_all | solution.py:396
  29.6 5.0 %shard_map.111 = (f32[8,20,8,128]{3,2,1,0:T(8,128)S(1)}, f32[8,20,8,128]{3,2,1,0:T(8,128)S(1)}, f32[20,8,128]{2,1,0:T(8,128)S(1)}) custom-call(f32[1024,128]{1,0:T(8,128)S(1)} %bitcast.1, s32[1,1024]{1,0:T(1,128)S(1)} %reshape.7.cols_ref, f32[16,128,128]{2,1,0:T(8,128)S(1)} %get-tuple-element.26.field_ref, f32[16,128,128]{2,1,0:T(8,128)S(1)} %get-tuple-element.27.cy_ref, ...), custom_call_target="tpu_custom_call" | custom-call | tf_op jit(solution)/shard_map/pallas_call | solution.py:375
  34.6 0.0 copy-start
  34.6 0.1 collective-permute-start.3
  34.7 2.1 %collective-permute-done.3.got_ref = f32[8,20,8,128]{3,2,1,0:T(8,128)S(1)} collective-permute-done((f32[8,20,8,128]{3,2,1,0:T(8,128)S(1)}, f32[8,20,8,128]{3,2,1,0:T(8,128)S(1)}, u32[]{:S(2)}, u32[]{:S(2)}) %collective-permute-start.3) | collective-permute-done | bytes 655392 | tf_op jit(solution)/shard_map/ppermute | solution.py:468
  36.8 0.1 shard_map.112
  36.9 0.5 collective-permute-start.10
  37.4 3.2 %collective-permute-start.2 = (f32[20,8,128]{2,1,0:T(8,128)S(1)}, f32[20,8,128]{2,1,0:T(8,128)S(1)}, u32[]{:S(2)}, u32[]{:S(2)}) collective-permute-start(f32[20,8,128]{2,1,0:T(8,128)S(1)} %get-tuple-element.29), channel_id=1, source_target_pairs={{0,8},{1,9},{2,10},{3,11},{4,12},{5,13},{6,14},{7,15},{8,0},{9,1},... | collective-permute-start | bytes 245768 | tf_op jit(solution)/shard_map/ppermute | solution.py:471
  40.6 2.2 %collective-permute-start.4 = (f32[20,8,128]{2,1,0:T(8,128)S(1)}, f32[20,8,128]{2,1,0:T(8,128)S(1)}, u32[]{:S(2)}, u32[]{:S(2)}) collective-permute-start(f32[20,8,128]{2,1,0:T(8,128)S(1)} %get-tuple-element.32), channel_id=1, source_target_pairs={{0,8},{1,9},{2,10},{3,11},{4,12},{5,13},{6,14},{7,15},{8,0},{9,1},... | collective-permute-start | bytes 245768 | tf_op jit(solution)/shard_map/ppermute | solution.py:471
  42.8 0.9 %collective-permute-start.5 = (f32[36,8,128]{2,1,0:T(8,128)S(1)}, f32[36,8,128]{2,1,0:T(8,128)S(1)}, u32[]{:S(2)}, u32[]{:S(2)}) collective-permute-start(f32[36,8,128]{2,1,0:T(8,128)S(1)} %get-tuple-element.34), channel_id=1, source_target_pairs={{0,6},{1,7},{2,8},{3,9},{4,10},{5,11},{6,12},{7,13},{8,14},{9,15},... | collective-permute-start | bytes 442376 | tf_op jit(solution)/shard_map/ppermute | solution.py:471
  43.7 3.5 %collective-permute-start.6 = (f32[36,8,128]{2,1,0:T(8,128)S(1)}, f32[36,8,128]{2,1,0:T(8,128)S(1)}, u32[]{:S(2)}, u32[]{:S(2)}) collective-permute-start(f32[36,8,128]{2,1,0:T(8,128)S(1)} %get-tuple-element.35), channel_id=1, source_target_pairs={{0,10},{1,11},{2,12},{3,13},{4,14},{5,15},{6,0},{7,1},{8,2},{9,3},... | collective-permute-start | bytes 442376 | tf_op jit(solution)/shard_map/ppermute | solution.py:471
  47.3 0.0 collective-permute-done.2.refs_0_
  47.3 0.0 collective-permute-start.7
  47.3 2.5 %collective-permute-done.4.refs_1_ = f32[20,8,128]{2,1,0:T(8,128)S(1)} collective-permute-done((f32[20,8,128]{2,1,0:T(8,128)S(1)}, f32[20,8,128]{2,1,0:T(8,128)S(1)}, u32[]{:S(2)}, u32[]{:S(2)}) %collective-permute-start.4) | collective-permute-done | bytes 81952 | tf_op jit(solution)/shard_map/ppermute | solution.py:471
  49.8 1.6 %collective-permute-start.8 = (f32[36,8,128]{2,1,0:T(8,128)S(1)}, f32[36,8,128]{2,1,0:T(8,128)S(1)}, u32[]{:S(2)}, u32[]{:S(2)}) collective-permute-start(f32[36,8,128]{2,1,0:T(8,128)S(1)} %get-tuple-element.37), channel_id=1, source_target_pairs={{0,12},{1,13},{2,14},{3,15},{4,0},{5,1},{6,2},{7,3},{8,4},{9,5},{1... | collective-permute-start | bytes 442376 | tf_op jit(solution)/shard_map/ppermute | solution.py:471
  51.4 0.0 collective-permute-done.10.refs_8_
  51.4 0.5 collective-permute-start.9
  51.9 0.0 copy-done
  51.9 1.9 %shard_map.114 = (f32[256,8,128]{2,1,0:T(8,128)S(1)}, f32[256,8,128]{2,1,0:T(8,128)S(1)}, f32[16,2,8,128]{3,2,1,0:T(8,128)S(1)}, f32[16,2,8,128]{3,2,1,0:T(8,128)S(1)}) custom-call(f32[8,256,128]{2,1,0:T(8,128)S(1)} %copy-done), custom_call_target="tpu_custom_call" | custom-call | tf_op jit(solution)/shard_map/pallas_call | solution.py:375
  53.8 9.4 %collective-permute-done.5.refs_3_ = f32[36,8,128]{2,1,0:T(8,128)S(1)} collective-permute-done((f32[36,8,128]{2,1,0:T(8,128)S(1)}, f32[36,8,128]{2,1,0:T(8,128)S(1)}, u32[]{:S(2)}, u32[]{:S(2)}) %collective-permute-start.5) | collective-permute-done | bytes 147488 | tf_op jit(solution)/shard_map/ppermute | solution.py:471
  63.1 1.2 %collective-permute-start.13 = (f32[16,2,8,128]{3,2,1,0:T(8,128)S(1)}, f32[16,2,8,128]{3,2,1,0:T(8,128)S(1)}, u32[]{:S(2)}, u32[]{:S(2)}) collective-permute-start(f32[16,2,8,128]{3,2,1,0:T(8,128)S(1)} %get-tuple-element.46.right_ref), channel_id=1, source_target_pairs={{0,16},{16,32},{32,48},{48,64},{64,80},{80,96},{96,112},{112,128},... | collective-permute-start | bytes 393224 | tf_op jit(solution)/shard_map/ppermute | solution.py:390
  64.3 0.0 collective-permute-done.6.refs_4_
  64.3 3.7 %collective-permute-start.14 = (f32[16,2,8,128]{3,2,1,0:T(8,128)S(1)}, f32[16,2,8,128]{3,2,1,0:T(8,128)S(1)}, u32[]{:S(2)}, u32[]{:S(2)}) collective-permute-start(f32[16,2,8,128]{3,2,1,0:T(8,128)S(1)} %get-tuple-element.45.left_ref), channel_id=1, source_target_pairs={{16,0},{32,16},{48,32},{64,48},{80,64},{96,80},{112,96},{128,112},... | collective-permute-start | bytes 393224 | tf_op jit(solution)/shard_map/ppermute | solution.py:391
  68.1 0.0 collective-permute-done.7.refs_5_
  68.1 0.0 collective-permute-done.8.refs_6_
  68.1 0.0 collective-permute-done.9.refs_7_
  68.1 1.0 %shard_map.113 = (f32[256,8,128]{2,1,0:T(8,128)S(1)}, f32[16,2,8,128]{3,2,1,0:T(8,128)S(1)}, f32[16,2,8,128]{3,2,1,0:T(8,128)S(1)}) custom-call(f32[20,8,128]{2,1,0:T(8,128)S(1)} %collective-permute-done.2.refs_0_, f32[20,8,128]{2,1,0:T(8,128)S(1)} %collective-permute-done.4.refs_1_, f32[36,8,128]{2,1,0:T(8,128)S(1)} %get-tuple-element.33.refs_2_, ...), custom_call_target="tpu_custom_call" | custom-call | tf_op jit(solution)/shard_map/pallas_call | solution.py:375
  69.1 1.3 %collective-permute-start.11 = (f32[16,2,8,128]{3,2,1,0:T(8,128)S(1)}, f32[16,2,8,128]{3,2,1,0:T(8,128)S(1)}, u32[]{:S(2)}, u32[]{:S(2)}) collective-permute-start(f32[16,2,8,128]{3,2,1,0:T(8,128)S(1)} %get-tuple-element.44.right_ref), channel_id=1, source_target_pairs={{0,16},{16,32},{32,48},{48,64},{64,80},{80,96},{96,112},{112,128},... | collective-permute-start | bytes 393224 | tf_op jit(solution)/shard_map/ppermute | solution.py:493
  70.4 3.8 %collective-permute-start.12 = (f32[16,2,8,128]{3,2,1,0:T(8,128)S(1)}, f32[16,2,8,128]{3,2,1,0:T(8,128)S(1)}, u32[]{:S(2)}, u32[]{:S(2)}) collective-permute-start(f32[16,2,8,128]{3,2,1,0:T(8,128)S(1)} %get-tuple-element.43.left_ref), channel_id=1, source_target_pairs={{16,0},{32,16},{48,32},{64,48},{80,64},{96,80},{112,96},{128,112},... | collective-permute-start | bytes 393224 | tf_op jit(solution)/shard_map/ppermute | solution.py:494
  74.2 0.0 collective-permute-done.13.west_ref
  74.2 0.0 collective-permute-done.14.east_ref
  74.2 0.6 shard_map.117.coef_ref
  74.8 1.2 %shard_map.116.inner_b = f32[128,8,128]{2,1,0:T(8,128)S(1)} custom-call(f32[256,8,128]{2,1,0:T(8,128)S(1)} %get-tuple-element.40.own_ref, f32[256,8,128]{2,1,0:T(8,128)S(1)} %get-tuple-element.41.cx_ref, f32[256,8,128]{2,1,0:T(8,128)S(1)} %get-tuple-element.42.low_ref), custom_call_target="tpu_custom_call" | custom-call | tf_op jit(solution)/shard_map/pallas_call | solution.py:375
  76.1 1.2 %shard_map.115.inner_a = f32[128,8,128]{2,1,0:T(8,128)S(1)} custom-call(f32[256,8,128]{2,1,0:T(8,128)S(1)} %get-tuple-element.40.own_ref, f32[256,8,128]{2,1,0:T(8,128)S(1)} %get-tuple-element.41.cx_ref, f32[256,8,128]{2,1,0:T(8,128)S(1)} %get-tuple-element.42.low_ref), custom_call_target="tpu_custom_call" | custom-call | tf_op jit(solution)/shard_map/pallas_call | solution.py:375
  77.3 0.0 collective-permute-done.11.west_ref
  77.3 0.0 collective-permute-done.12.east_ref
  77.3 2.1 %shard_map.118 = f32[8,256,128]{2,1,0:T(8,128)} custom-call(f32[128,8,128]{2,1,0:T(8,128)S(1)} %shard_map.115.inner_a, f32[128,8,128]{2,1,0:T(8,128)S(1)} %shard_map.116.inner_b, f32[16,2,8,128]{3,2,1,0:T(8,128)S(1)} %get-tuple-element.43.left_ref, f32[16,2,8,128]{3,2,1,0:T(8,128)S(1)} %get-tuple-element.44.right_ref, ...), custom_call_target="tpu_custom_call" | custom-call | tf_op jit(solution)/shard_map/pallas_call | solution.py:375
  (2 shorter events, 0.0 us)
Async XLA Ops:
  2.3 27.4 %all-to-all-start = ((f32[16,64,128]{2,1,0:T(8,128)}), f32[16,64,128]{2,1,0:T(8,128)S(1)}, u32[]{:S(2)}, u32[]{:S(2)}) async-start(f32[16,64,128]{2,1,0:T(8,128)} %shard_map.109), calls=%async_computation | async-start | bytes 1048576 | tf_op jit(solution)/shard_map/all_to_all | solution.py:396
  15.0 5.5 %copy-start.1 = (s32[1,16,64]{2,1,0:T(8,128)S(1)}, s32[1,16,64]{2,1,0:T(8,128)}, u32[]{:S(2)}) copy-start(s32[1,16,64]{2,1,0:T(8,128)} %param.21) | copy-start | bytes 12292
  15.0 12.1 %collective-permute-start = (f32[2,128,128]{2,1,0:T(8,128)S(1)}, f32[2,128,128]{2,1,0:T(8,128)S(1)}, u32[]{:S(2)}, u32[]{:S(2)}) collective-permute-start(f32[2,128,128]{2,1,0:T(8,128)S(1)} %slice.6), channel_id=1, source_target_pairs={{0,1},{1,2},{2,3},{3,4},{4,5},{5,6},{6,7},{7,8},{8,9},{9,10},{10,1... | collective-permute-start | bytes 393224 | tf_op jit(solution)/shard_map/ppermute | solution.py:390
  18.5 8.5 %collective-permute-start.1 = (f32[1,128,128]{2,1,0:T(8,128)S(1)}, f32[1,128,128]{2,1,0:T(8,128)S(1)}, u32[]{:S(2)}, u32[]{:S(2)}) collective-permute-start(f32[1,128,128]{2,1,0:T(8,128)S(1)} %slice.7), channel_id=1, source_target_pairs={{1,0},{2,1},{3,2},{4,3},{5,4},{6,5},{7,6},{8,7},{9,8},{10,9},{11,1... | collective-permute-start | bytes 196616 | tf_op jit(solution)/shard_map/ppermute | solution.py:391
  34.6 17.3 %copy-start = (f32[8,256,128]{2,1,0:T(8,128)S(1)}, f32[8,256,128]{2,1,0:T(8,128)}, u32[]{:S(2)}) copy-start(f32[8,256,128]{2,1,0:T(8,128)} %cx_ref.1) | copy-start | bytes 3145732
  34.6 2.2 %collective-permute-start.3 = (f32[8,20,8,128]{3,2,1,0:T(8,128)S(1)}, f32[8,20,8,128]{3,2,1,0:T(8,128)S(1)}, u32[]{:S(2)}, u32[]{:S(2)}) collective-permute-start(f32[8,20,8,128]{3,2,1,0:T(8,128)S(1)} %get-tuple-element.31), channel_id=1, source_target_pairs={{0,1},{1,0},{2,3},{3,2},{4,5},{5,4},{6,7},{7,6},{8,9},{9,8},{10,11... | collective-permute-start | bytes 1966088 | tf_op jit(solution)/shard_map/ppermute | solution.py:468
  36.9 14.5 %collective-permute-start.10 = (f32[36,8,128]{2,1,0:T(8,128)S(1)}, f32[36,8,128]{2,1,0:T(8,128)S(1)}, u32[]{:S(2)}, u32[]{:S(2)}) collective-permute-start(f32[36,8,128]{2,1,0:T(8,128)S(1)} %get-tuple-element.39), channel_id=1, source_target_pairs={{0,14},{1,15},{2,0},{3,1},{4,2},{5,3},{6,4},{7,5},{8,6},{9,7},{10,... | collective-permute-start | bytes 442376 | tf_op jit(solution)/shard_map/ppermute | solution.py:471
  37.4 9.9 %collective-permute-start.2 = (f32[20,8,128]{2,1,0:T(8,128)S(1)}, f32[20,8,128]{2,1,0:T(8,128)S(1)}, u32[]{:S(2)}, u32[]{:S(2)}) collective-permute-start(f32[20,8,128]{2,1,0:T(8,128)S(1)} %get-tuple-element.29), channel_id=1, source_target_pairs={{0,8},{1,9},{2,10},{3,11},{4,12},{5,13},{6,14},{7,15},{8,0},{9,1},... | collective-permute-start | bytes 245768 | tf_op jit(solution)/shard_map/ppermute | solution.py:471
  40.6 9.1 %collective-permute-start.4 = (f32[20,8,128]{2,1,0:T(8,128)S(1)}, f32[20,8,128]{2,1,0:T(8,128)S(1)}, u32[]{:S(2)}, u32[]{:S(2)}) collective-permute-start(f32[20,8,128]{2,1,0:T(8,128)S(1)} %get-tuple-element.32), channel_id=1, source_target_pairs={{0,8},{1,9},{2,10},{3,11},{4,12},{5,13},{6,14},{7,15},{8,0},{9,1},... | collective-permute-start | bytes 245768 | tf_op jit(solution)/shard_map/ppermute | solution.py:471
  42.8 20.3 %collective-permute-start.5 = (f32[36,8,128]{2,1,0:T(8,128)S(1)}, f32[36,8,128]{2,1,0:T(8,128)S(1)}, u32[]{:S(2)}, u32[]{:S(2)}) collective-permute-start(f32[36,8,128]{2,1,0:T(8,128)S(1)} %get-tuple-element.34), channel_id=1, source_target_pairs={{0,6},{1,7},{2,8},{3,9},{4,10},{5,11},{6,12},{7,13},{8,14},{9,15},... | collective-permute-start | bytes 442376 | tf_op jit(solution)/shard_map/ppermute | solution.py:471
  43.7 20.6 %collective-permute-start.6 = (f32[36,8,128]{2,1,0:T(8,128)S(1)}, f32[36,8,128]{2,1,0:T(8,128)S(1)}, u32[]{:S(2)}, u32[]{:S(2)}) collective-permute-start(f32[36,8,128]{2,1,0:T(8,128)S(1)} %get-tuple-element.35), channel_id=1, source_target_pairs={{0,10},{1,11},{2,12},{3,13},{4,14},{5,15},{6,0},{7,1},{8,2},{9,3},... | collective-permute-start | bytes 442376 | tf_op jit(solution)/shard_map/ppermute | solution.py:471
  47.3 20.8 %collective-permute-start.7 = (f32[36,8,128]{2,1,0:T(8,128)S(1)}, f32[36,8,128]{2,1,0:T(8,128)S(1)}, u32[]{:S(2)}, u32[]{:S(2)}) collective-permute-start(f32[36,8,128]{2,1,0:T(8,128)S(1)} %get-tuple-element.36), channel_id=1, source_target_pairs={{0,4},{1,5},{2,6},{3,7},{4,8},{5,9},{6,10},{7,11},{8,12},{9,13},{1... | collective-permute-start | bytes 442376 | tf_op jit(solution)/shard_map/ppermute | solution.py:471
  49.8 18.3 %collective-permute-start.8 = (f32[36,8,128]{2,1,0:T(8,128)S(1)}, f32[36,8,128]{2,1,0:T(8,128)S(1)}, u32[]{:S(2)}, u32[]{:S(2)}) collective-permute-start(f32[36,8,128]{2,1,0:T(8,128)S(1)} %get-tuple-element.37), channel_id=1, source_target_pairs={{0,12},{1,13},{2,14},{3,15},{4,0},{5,1},{6,2},{7,3},{8,4},{9,5},{1... | collective-permute-start | bytes 442376 | tf_op jit(solution)/shard_map/ppermute | solution.py:471
  51.4 16.7 %collective-permute-start.9 = (f32[36,8,128]{2,1,0:T(8,128)S(1)}, f32[36,8,128]{2,1,0:T(8,128)S(1)}, u32[]{:S(2)}, u32[]{:S(2)}) collective-permute-start(f32[36,8,128]{2,1,0:T(8,128)S(1)} %get-tuple-element.38), channel_id=1, source_target_pairs={{0,2},{1,3},{2,4},{3,5},{4,6},{5,7},{6,8},{7,9},{8,10},{9,11},{10,... | collective-permute-start | bytes 442376 | tf_op jit(solution)/shard_map/ppermute | solution.py:471
  63.1 11.1 %collective-permute-start.13 = (f32[16,2,8,128]{3,2,1,0:T(8,128)S(1)}, f32[16,2,8,128]{3,2,1,0:T(8,128)S(1)}, u32[]{:S(2)}, u32[]{:S(2)}) collective-permute-start(f32[16,2,8,128]{3,2,1,0:T(8,128)S(1)} %get-tuple-element.46.right_ref), channel_id=1, source_target_pairs={{0,16},{16,32},{32,48},{48,64},{64,80},{80,96},{96,112},{112,128},... | collective-permute-start | bytes 393224 | tf_op jit(solution)/shard_map/ppermute | solution.py:390
  64.3 9.9 %collective-permute-start.14 = (f32[16,2,8,128]{3,2,1,0:T(8,128)S(1)}, f32[16,2,8,128]{3,2,1,0:T(8,128)S(1)}, u32[]{:S(2)}, u32[]{:S(2)}) collective-permute-start(f32[16,2,8,128]{3,2,1,0:T(8,128)S(1)} %get-tuple-element.45.left_ref), channel_id=1, source_target_pairs={{16,0},{32,16},{48,32},{64,48},{80,64},{96,80},{112,96},{128,112},... | collective-permute-start | bytes 393224 | tf_op jit(solution)/shard_map/ppermute | solution.py:391
  69.1 8.2 %collective-permute-start.11 = (f32[16,2,8,128]{3,2,1,0:T(8,128)S(1)}, f32[16,2,8,128]{3,2,1,0:T(8,128)S(1)}, u32[]{:S(2)}, u32[]{:S(2)}) collective-permute-start(f32[16,2,8,128]{3,2,1,0:T(8,128)S(1)} %get-tuple-element.44.right_ref), channel_id=1, source_target_pairs={{0,16},{16,32},{32,48},{48,64},{64,80},{80,96},{96,112},{112,128},... | collective-permute-start | bytes 393224 | tf_op jit(solution)/shard_map/ppermute | solution.py:493
  70.4 6.9 %collective-permute-start.12 = (f32[16,2,8,128]{3,2,1,0:T(8,128)S(1)}, f32[16,2,8,128]{3,2,1,0:T(8,128)S(1)}, u32[]{:S(2)}, u32[]{:S(2)}) collective-permute-start(f32[16,2,8,128]{3,2,1,0:T(8,128)S(1)} %get-tuple-element.43.left_ref), channel_id=1, source_target_pairs={{16,0},{32,16},{48,32},{64,48},{80,64},{96,80},{112,96},{128,112},... | collective-permute-start | bytes 393224 | tf_op jit(solution)/shard_map/ppermute | solution.py:494

commit v6 on v5

--- a/solution.py
+++ b/solution.py
@@ -1,5 +1,3 @@
-import functools
-
 import jax
 import jax.numpy as jnp
 from jax import lax
@@ -310,17 +308,16 @@
     lax.fori_loop(0, BANDS // CHUNK, pack, 0)
 
 
-def zonal_kernel(part, own_ref, cx_ref, low_ref, out_ref, first, second):
+def zonal_kernel(own_ref, cx_ref, low_ref, out_ref, first, second):
     tiles = CHUNK * ROWS
-    chunks = BANDS // CHUNK // 2
 
     def sources(i, carry):
         old, new = first, second
         for step in range(XSTEPS):
             for t in range(tiles):
-                value = own_ref[(part * chunks + i) * tiles + t] if step == 0 else old[t]
-                up = jnp.maximum(cx_ref[(part * chunks + i) * tiles + t], 0.0)
-                low = low_ref[(part * chunks + i) * tiles + t]
+                value = own_ref[i * tiles + t] if step == 0 else old[t]
+                up = jnp.maximum(cx_ref[i * tiles + t], 0.0)
+                low = low_ref[i * tiles + t]
                 value = zonal_sweep(value, 1.0 - up + low, up, low)
                 if step == XSTEPS - 1:
                     out_ref[i * tiles + t] = value
@@ -329,10 +326,10 @@
             old, new = new, old
         return carry
 
-    lax.fori_loop(0, chunks, sources, 0)
-
-
-def merge_kernel(inner_a, inner_b, left_ref, right_ref, west_ref, east_ref, coef_ref, out_hbm, sides, left_buf, right_buf, out_ref, sem):
+    lax.fori_loop(0, BANDS // CHUNK, sources, 0)
+
+
+def merge_kernel(inner_ref, left_ref, right_ref, west_ref, east_ref, coef_ref, out_hbm, sides, left_buf, right_buf, out_ref, sem):
     count = BANDS * HALVES
     for n in range(count):
         s, half = n // HALVES, n % HALVES
@@ -360,8 +357,7 @@
                 packed = sides[i * HALVES + k]
                 for g in range(ROWS // HALVES):
                     lat = i * ROWS + k * (ROWS // HALVES) + g
-                    inner = inner_a[lat] if i < BANDS // 2 else inner_b[lat - BANDS // 2 * ROWS]
-                    out_ref[:, lat, :] = jnp.where(outer, turned(packed, -STRIP * g - XSTEPS), inner)
+                    out_ref[:, lat, :] = jnp.where(outer, turned(packed, -STRIP * g - XSTEPS), inner_ref[lat])
         store(c).start()
     for c in range(BANDS // CHUNK):
         store(c).wait()
@@ -489,23 +485,14 @@
         (cx_left, cx_right, cx_west, cx_east),
     )
     own, left, right = call(pack_kernel, [(tiles, f32), (strips, f32), (strips, f32)], moved)
-    regions = lax.axis_size("region")
-    west = lax.ppermute(right, "region", [(i, (i + 1) % regions) for i in range(regions)])
-    east = lax.ppermute(left, "region", [((i + 1) % regions, i) for i in range(regions)])
+    west, east = ring_pair(right, left, "region", True)
     chunk = pltpu.VMEM((CHUNK * ROWS, SLAB, LON), f32)
-    inner = []
-    for part in range(2):
-        inner += call(
-            functools.partial(zonal_kernel, part),
-            [((BANDS * ROWS // 2, SLAB, LON), f32)],
-            (own, cx, cx_low),
-            (chunk,) * 2,
-        )
+    (inner,) = call(zonal_kernel, [(tiles, f32)], (own, cx, cx_low), (chunk,) * 2)
     flat = pltpu.VMEM((BANDS * HALVES, SLAB, LON), f32)
     return call(
         merge_kernel,
         [((SLAB, BANDS * ROWS, LON), f32)],
-        (*inner, left, right, west, east, coef),
+        (inner, left, right, west, east, coef),
         (flat,) * 3 + (pltpu.VMEM((SLAB, BANDS * ROWS, LON), f32), dma((BANDS // CHUNK,))),
         hbm_out=(0,),
     )[0]
@@ -526,6 +513,4 @@
         P("region", "band", None),
     )
     out_specs = P("band", None, "region")
-    return jax.shard_map(
-        step_adjoint, mesh=mesh, in_specs=in_specs, out_specs=out_specs, check_vma=False
-    )
+    return jax.shard_map(step_adjoint, mesh=mesh, in_specs=in_specs, out_specs=out_specs, check_vma=False)

time: 80.9 us -> 80.9 us (level)
    ppermute x2 -> x0, starting transfers between devices: 5.09 us -> none  [the longest x1 3.81 us: step_adjoint(): lax.ppermute(left, 'region', [((i + 1) % regions, i) for i in range(regio...]
    ppermute x2 -> x3, starting transfers between devices: 5.66 us -> 9.47 us  [ring_pair(): from_next = lax.ppermute(down_value, axis, [(b, a) for a, b in up])]
    ppermute x2 -> x3, starting transfers between devices: 4.75 us -> 6.03 us  [ring_pair(): from_prev = lax.ppermute(up_value, axis, up)]
    ppermute x2 -> x3, waiting for transfers between devices: 6.48 us -> 6.48 us  [ring_pair(): from_next = lax.ppermute(down_value, axis, [(b, a) for a, b in up])]
    pallas_call x10 -> x9, Pallas kernels: 18.1 us -> 18.1 us  [call(): pl.pallas_call(body, out_shape=[(pltpu.HBM if k in hbm_out else jax.Shape...]
where the time goes in v6:
time: 80.9 us; the launch traced here: 79.6 us
  starting transfers between devices  38 us (47%)
  waiting for transfers between devices  23.1 us (29%)
  Pallas kernels  18.1 us (22%)
    pallas_call x9, Pallas kernels, call(): pl.pallas_call(body, out_shape=[(pltpu.HBM if k in hbm_out else jax.Shape...  18.1 us
    ppermute x8, starting transfers between devices, move(): lax.ppermute(block, 'band', [(i, (i + CORES * t) % BANDS) for i in range(...  12.5 us
    ppermute x8, waiting for transfers between devices, move(): lax.ppermute(block, 'band', [(i, (i + CORES * t) % BANDS) for i in range(...  11.9 us
    all_to_all x1, starting transfers between devices, swap_bands(): lax.all_to_all(blocks, 'band', split_axis=0, concat_axis=0, tiled=True)  9.98 us
    ppermute x3, starting transfers between devices, ring_pair(): from_next = lax.ppermute(down_value, axis, [(b, a) for a, b in up])  9.47 us
    ppermute x3, waiting for transfers between devices, ring_pair(): from_next = lax.ppermute(down_value, axis, [(b, a) for a, b in up])  6.48 us
    ppermute x3, starting transfers between devices, ring_pair(): from_prev = lax.ppermute(up_value, axis, up)  6.03 us
    all_to_all x1, waiting for transfers between devices, swap_bands(): lax.all_to_all(blocks, 'band', split_axis=0, concat_axis=0, tiled=True)  2.6 us
  transfers between devices with their start and end apart: 16, of which 5 were waited for; matrix products, arithmetic and copies ran while one was open for 0% of the time, Pallas kernels for 11%

profile of v6, /device:TPU:1, one launch (start us, length us, event | category | flops | bytes accessed | tf_op | source)
XLA Modules:
  0.0 79.6 jit_solution(4660906826607175407)
XLA Ops:
  0.0 2.3 %shard_map.109 = f32[16,64,128]{2,1,0:T(8,128)} custom-call(s32[1,16]{1,0:T(1,128)} %count_hbm.1, f32[1,16,64]{2,1,0:T(8,128)} %value_hbm.1, f32[1,16,64,128]{3,2,1,0:T(8,128)} %kern_hbm.1), custom_call_target="tpu_custom_call" | custom-call | tf_op jit(solution)/shard_map/pallas_call | solution.py:371
  2.3 10.0 %all-to-all-start = ((f32[16,64,128]{2,1,0:T(8,128)}), f32[16,64,128]{2,1,0:T(8,128)S(1)}, u32[]{:S(2)}, u32[]{:S(2)}) async-start(f32[16,64,128]{2,1,0:T(8,128)} %shard_map.109), calls=%async_computation | async-start | bytes 1048576 | tf_op jit(solution)/shard_map/all_to_all | solution.py:392
  12.3 2.7 %shard_map.110 = (f32[16,128,128]{2,1,0:T(8,128)S(1)}, f32[16,128,128]{2,1,0:T(8,128)S(1)}, bf16[16,128,256]{2,1,0:T(8,128)(2,1)}) custom-call(f32[128,16,128]{2,1,0:T(8,128)} %field_hbm.1, f32[128,16,128]{2,1,0:T(8,128)} %cy_hbm.1, f32[16,128,128]{2,1,0:T(8,128)} %diff_hbm.1), custom_call_target="tpu_custom_call" | custom-call | tf_op jit(solution)/shard_map/pallas_call | solution.py:371
  15.0 0.0 copy-start.1
  15.0 3.5 %collective-permute-start = (f32[2,128,128]{2,1,0:T(8,128)S(1)}, f32[2,128,128]{2,1,0:T(8,128)S(1)}, u32[]{:S(2)}, u32[]{:S(2)}) collective-permute-start(f32[2,128,128]{2,1,0:T(8,128)S(1)} %slice.6), channel_id=1, source_target_pairs={{0,1},{1,2},{2,3},{3,4},{4,5},{5,6},{6,7},{7,8},{8,9},{9,10},{10,1... | collective-permute-start | bytes 393224 | tf_op jit(solution)/shard_map/ppermute | solution.py:386
  18.5 1.9 %collective-permute-start.1 = (f32[1,128,128]{2,1,0:T(8,128)S(1)}, f32[1,128,128]{2,1,0:T(8,128)S(1)}, u32[]{:S(2)}, u32[]{:S(2)}) collective-permute-start(f32[1,128,128]{2,1,0:T(8,128)S(1)} %slice.7), channel_id=1, source_target_pairs={{1,0},{2,1},{3,2},{4,3},{5,4},{6,5},{7,6},{8,7},{9,8},{10,9},{11,1... | collective-permute-start | bytes 196616 | tf_op jit(solution)/shard_map/ppermute | solution.py:387
  20.5 0.0 copy-done.1
  20.5 0.1 reshape.7.cols_ref
  20.6 6.5 %collective-permute-done.1.after_ref = f32[1,128,128]{2,1,0:T(8,128)S(1)} collective-permute-done((f32[1,128,128]{2,1,0:T(8,128)S(1)}, f32[1,128,128]{2,1,0:T(8,128)S(1)}, u32[]{:S(2)}, u32[]{:S(2)}) %collective-permute-start.1) | collective-permute-done | bytes 65568 | tf_op jit(solution)/shard_map/ppermute | solution.py:387
  27.0 0.0 collective-permute-done.before_ref
  27.0 2.6 %all-to-all-done = f32[16,64,128]{2,1,0:T(8,128)S(1)} async-done(((f32[16,64,128]{2,1,0:T(8,128)}), f32[16,64,128]{2,1,0:T(8,128)S(1)}, u32[]{:S(2)}, u32[]{:S(2)}) %all-to-all-start) | async-done | bytes 524320 | tf_op jit(solution)/shard_map/all_to_all | solution.py:392
  29.6 5.0 %shard_map.111 = (f32[8,20,8,128]{3,2,1,0:T(8,128)S(1)}, f32[8,20,8,128]{3,2,1,0:T(8,128)S(1)}, f32[20,8,128]{2,1,0:T(8,128)S(1)}) custom-call(f32[1024,128]{1,0:T(8,128)S(1)} %bitcast.1, s32[1,1024]{1,0:T(1,128)S(1)} %reshape.7.cols_ref, f32[16,128,128]{2,1,0:T(8,128)S(1)} %get-tuple-element.26.field_ref, f32[16,128,128]{2,1,0:T(8,128)S(1)} %get-tuple-element.27.cy_ref, ...), custom_call_target="tpu_custom_call" | custom-call | tf_op jit(solution)/shard_map/pallas_call | solution.py:371
  34.6 0.0 copy-start
  34.6 0.1 collective-permute-start.3
  34.7 2.1 %collective-permute-done.3.got_ref = f32[8,20,8,128]{3,2,1,0:T(8,128)S(1)} collective-permute-done((f32[8,20,8,128]{3,2,1,0:T(8,128)S(1)}, f32[8,20,8,128]{3,2,1,0:T(8,128)S(1)}, u32[]{:S(2)}, u32[]{:S(2)}) %collective-permute-start.3) | collective-permute-done | bytes 655392 | tf_op jit(solution)/shard_map/ppermute | solution.py:464
  36.8 0.1 shard_map.112
  36.9 0.5 collective-permute-start.10
  37.4 3.2 %collective-permute-start.2 = (f32[20,8,128]{2,1,0:T(8,128)S(1)}, f32[20,8,128]{2,1,0:T(8,128)S(1)}, u32[]{:S(2)}, u32[]{:S(2)}) collective-permute-start(f32[20,8,128]{2,1,0:T(8,128)S(1)} %get-tuple-element.29), channel_id=1, source_target_pairs={{0,8},{1,9},{2,10},{3,11},{4,12},{5,13},{6,14},{7,15},{8,0},{9,1},... | collective-permute-start | bytes 245768 | tf_op jit(solution)/shard_map/ppermute | solution.py:467
  40.6 2.2 %collective-permute-start.4 = (f32[20,8,128]{2,1,0:T(8,128)S(1)}, f32[20,8,128]{2,1,0:T(8,128)S(1)}, u32[]{:S(2)}, u32[]{:S(2)}) collective-permute-start(f32[20,8,128]{2,1,0:T(8,128)S(1)} %get-tuple-element.32), channel_id=1, source_target_pairs={{0,8},{1,9},{2,10},{3,11},{4,12},{5,13},{6,14},{7,15},{8,0},{9,1},... | collective-permute-start | bytes 245768 | tf_op jit(solution)/shard_map/ppermute | solution.py:467
  42.8 0.9 %collective-permute-start.5 = (f32[36,8,128]{2,1,0:T(8,128)S(1)}, f32[36,8,128]{2,1,0:T(8,128)S(1)}, u32[]{:S(2)}, u32[]{:S(2)}) collective-permute-start(f32[36,8,128]{2,1,0:T(8,128)S(1)} %get-tuple-element.34), channel_id=1, source_target_pairs={{0,6},{1,7},{2,8},{3,9},{4,10},{5,11},{6,12},{7,13},{8,14},{9,15},... | collective-permute-start | bytes 442376 | tf_op jit(solution)/shard_map/ppermute | solution.py:467
  43.7 3.5 %collective-permute-start.6 = (f32[36,8,128]{2,1,0:T(8,128)S(1)}, f32[36,8,128]{2,1,0:T(8,128)S(1)}, u32[]{:S(2)}, u32[]{:S(2)}) collective-permute-start(f32[36,8,128]{2,1,0:T(8,128)S(1)} %get-tuple-element.35), channel_id=1, source_target_pairs={{0,10},{1,11},{2,12},{3,13},{4,14},{5,15},{6,0},{7,1},{8,2},{9,3},... | collective-permute-start | bytes 442376 | tf_op jit(solution)/shard_map/ppermute | solution.py:467
  47.3 0.0 collective-permute-done.2.refs_0_
  47.3 0.0 collective-permute-start.7
  47.3 2.5 %collective-permute-done.4.refs_1_ = f32[20,8,128]{2,1,0:T(8,128)S(1)} collective-permute-done((f32[20,8,128]{2,1,0:T(8,128)S(1)}, f32[20,8,128]{2,1,0:T(8,128)S(1)}, u32[]{:S(2)}, u32[]{:S(2)}) %collective-permute-start.4) | collective-permute-done | bytes 81952 | tf_op jit(solution)/shard_map/ppermute | solution.py:467
  49.8 1.6 %collective-permute-start.8 = (f32[36,8,128]{2,1,0:T(8,128)S(1)}, f32[36,8,128]{2,1,0:T(8,128)S(1)}, u32[]{:S(2)}, u32[]{:S(2)}) collective-permute-start(f32[36,8,128]{2,1,0:T(8,128)S(1)} %get-tuple-element.37), channel_id=1, source_target_pairs={{0,12},{1,13},{2,14},{3,15},{4,0},{5,1},{6,2},{7,3},{8,4},{9,5},{1... | collective-permute-start | bytes 442376 | tf_op jit(solution)/shard_map/ppermute | solution.py:467
  51.4 0.0 collective-permute-done.10.refs_8_
  51.4 0.5 collective-permute-start.9
  51.9 0.0 copy-done
  51.9 1.9 %shard_map.114 = (f32[256,8,128]{2,1,0:T(8,128)S(1)}, f32[256,8,128]{2,1,0:T(8,128)S(1)}, f32[16,2,8,128]{3,2,1,0:T(8,128)S(1)}, f32[16,2,8,128]{3,2,1,0:T(8,128)S(1)}) custom-call(f32[8,256,128]{2,1,0:T(8,128)S(1)} %copy-done), custom_call_target="tpu_custom_call" | custom-call | tf_op jit(solution)/shard_map/pallas_call | solution.py:371
  53.8 9.4 %collective-permute-done.5.refs_3_ = f32[36,8,128]{2,1,0:T(8,128)S(1)} collective-permute-done((f32[36,8,128]{2,1,0:T(8,128)S(1)}, f32[36,8,128]{2,1,0:T(8,128)S(1)}, u32[]{:S(2)}, u32[]{:S(2)}) %collective-permute-start.5) | collective-permute-done | bytes 147488 | tf_op jit(solution)/shard_map/ppermute | solution.py:467
  63.1 1.2 %collective-permute-start.13 = (f32[16,2,8,128]{3,2,1,0:T(8,128)S(1)}, f32[16,2,8,128]{3,2,1,0:T(8,128)S(1)}, u32[]{:S(2)}, u32[]{:S(2)}) collective-permute-start(f32[16,2,8,128]{3,2,1,0:T(8,128)S(1)} %get-tuple-element.46.right_ref), channel_id=1, source_target_pairs={{0,16},{16,32},{32,48},{48,64},{64,80},{80,96},{96,112},{112,128},... | collective-permute-start | bytes 393224 | tf_op jit(solution)/shard_map/ppermute | solution.py:386
  64.3 0.0 collective-permute-done.6.refs_4_
  64.3 3.7 %collective-permute-start.14 = (f32[16,2,8,128]{3,2,1,0:T(8,128)S(1)}, f32[16,2,8,128]{3,2,1,0:T(8,128)S(1)}, u32[]{:S(2)}, u32[]{:S(2)}) collective-permute-start(f32[16,2,8,128]{3,2,1,0:T(8,128)S(1)} %get-tuple-element.45.left_ref), channel_id=1, source_target_pairs={{16,0},{32,16},{48,32},{64,48},{80,64},{96,80},{112,96},{128,112},... | collective-permute-start | bytes 393224 | tf_op jit(solution)/shard_map/ppermute | solution.py:387
  68.1 0.0 collective-permute-done.7.refs_5_
  68.1 0.0 collective-permute-done.8.refs_6_
  68.1 0.0 collective-permute-done.9.refs_7_
  68.1 1.0 %shard_map.113 = (f32[256,8,128]{2,1,0:T(8,128)S(1)}, f32[16,2,8,128]{3,2,1,0:T(8,128)S(1)}, f32[16,2,8,128]{3,2,1,0:T(8,128)S(1)}) custom-call(f32[20,8,128]{2,1,0:T(8,128)S(1)} %collective-permute-done.2.refs_0_, f32[20,8,128]{2,1,0:T(8,128)S(1)} %collective-permute-done.4.refs_1_, f32[36,8,128]{2,1,0:T(8,128)S(1)} %get-tuple-element.33.refs_2_, ...), custom_call_target="tpu_custom_call" | custom-call | tf_op jit(solution)/shard_map/pallas_call | solution.py:371
  69.1 1.3 %collective-permute-start.11 = (f32[16,2,8,128]{3,2,1,0:T(8,128)S(1)}, f32[16,2,8,128]{3,2,1,0:T(8,128)S(1)}, u32[]{:S(2)}, u32[]{:S(2)}) collective-permute-start(f32[16,2,8,128]{3,2,1,0:T(8,128)S(1)} %get-tuple-element.44.right_ref), channel_id=1, source_target_pairs={{0,16},{16,32},{32,48},{48,64},{64,80},{80,96},{96,112},{112,128},... | collective-permute-start | bytes 393224 | tf_op jit(solution)/shard_map/ppermute | solution.py:386
  70.4 3.8 %collective-permute-start.12 = (f32[16,2,8,128]{3,2,1,0:T(8,128)S(1)}, f32[16,2,8,128]{3,2,1,0:T(8,128)S(1)}, u32[]{:S(2)}, u32[]{:S(2)}) collective-permute-start(f32[16,2,8,128]{3,2,1,0:T(8,128)S(1)} %get-tuple-element.43.left_ref), channel_id=1, source_target_pairs={{16,0},{32,16},{48,32},{64,48},{80,64},{96,80},{112,96},{128,112},... | collective-permute-start | bytes 393224 | tf_op jit(solution)/shard_map/ppermute | solution.py:387
  74.2 0.0 collective-permute-done.13.west_ref
  74.2 0.0 collective-permute-done.14.east_ref
  74.2 0.6 shard_map.116.coef_ref
  74.8 2.5 %shard_map.115.inner_ref = f32[256,8,128]{2,1,0:T(8,128)S(1)} custom-call(f32[256,8,128]{2,1,0:T(8,128)S(1)} %get-tuple-element.40.own_ref, f32[256,8,128]{2,1,0:T(8,128)S(1)} %get-tuple-element.41.cx_ref, f32[256,8,128]{2,1,0:T(8,128)S(1)} %get-tuple-element.42.low_ref), custom_call_target="tpu_custom_call" | custom-call | tf_op jit(solution)/shard_map/pallas_call | solution.py:371
  77.3 0.0 collective-permute-done.11.west_ref
  77.3 0.0 collective-permute-done.12.east_ref
  77.3 2.1 %shard_map.117 = f32[8,256,128]{2,1,0:T(8,128)} custom-call(f32[256,8,128]{2,1,0:T(8,128)S(1)} %shard_map.115.inner_ref, f32[16,2,8,128]{3,2,1,0:T(8,128)S(1)} %get-tuple-element.43.left_ref, f32[16,2,8,128]{3,2,1,0:T(8,128)S(1)} %get-tuple-element.44.right_ref, f32[16,2,8,128]{3,2,1,0:T(8,128)S(1)} %collective-permute-done.11.west_ref, ...), custom_call_target="tpu_custom_call" | custom-call | tf_op jit(solution)/shard_map/pallas_call | solution.py:371
  (2 shorter events, 0.0 us)
Async XLA Ops:
  2.3 27.4 %all-to-all-start = ((f32[16,64,128]{2,1,0:T(8,128)}), f32[16,64,128]{2,1,0:T(8,128)S(1)}, u32[]{:S(2)}, u32[]{:S(2)}) async-start(f32[16,64,128]{2,1,0:T(8,128)} %shard_map.109), calls=%async_computation | async-start | bytes 1048576 | tf_op jit(solution)/shard_map/all_to_all | solution.py:392
  15.0 5.5 %copy-start.1 = (s32[1,16,64]{2,1,0:T(8,128)S(1)}, s32[1,16,64]{2,1,0:T(8,128)}, u32[]{:S(2)}) copy-start(s32[1,16,64]{2,1,0:T(8,128)} %param.21) | copy-start | bytes 12292
  15.0 12.1 %collective-permute-start = (f32[2,128,128]{2,1,0:T(8,128)S(1)}, f32[2,128,128]{2,1,0:T(8,128)S(1)}, u32[]{:S(2)}, u32[]{:S(2)}) collective-permute-start(f32[2,128,128]{2,1,0:T(8,128)S(1)} %slice.6), channel_id=1, source_target_pairs={{0,1},{1,2},{2,3},{3,4},{4,5},{5,6},{6,7},{7,8},{8,9},{9,10},{10,1... | collective-permute-start | bytes 393224 | tf_op jit(solution)/shard_map/ppermute | solution.py:386
  18.5 8.5 %collective-permute-start.1 = (f32[1,128,128]{2,1,0:T(8,128)S(1)}, f32[1,128,128]{2,1,0:T(8,128)S(1)}, u32[]{:S(2)}, u32[]{:S(2)}) collective-permute-start(f32[1,128,128]{2,1,0:T(8,128)S(1)} %slice.7), channel_id=1, source_target_pairs={{1,0},{2,1},{3,2},{4,3},{5,4},{6,5},{7,6},{8,7},{9,8},{10,9},{11,1... | collective-permute-start | bytes 196616 | tf_op jit(solution)/shard_map/ppermute | solution.py:387
  34.6 17.3 %copy-start = (f32[8,256,128]{2,1,0:T(8,128)S(1)}, f32[8,256,128]{2,1,0:T(8,128)}, u32[]{:S(2)}) copy-start(f32[8,256,128]{2,1,0:T(8,128)} %cx_ref.1) | copy-start | bytes 3145732
  34.6 2.2 %collective-permute-start.3 = (f32[8,20,8,128]{3,2,1,0:T(8,128)S(1)}, f32[8,20,8,128]{3,2,1,0:T(8,128)S(1)}, u32[]{:S(2)}, u32[]{:S(2)}) collective-permute-start(f32[8,20,8,128]{3,2,1,0:T(8,128)S(1)} %get-tuple-element.31), channel_id=1, source_target_pairs={{0,1},{1,0},{2,3},{3,2},{4,5},{5,4},{6,7},{7,6},{8,9},{9,8},{10,11... | collective-permute-start | bytes 1966088 | tf_op jit(solution)/shard_map/ppermute | solution.py:464
  36.9 14.5 %collective-permute-start.10 = (f32[36,8,128]{2,1,0:T(8,128)S(1)}, f32[36,8,128]{2,1,0:T(8,128)S(1)}, u32[]{:S(2)}, u32[]{:S(2)}) collective-permute-start(f32[36,8,128]{2,1,0:T(8,128)S(1)} %get-tuple-element.39), channel_id=1, source_target_pairs={{0,14},{1,15},{2,0},{3,1},{4,2},{5,3},{6,4},{7,5},{8,6},{9,7},{10,... | collective-permute-start | bytes 442376 | tf_op jit(solution)/shard_map/ppermute | solution.py:467
  37.4 9.9 %collective-permute-start.2 = (f32[20,8,128]{2,1,0:T(8,128)S(1)}, f32[20,8,128]{2,1,0:T(8,128)S(1)}, u32[]{:S(2)}, u32[]{:S(2)}) collective-permute-start(f32[20,8,128]{2,1,0:T(8,128)S(1)} %get-tuple-element.29), channel_id=1, source_target_pairs={{0,8},{1,9},{2,10},{3,11},{4,12},{5,13},{6,14},{7,15},{8,0},{9,1},... | collective-permute-start | bytes 245768 | tf_op jit(solution)/shard_map/ppermute | solution.py:467
  40.6 9.1 %collective-permute-start.4 = (f32[20,8,128]{2,1,0:T(8,128)S(1)}, f32[20,8,128]{2,1,0:T(8,128)S(1)}, u32[]{:S(2)}, u32[]{:S(2)}) collective-permute-start(f32[20,8,128]{2,1,0:T(8,128)S(1)} %get-tuple-element.32), channel_id=1, source_target_pairs={{0,8},{1,9},{2,10},{3,11},{4,12},{5,13},{6,14},{7,15},{8,0},{9,1},... | collective-permute-start | bytes 245768 | tf_op jit(solution)/shard_map/ppermute | solution.py:467
  42.8 20.3 %collective-permute-start.5 = (f32[36,8,128]{2,1,0:T(8,128)S(1)}, f32[36,8,128]{2,1,0:T(8,128)S(1)}, u32[]{:S(2)}, u32[]{:S(2)}) collective-permute-start(f32[36,8,128]{2,1,0:T(8,128)S(1)} %get-tuple-element.34), channel_id=1, source_target_pairs={{0,6},{1,7},{2,8},{3,9},{4,10},{5,11},{6,12},{7,13},{8,14},{9,15},... | collective-permute-start | bytes 442376 | tf_op jit(solution)/shard_map/ppermute | solution.py:467
  43.7 20.6 %collective-permute-start.6 = (f32[36,8,128]{2,1,0:T(8,128)S(1)}, f32[36,8,128]{2,1,0:T(8,128)S(1)}, u32[]{:S(2)}, u32[]{:S(2)}) collective-permute-start(f32[36,8,128]{2,1,0:T(8,128)S(1)} %get-tuple-element.35), channel_id=1, source_target_pairs={{0,10},{1,11},{2,12},{3,13},{4,14},{5,15},{6,0},{7,1},{8,2},{9,3},... | collective-permute-start | bytes 442376 | tf_op jit(solution)/shard_map/ppermute | solution.py:467
  47.3 20.8 %collective-permute-start.7 = (f32[36,8,128]{2,1,0:T(8,128)S(1)}, f32[36,8,128]{2,1,0:T(8,128)S(1)}, u32[]{:S(2)}, u32[]{:S(2)}) collective-permute-start(f32[36,8,128]{2,1,0:T(8,128)S(1)} %get-tuple-element.36), channel_id=1, source_target_pairs={{0,4},{1,5},{2,6},{3,7},{4,8},{5,9},{6,10},{7,11},{8,12},{9,13},{1... | collective-permute-start | bytes 442376 | tf_op jit(solution)/shard_map/ppermute | solution.py:467
  49.8 18.3 %collective-permute-start.8 = (f32[36,8,128]{2,1,0:T(8,128)S(1)}, f32[36,8,128]{2,1,0:T(8,128)S(1)}, u32[]{:S(2)}, u32[]{:S(2)}) collective-permute-start(f32[36,8,128]{2,1,0:T(8,128)S(1)} %get-tuple-element.37), channel_id=1, source_target_pairs={{0,12},{1,13},{2,14},{3,15},{4,0},{5,1},{6,2},{7,3},{8,4},{9,5},{1... | collective-permute-start | bytes 442376 | tf_op jit(solution)/shard_map/ppermute | solution.py:467
  51.4 16.7 %collective-permute-start.9 = (f32[36,8,128]{2,1,0:T(8,128)S(1)}, f32[36,8,128]{2,1,0:T(8,128)S(1)}, u32[]{:S(2)}, u32[]{:S(2)}) collective-permute-start(f32[36,8,128]{2,1,0:T(8,128)S(1)} %get-tuple-element.38), channel_id=1, source_target_pairs={{0,2},{1,3},{2,4},{3,5},{4,6},{5,7},{6,8},{7,9},{8,10},{9,11},{10,... | collective-permute-start | bytes 442376 | tf_op jit(solution)/shard_map/ppermute | solution.py:467
  63.1 11.1 %collective-permute-start.13 = (f32[16,2,8,128]{3,2,1,0:T(8,128)S(1)}, f32[16,2,8,128]{3,2,1,0:T(8,128)S(1)}, u32[]{:S(2)}, u32[]{:S(2)}) collective-permute-start(f32[16,2,8,128]{3,2,1,0:T(8,128)S(1)} %get-tuple-element.46.right_ref), channel_id=1, source_target_pairs={{0,16},{16,32},{32,48},{48,64},{64,80},{80,96},{96,112},{112,128},... | collective-permute-start | bytes 393224 | tf_op jit(solution)/shard_map/ppermute | solution.py:386
  64.3 9.9 %collective-permute-start.14 = (f32[16,2,8,128]{3,2,1,0:T(8,128)S(1)}, f32[16,2,8,128]{3,2,1,0:T(8,128)S(1)}, u32[]{:S(2)}, u32[]{:S(2)}) collective-permute-start(f32[16,2,8,128]{3,2,1,0:T(8,128)S(1)} %get-tuple-element.45.left_ref), channel_id=1, source_target_pairs={{16,0},{32,16},{48,32},{64,48},{80,64},{96,80},{112,96},{128,112},... | collective-permute-start | bytes 393224 | tf_op jit(solution)/shard_map/ppermute | solution.py:387
  69.1 8.2 %collective-permute-start.11 = (f32[16,2,8,128]{3,2,1,0:T(8,128)S(1)}, f32[16,2,8,128]{3,2,1,0:T(8,128)S(1)}, u32[]{:S(2)}, u32[]{:S(2)}) collective-permute-start(f32[16,2,8,128]{3,2,1,0:T(8,128)S(1)} %get-tuple-element.44.right_ref), channel_id=1, source_target_pairs={{0,16},{16,32},{32,48},{48,64},{64,80},{80,96},{96,112},{112,128},... | collective-permute-start | bytes 393224 | tf_op jit(solution)/shard_map/ppermute | solution.py:386
  70.4 6.9 %collective-permute-start.12 = (f32[16,2,8,128]{3,2,1,0:T(8,128)S(1)}, f32[16,2,8,128]{3,2,1,0:T(8,128)S(1)}, u32[]{:S(2)}, u32[]{:S(2)}) collective-permute-start(f32[16,2,8,128]{3,2,1,0:T(8,128)S(1)} %get-tuple-element.43.left_ref), channel_id=1, source_target_pairs={{16,0},{32,16},{48,32},{64,48},{80,64},{96,80},{112,96},{128,112},... | collective-permute-start | bytes 393224 | tf_op jit(solution)/shard_map/ppermute | solution.py:387
